TPU v7x, 512 devices: a whole 4x8x8 slice. The times are simulated.
512 devices in a mesh: dp: 32 (over y, x), col: 16 (over z, core).
Axes of the slice: x: 4, y: 8, z: 8, core: 2. Of those that a mesh axis runs over, the one named last changes fastest.
Arguments:
- grad_out: bfloat16 [32768, 3584], P('dp', 'col'), may hold values from -6 to 6
- residual: bfloat16 [32768, 3584], P('dp', 'col'), may hold values from -6 to 6
- confounders: bfloat16 [32768, 512], P('dp'), may hold values from -6 to 6
- gram_factor: float32 [512, 512], replicated, as said below
- proj_weight: bfloat16 [3584, 3584], P('dp', 'col'), may hold values from -0.09375 to 0.09375
- doc_lengths: int32 [32768], P(('dp', 'col')), may hold values from 1 to 512, as said below
Outputs:
- token_grad: float32 [32768, 3584], P(('dp', 'col'))
- weight_grad: float32 [3584, 3584], P('dp', 'col')
Inputs may be any that keep to these rules, and one draw needn't show every extreme that they name: `gram_factor`: lower triangular with a positive diagonal. `doc_lengths`: at least one document has 512 tokens.
All inputs are finite; a program needn't handle non-finite values.
Results may differ from a plain program's by a relative error of at most 0.0026.
Values may be sent and summed in bfloat16 or wider, within the bound.
No kernel may reach another device: no remote copies, remote signals or barrier semaphores. Data moves between devices by JAX's collectives and lax.ppermute only.
A program may use at most 64 MiB of HBM per device.

v0:
```python
import jax
import jax.numpy as jnp
from jax import lax
from jax.sharding import PartitionSpec as P


def solve_gram(factor, rhs):
    inner = lax.linalg.triangular_solve(factor, rhs, left_side=True, lower=True)
    return lax.linalg.triangular_solve(factor, inner, left_side=True, lower=True, transpose_a=True)


def shards(grad_out, residual, confounders, gram_factor, proj_weight, doc_lengths):
    grad_full = lax.all_gather(grad_out, "col", axis=1, tiled=True)
    docs_total = grad_out.shape[0] * lax.axis_size("dp")
    norm_scale = docs_total ** (-0.5)
    own_rows = proj_weight.shape[0]
    full_term = lax.dot_general(
        grad_full, residual, (((0,), (0,)), ((), ())), preferred_element_type=jnp.float32
    )
    summed_all = lax.psum(full_term, "dp")
    summed = lax.dynamic_slice_in_dim(summed_all, lax.axis_index("dp") * own_rows, own_rows, 0)
    weight_grad = summed * norm_scale
    dense_grad = jnp.dot(
        grad_full,
        lax.all_gather(proj_weight, "dp", axis=0, tiled=True),
        preferred_element_type=jnp.float32,
    )
    dense_b = dense_grad.astype(jnp.bfloat16)
    partial_value = lax.dot_general(
        confounders, dense_b, (((0,), (0,)), ((), ())), preferred_element_type=jnp.float32
    )
    moments = lax.psum(partial_value, "dp")
    coef_b = solve_gram(gram_factor, moments).astype(jnp.bfloat16)
    pooled = dense_grad - jnp.dot(confounders, coef_b, preferred_element_type=jnp.float32)
    doc_grad = lax.all_to_all(pooled, "col", split_axis=0, concat_axis=1, tiled=True)
    token_grad = doc_grad / doc_lengths.astype(jnp.float32)[:, None]
    return (token_grad, weight_grad)


def solution(mesh):
    placed = (P("dp", "col"), P("dp", "col"), P("dp", None), P(), P("dp", "col"), P(("dp", "col")))
    return jax.shard_map(
        shards,
        mesh=mesh,
        in_specs=placed,
        out_specs=(P(("dp", "col"), None), P("dp", "col")),
        check_vma=False,
    )
```

profile of v0, /device:TPU:1, one launch (start us, length us, event | category | flops | bytes accessed | tf_op | source)
XLA Modules:
  0.0 392.3 jit_solution(9254413336297546510)
XLA Ops:
  7.2 0.0 copy-start
  7.2 0.0 all-gather.5.cloned.1.call-start
  7.2 0.7 all-gather.5.cloned.1.call-update
  7.9 0.0 all-gather.3.cloned.1.call-start
  8.0 0.7 all-gather.3.cloned.1.call-update
  8.7 0.0 copy-start.2
  8.7 0.0 all-reduce.3.cloned.1.call-start
  8.7 86.1 %all-gather.5.cloned.1.call-done = bf16[3584,224]{1,0:T(8,128)(2,1)} async-done(((bf16[112,224]{1,0:T(8,128)(2,1)}), bf16[3584,224]{1,0:T(8,128)(2,1)}) %all-gather.5.cloned.1.call-update) | async-done | bytes 1605648 | tf_op jit(solution)/shard_map/all_gather | solution.py:25
  94.8 59.2 %all-gather.3.cloned.1.call-done = bf16[1024,3584]{0,1:T(8,128)(2,1)} async-done(((bf16[1024,224]{0,1:T(8,128)(2,1)}), bf16[1024,3584]{0,1:T(8,128)(2,1)}) %all-gather.3.cloned.1.call-update) | async-done | bytes 7340048 | tf_op jit(solution)/shard_map/all_gather | solution.py:13
  154.0 0.0 copy-start.1
  154.0 5.6 %fusion.49 = f32[1024,224]{0,1:T(8,128)S(1)} fusion(bf16[1024,3584]{0,1:T(8,128)(2,1)} %all-gather.3.cloned.1.call-done, bf16[3584,224]{1,0:T(8,128)(2,1)} %all-gather.5.cloned.1.call-done), kind=kOutput, calls=%fused_computation.68 | convolution fusion | flops 1644167168 | bytes 9863168 | tf_op jit(solution)/shard_map/dot_general | solution.py:23
  159.6 0.0 copy-done
  159.6 1.2 convolution_bitcast_fusion.1
  160.8 0.0 copy-done.2
  160.8 0.0 copy-done.1
  160.8 4.0 %fusion.50 = f32[3584,224]{1,0:T(8,128)} fusion(bf16[1024,3584]{0,1:T(8,128)(2,1)S(1)} %copy-done.1, bf16[1024,224]{0,1:T(8,128)(2,1)S(1)} %copy-done.2), kind=kOutput, calls=%fused_computation.69 | convolution fusion | flops 1644167168 | bytes 11010048 | tf_op jit(solution)/shard_map/dot_general | solution.py:17
  164.8 0.0 all-reduce.3.cloned.1.call-update
  164.8 1.3 fusion.1
  166.2 8.0 %while.1 = (s32[]{:T(128)}, f32[512,512]{1,0:T(8,128)S(1)}, s32[4,2]{0,1:T(2,128)S(1)}, f32[4,128,128]{2,1,0:T(8,128)S(1)}, s32[]{:T(128)}) while((s32[]{:T(128)}, f32[512,512]{1,0:T(8,128)S(1)}, s32[4,2]{0,1:T(2,128)S(1)}, f32[4,128,128]{2,1,0:T(8,128)S(1)}, s32[]{:T(128)}) %tuple.26), condition=%wide.while_cond, body=%wide.while_body.sunk | while | flops 2 | bytes 131189 | solution.py:9
  166.2 0.1 constant_dynamic-slice_fusion.2
  166.3 0.6 fusion.67
  166.9 1.3 bitcast_dynamic-update-slice_fusion.2
  168.2 0.1 constant_dynamic-slice_fusion.2
  168.3 0.6 fusion.67
  168.9 1.3 bitcast_dynamic-update-slice_fusion.2
  170.2 0.1 constant_dynamic-slice_fusion.2
  170.3 0.6 fusion.67
  170.9 1.3 bitcast_dynamic-update-slice_fusion.2
  172.2 0.1 constant_dynamic-slice_fusion.2
  172.3 0.6 fusion.67
  172.9 1.3 bitcast_dynamic-update-slice_fusion.2
  174.2 39.3 %custom-call.5 = f32[4,128,128]{1,2,0:T(8,128)S(1)} custom-call(f32[4,128,128]{2,1,0:T(8,128)S(1)} %get-tuple-element.9), custom_call_target="InvertDiagBlocksLowerTriangular" | custom-call | tf_op jit(solution)/shard_map/triangular_solve | solution.py:9
  213.5 120.8 %all-reduce.3.cloned.1.call-done = (f32[512,224]{0,1:T(8,128)}, f32[3584,224]{1,0:T(8,128)}) async-done(((f32[512,224]{0,1:T(8,128)}, f32[3584,224]{1,0:T(8,128)}), (f32[512,224]{0,1:T(8,128)}, f32[3584,224]{1,0:T(8,128)})) %all-reduce.3.cloned.1.call-update) | async-done | bytes 3670032 | tf_op jit(solution)/shard_map/psum | solution.py:32
  334.3 1.1 fusion.30
  335.5 1.2 convolution_subtract_fusion.1
  336.6 0.2 fusion.35
  336.9 1.3 convolution_subtract_fusion.3
  338.1 0.3 fusion.37
  338.4 1.4 convolution_subtract_fusion.5
  339.8 0.2 fusion.39
  340.0 0.3 fusion.46
  340.3 0.3 convolution_subtract_fusion
  340.5 0.3 fusion.47
  340.8 0.3 convolution_subtract_fusion.2
  341.2 0.3 fusion.48
  341.5 0.5 convolution_subtract_fusion.4
  341.9 0.0 copy-start.3
  341.9 0.3 convolution_convert_fusion
  342.2 0.5 fusion
  342.7 1.3 copy.10
  344.0 11.5 %all-to-all-start = ((f32[16,64,224]{2,1,0:T(8,128)}), f32[16,64,224]{2,1,0:T(8,128)S(1)}, u32[]{:S(2)}, u32[]{:S(2)}) async-start(f32[16,64,224]{2,1,0:T(8,128)} %bitcast.6), calls=%async_computation | async-start | bytes 2097152 | tf_op jit(solution)/shard_map/all_to_all | solution.py:35
  355.5 0.0 copy-done.3
  355.5 1.6 dynamic-slice_multiply_fusion
  357.1 26.4 %all-to-all-done = f32[16,64,224]{2,1,0:T(8,128)S(1)} async-done(((f32[16,64,224]{2,1,0:T(8,128)}), f32[16,64,224]{2,1,0:T(8,128)S(1)}, u32[]{:S(2)}, u32[]{:S(2)}) %all-to-all-start) | async-done | bytes 917536 | tf_op jit(solution)/shard_map/all_to_all | solution.py:35
  383.5 0.6 copy.11
  384.1 0.6 all_to_all.17
  384.7 1.1 broadcast_divide_fusion
  (4 shorter events, 0.0 us)
Async XLA Ops:
  7.2 152.4 %copy-start = (bf16[1024,512]{1,0:T(8,128)(2,1)S(1)}, bf16[1024,512]{1,0:T(8,128)(2,1)}, u32[]{:S(2)}) copy-start(bf16[1024,512]{1,0:T(8,128)(2,1)} %param.8) | copy-start | bytes 3145732
  7.2 87.6 %all-gather.5.cloned.1.call-start = ((), (), s32[]{:S(2)}) async-start(), calls=%async_computation.2 | async-start | bytes 1892352 | tf_op jit(solution)/shard_map/all_gather | solution.py:25
  7.9 146.0 %all-gather.3.cloned.1.call-start = ((), (), s32[]{:S(2)}) async-start(), calls=%async_computation.1 | async-start | bytes 7798784 | tf_op jit(solution)/shard_map/all_gather | solution.py:13
  8.7 152.1 %copy-start.2 = (bf16[1024,224]{0,1:T(8,128)(2,1)S(1)}, bf16[1024,224]{0,1:T(8,128)(2,1)}, u32[]{:S(2)}) copy-start(bf16[1024,224]{0,1:T(8,128)(2,1)} %param.7) | copy-start | bytes 1376260
  8.7 325.6 %all-reduce.3.cloned.1.call-start = ((), (), s32[]{:S(2)}) async-start(), calls=%async_computation.3 | async-start | bytes 8257536 | tf_op jit(solution)/shard_map/psum | solution.py:32
  154.0 6.8 %copy-start.1 = (bf16[1024,3584]{0,1:T(8,128)(2,1)S(1)}, bf16[1024,3584]{0,1:T(8,128)(2,1)}, u32[]{:S(2)}) copy-start(bf16[1024,3584]{0,1:T(8,128)(2,1)} %all-gather.3.cloned.1.call-done) | copy-start | bytes 22020100
  341.9 13.6 %copy-start.3 = (s32[64]{0:T(128)S(1)}, s32[64]{0:T(128)}, u32[]{:S(2)}) copy-start(s32[64]{0:T(128)} %param.11) | copy-start | bytes 772
  344.0 39.5 %all-to-all-start = ((f32[16,64,224]{2,1,0:T(8,128)}), f32[16,64,224]{2,1,0:T(8,128)S(1)}, u32[]{:S(2)}, u32[]{:S(2)}) async-start(f32[16,64,224]{2,1,0:T(8,128)} %bitcast.6), calls=%async_computation | async-start | bytes 2097152 | tf_op jit(solution)/shard_map/all_to_all | solution.py:35
Sparse Core Ops, SparseCore 0:
  11.1 83.6 all-gather.4
  96.9 57.0 all-gather.2
  164.9 169.3 all-reduce.2
where the time goes:
time: 393 us; the launch traced here: 392 us
  waiting for transfers between devices  294 us (75%)
  other arithmetic  43.3 us (11%)
  matrix products  19.1 us (5%)
  between operations  14 us (4%)
  starting transfers between devices  11.6 us (3%)
  local copies, waits for them, and re-layouts  10.5 us (3%)
    psum x1, waiting for transfers between devices, shards(): moments = lax.psum(partial_value, 'dp')  121 us
    all_gather x1, waiting for transfers between devices, shards(): lax.all_gather(proj_weight, 'dp', axis=0, tiled=True)  86.1 us
    all_gather x1, waiting for transfers between devices, shards(): grad_full = lax.all_gather(grad_out, 'col', axis=1, tiled=True)  59.2 us
    another operation x3, other arithmetic, solve_gram(): lax.linalg.triangular_solve(factor, inner, left_side=True, lower=True, tr...  40.7 us
    all_to_all x1, waiting for transfers between devices, shards(): lax.all_to_all(pooled, 'col', split_axis=0, concat_axis=1, tiled=True)  26.4 us
    all_to_all x1, starting transfers between devices, shards(): lax.all_to_all(pooled, 'col', split_axis=0, concat_axis=1, tiled=True)  11.5 us
    another operation x12, local copies, waits for them, and re-layouts  7.92 us
  transfers between devices with their start and end apart: 4, of which 4 were waited for; matrix products, arithmetic and copies ran while one was open for 13% of the time, Pallas kernels for 0%

commit v1 on v0

v1 whole, which is shorter than its diff:
```python
import jax
import jax.numpy as jnp
from jax import lax
from jax.experimental import pallas as pl
from jax.experimental.pallas import tpu as pltpu
from jax.sharding import Mesh, PartitionSpec as P

HI = lax.Precision.HIGHEST
F32 = jnp.float32
BF16 = jnp.bfloat16
DP = ("y", "x")
COL = ("z", "c")


def dot_hi(a, b, dims=(((1,), (0,)), ((), ()))):
    return lax.dot_general(a, b, dims, precision=HI, preferred_element_type=F32)


def gram_inverse_kernel(factor_ref, out_ref):
    size, base, half = factor_ref.shape[0], 8, factor_ref.shape[0] // 2
    count = size // base
    factor = factor_ref[...]
    block = lax.broadcasted_iota(jnp.int32, (count, base, size), 0)
    lane = lax.broadcasted_iota(jnp.int32, (count, base, size), 2)
    own = block == lane // base
    diag = jnp.sum(jnp.where(own, factor.reshape(count, base, size), 0.0), 0)
    lane = lax.broadcasted_iota(jnp.int32, (base, size), 1) % base
    picked = jnp.concatenate([jnp.where(lane == m, diag, 0.0) for m in range(base)], 0)
    rows = lax.broadcasted_iota(jnp.int32, (size, size), 0)
    cols = lax.broadcasted_iota(jnp.int32, (size, size), 1)
    same = jnp.where(rows // base == cols // base, 1.0, 0.0).astype(F32)
    entry = dot_hi(picked, same)
    lane = lane[:1]
    solved = []
    for r in range(base):
        acc = jnp.where(lane == r, 1.0, 0.0)
        for m in range(r):
            acc = acc - entry[m * base + r : m * base + r + 1] * solved[m]
        solved.append(acc / entry[r * base + r : r * base + r + 1])
    solved = jnp.concatenate(solved, 0)
    inv = jnp.where(own, solved[None], 0.0).reshape(size, size)
    tops = [inv[:half, :half], inv[half:, half:]]
    facs = [factor[:half, :half], factor[half:, half:]]
    rows, cols = rows[:half, :half], cols[:half, :half]
    step = base
    while step < half:
        pair = (rows // (2 * step) == cols // (2 * step)) & (rows % (2 * step) >= step) & (cols % (2 * step) < step)
        tops = [t - dot_hi(t, dot_hi(jnp.where(pair, f, 0.0), t)) for t, f in zip(tops, facs)]
        step *= 2
    left = -dot_hi(tops[1], dot_hi(factor[half:, :half], tops[0]))
    trans = (((0,), (0,)), ((), ()))
    out_ref[:half, :half] = dot_hi(tops[0], tops[0], trans) + dot_hi(left, left, trans)
    out_ref[half:, :half] = dot_hi(tops[1], left, trans)
    out_ref[:half, half:] = dot_hi(left, tops[1], trans)
    out_ref[half:, half:] = dot_hi(tops[1], tops[1], trans)


def gram_inverse(factor):
    return pl.pallas_call(
        gram_inverse_kernel,
        out_shape=jax.ShapeDtypeStruct(factor.shape, F32),
        compiler_params=pltpu.CompilerParams(vmem_limit_bytes=32 * 1024 * 1024),
        name="gram_inverse",
    )(factor)


def spread(x, axes, count):
    copies = jnp.broadcast_to(x[None], (count,) + x.shape)
    return lax.all_to_all(copies, axes, split_axis=0, concat_axis=0, tiled=True)


def weight_grad_kernel(place_ref, mine_ref, theirs_ref, residual_ref, *out_refs):
    core, chip = place_ref[0], place_ref[1]
    rows = out_refs[0].shape[1]
    per = mine_ref.shape[0] // rows
    for d, out_ref in enumerate(out_refs):
        target = (chip + d) % len(out_refs)
        at = pl.ds(pl.multiple_of((target % per) * rows, rows), rows)
        cols = jnp.where(target // per == core, mine_ref[at, :], theirs_ref[at, :])
        out = lax.dot_general(cols, residual_ref[...], (((1,), (1,)), ((), ())), preferred_element_type=F32)
        out_ref[0] = out.astype(BF16)


def partial_weight_grads(place, mine, theirs, residual, blocks, parts, rows):
    width, docs = residual.shape
    spec = pl.BlockSpec((width, docs), lambda i, p: (i, 0))
    return pl.pallas_call(
        weight_grad_kernel,
        out_shape=[jax.ShapeDtypeStruct((blocks, rows, width), BF16)] * parts,
        grid_spec=pltpu.PrefetchScalarGridSpec(
            num_scalar_prefetch=1,
            grid=(blocks,),
            in_specs=[spec, spec, pl.BlockSpec((width, docs), lambda i, p: (0, 0))],
            out_specs=[pl.BlockSpec((1, rows, width), lambda i, p: (i, 0, 0))] * parts,
        ),
        name="partial_weight_grads",
    )(place, mine, theirs, residual)


def shards(grad_out, residual, confounders, gram_factor, proj_weight, doc_lengths):
    ny, nx, nz, nc = (lax.axis_size(a) for a in ("y", "x", "z", "c"))
    ndp, ncol = ny * nx, nz * nc
    docs, width = grad_out.shape
    own_rows = proj_weight.shape[0]
    kdim = confounders.shape[1]
    norm_scale = (docs * ndp) ** (-0.5)
    core = lax.axis_index("c")

    mine = lax.all_gather(grad_out.T, "z", axis=0, tiled=True)
    theirs = lax.ppermute(mine, "c", [(0, 1), (1, 0)])

    cross = lax.dot_general(confounders, grad_out, (((0,), (0,)), ((), ())), preferred_element_type=F32)
    cross = lax.all_to_all(cross.reshape(ndp, kdim // ndp, width), DP, split_axis=0, concat_axis=0, tiled=True)
    cross = spread(jnp.sum(cross, 0), COL, ncol)
    cross = jnp.transpose(cross, (1, 0, 2)).reshape(kdim // ndp, ncol * width)

    weight = lax.all_gather(proj_weight[None], "y", axis=0, tiled=True)
    half = ny // 2
    weight = [lax.all_gather(w, "x", axis=1, tiled=True) for w in (weight[:half], weight[half:])]
    weight = jnp.concatenate(weight, 0).reshape(ndp * own_rows, width)
    moments = dot_hi(cross, weight.astype(F32))
    moments = spread(moments, DP, ndp).reshape(kdim, width)
    inverse = gram_inverse(gram_factor)
    coef_b = dot_hi(inverse, moments).astype(BF16)

    place = jnp.stack([core, lax.axis_index("x")]).astype(jnp.int32)
    parts = partial_weight_grads(place, mine, theirs, residual.T, nz, nx, own_rows)
    total = parts[0].astype(F32)
    for d in range(1, nx):
        total = total + lax.ppermute(parts[d], "x", [(i, (i + d) % nx) for i in range(nx)]).astype(F32)
    parts = lax.all_to_all(total.astype(BF16), "y", split_axis=0, concat_axis=0, tiled=True)
    total = parts[0].astype(F32)
    for i in range(1, ny):
        total = total + parts[i].astype(F32)
    weight_grad = total * norm_scale

    split = weight.reshape(nz, nc, width, width)
    w_mine = lax.dynamic_index_in_dim(split, core, 1, keepdims=False).reshape(nz * width, width)
    w_theirs = lax.dynamic_index_in_dim(split, 1 - core, 1, keepdims=False).reshape(nz * width, width)
    pooled = jnp.dot(mine.T, w_mine, preferred_element_type=F32)
    pooled = pooled + jnp.dot(theirs.T, w_theirs, preferred_element_type=F32)
    pooled = pooled - jnp.dot(confounders, coef_b, preferred_element_type=F32)
    doc_grad = lax.all_to_all(pooled.astype(BF16), COL, split_axis=0, concat_axis=1, tiled=True)
    token_grad = doc_grad.astype(F32) / doc_lengths.astype(F32)[:, None]
    return (token_grad, weight_grad)


def solution(mesh):
    fine = Mesh(mesh.devices.reshape(8, 4, 8, 2), ("y", "x", "z", "c"))
    placed = (P(DP, COL), P(DP, COL), P(DP, None), P(), P(DP, COL), P(DP + COL))
    return jax.shard_map(
        shards,
        mesh=fine,
        in_specs=placed,
        out_specs=(P(DP + COL, None), P(DP, COL)),
        check_vma=False,
    )
```

time: 393 us -> 267 us (0.68)
  waiting for transfers between devices: 294 us -> 94.9 us
  blocking collectives: 0 us -> 52.8 us
  starting transfers between devices: 11.6 us -> 56.8 us
  other arithmetic: 43.3 us -> 4.6 us
  Pallas kernels: 0 us -> 18.6 us
  matrix products: 19.1 us -> 14.5 us
    psum x1 -> x0, waiting for transfers between devices: 121 us -> none  [shards(): moments = lax.psum(partial_value, 'dp')]
    all_gather x2 -> x1, waiting for transfers between devices: 145 us -> 60.8 us  [shards(): mine = lax.all_gather(grad_out.T, 'z', axis=0, tiled=True)]
    all_gather x0 -> x3, blocking collectives: none -> 52.8 us  [the longest x1 28.9 us: shards(): weight = lax.all_gather(proj_weight[None], 'y', axis=0, tiled=True)]
    another operation x3 -> x1, other arithmetic: 40.7 us -> 0.66 us  [shards(): place = jnp.stack([core, lax.axis_index('x')]).astype(jnp.int32)]
    all_to_all x1 -> x5, starting transfers between devices: 11.5 us -> 44.7 us  [the longest x2 20.2 us: spread(): return lax.all_to_all(copies, axes, split_axis=0, concat_axis=0, tiled=True)]
    pallas_call x0 -> x2, Pallas kernels: none -> 18.6 us  [the longest x1 10.3 us: partial_weight_grads(): pl.pallas_call(weight_grad_kernel, out_shape=[jax.ShapeDtypeStruct((block...]
    ppermute x0 -> x4, waiting for transfers between devices: none -> 18 us  [the longest x3 18 us: shards(): lax.ppermute(parts[d], 'x', [(i, (i + d) % nx) for i in range(nx)])]
    ppermute x0 -> x4, starting transfers between devices: none -> 12.1 us  [the longest x3 9.34 us: shards(): lax.ppermute(parts[d], 'x', [(i, (i + d) % nx) for i in range(nx)])]
  transfers between devices with their start and end apart: 4 -> 10, of which waited for: 4 -> 6; matrix products, arithmetic and copies ran while one was open for 13% -> 8% of each run, Pallas kernels for 0% -> 7%
where the time goes in v1:
time: 267 us; the launch traced here: 265 us
  waiting for transfers between devices  94.9 us (36%)
  starting transfers between devices  56.8 us (21%)
  blocking collectives  52.8 us (20%)
  Pallas kernels  18.6 us (7%)
  matrix products  14.5 us (5%)
  between operations  14.3 us (5%)
  local copies, waits for them, and re-layouts  8.46 us (3%)
  other arithmetic  4.6 us (2%)
    all_gather x1, waiting for transfers between devices, shards(): mine = lax.all_gather(grad_out.T, 'z', axis=0, tiled=True)  60.8 us
    all_gather x1, blocking collectives, shards(): weight = lax.all_gather(proj_weight[None], 'y', axis=0, tiled=True)  28.9 us
    all_gather x2, blocking collectives, shards(): lax.all_gather(w, 'x', axis=1, tiled=True)  24 us
    all_to_all x2, starting transfers between devices, spread(): return lax.all_to_all(copies, axes, split_axis=0, concat_axis=0, tiled=True)  20.2 us
    ppermute x3, waiting for transfers between devices, shards(): lax.ppermute(parts[d], 'x', [(i, (i + d) % nx) for i in range(nx)])  18 us
    all_to_all x1, waiting for transfers between devices, shards(): lax.all_to_all(total.astype(BF16), 'y', split_axis=0, concat_axis=0, tile...  12.8 us
    all_to_all x1, starting transfers between devices, shards(): lax.all_to_all(pooled.astype(BF16), COL, split_axis=0, concat_axis=1, til...  11.8 us
    pallas_call x1, Pallas kernels, partial_weight_grads(): pl.pallas_call(weight_grad_kernel, out_shape=[jax.ShapeDtypeStruct((block...  10.3 us
  transfers between devices with their start and end apart: 10, of which 6 were waited for; matrix products, arithmetic and copies ran while one was open for 8% of the time, Pallas kernels for 7%

profile of v1, /device:TPU:1, one launch (start us, length us, event | category | flops | bytes accessed | tf_op | source)
XLA Modules:
  0.0 264.9 jit_solution(4674614477517140584)
XLA Ops:
  7.2 0.0 copy-start
  7.2 0.0 copy-start.3
  7.2 0.0 all-gather.3.cloned.1.call-start
  7.2 0.7 all-gather.3.cloned.1.call-update
  7.9 60.8 %all-gather.3.cloned.1.call-done.mine_ref = bf16[1792,1024]{1,0:T(8,128)(2,1)} async-done(((bf16[224,1024]{1,0:T(8,128)(2,1)}), bf16[1792,1024]{1,0:T(8,128)(2,1)}) %all-gather.3.cloned.1.call-update) | async-done | bytes 3670032 | tf_op jit(solution)/shard_map/all_gather | solution.py:109
  68.7 2.7 %collective-permute-start = (bf16[1792,1024]{1,0:T(8,128)(2,1)}, bf16[1792,1024]{1,0:T(8,128)(2,1)}, u32[]{:S(2)}, u32[]{:S(2)}) collective-permute-start(bf16[1792,1024]{1,0:T(8,128)(2,1)} %all-gather.3.cloned.1.call-done.mine_ref), channel_id=1, source_target_pairs={{0,1},{1,0},{2,3},{3,2},{4,5},{5,4},{6,7},{7,6},{8,9},{9,8},{10,11... | collective-permute-start | bytes 11010056 | tf_op jit(solution)/shard_map/ppermute | solution.py:110
  71.4 0.0 copy-done
  71.4 2.3 fusion.4
  73.7 9.3 %all-to-all-start = ((f32[32,16,224]{2,1,0:T(8,128)}), f32[32,16,224]{2,1,0:T(8,128)S(1)}, u32[]{:S(2)}, u32[]{:S(2)}) async-start(f32[32,16,224]{2,1,0:T(8,128)} %bitcast.6), calls=%async_computation | async-start | bytes 1048576 | tf_op jit(solution)/shard_map/all_to_all | solution.py:113
  83.0 0.0 copy-done.3
  83.0 28.9 %all-gather = bf16[896,224]{1,0:T(8,128)(2,1)S(1)} all-gather(bf16[112,224]{1,0:T(8,128)(2,1)S(1)} %copy-done.3), channel_id=2, replica_groups=mesh['y'=8,'x'=4,'z'=8,'c'=2] {'y'}, dimensions={0}, use_global_device_ids=true | all-gather | bytes 451584 | tf_op jit(solution)/shard_map/all_gather | solution.py:117
  111.9 0.7 fusion.2
  112.6 11.6 %all_gather.13 = bf16[4,448,224]{2,1,0:T(8,128)(2,1)S(1)} all-gather(bf16[4,112,224]{2,1,0:T(8,128)(2,1)S(1)} %bitcast.38), channel_id=1, replica_groups=mesh['y'=8,'x'=4,'z'=8,'c'=2] {'x'}, dimensions={1}, use_global_device_ids=true | all-gather | bytes 1003520 | tf_op jit(solution)/shard_map/all_gather | solution.py:119
  124.2 0.1 constant_dynamic-update-slice_fusion.1
  124.3 0.0 all-to-all-done
  124.3 0.1 reduce_sum.9
  124.3 0.7 broadcast_in_dim.7
  125.1 12.5 %all-to-all-start.1 = ((f32[16,16,224]{2,1,0:T(8,128)}), f32[16,16,224]{2,1,0:T(8,128)S(1)}, u32[]{:S(2)}, u32[]{:S(2)}) async-start(f32[16,16,224]{2,1,0:T(8,128)} %broadcast_in_dim.7), calls=%async_computation.1 | async-start | bytes 524288 | tf_op jit(solution)/shard_map/all_to_all | solution.py:69
  137.6 12.3 %all_gather.14 = bf16[4,448,224]{2,1,0:T(8,128)(2,1)S(1)} all-gather(bf16[4,112,224]{2,1,0:T(8,128)(2,1)} %bitcast.37), channel_id=1, replica_groups=mesh['y'=8,'x'=4,'z'=8,'c'=2] {'x'}, dimensions={1}, use_global_device_ids=true | all-gather | bytes 1003520 | tf_op jit(solution)/shard_map/all_gather | solution.py:119
  149.9 0.1 constant_dynamic-update-slice_fusion
  150.0 0.0 copy-start.2
  150.0 0.0 all-to-all-done.1
  150.0 0.2 copy.15
  150.2 0.2 reshape.50
  150.3 1.0 copy-done.2
  151.3 0.0 copy-start.1
  151.3 2.4 fusion.5
  153.7 0.9 broadcast_in_dim.8
  154.6 7.7 %all-to-all-start.2 = ((f32[32,16,224]{2,1,0:T(8,128)}), f32[32,16,224]{2,1,0:T(8,128)}, u32[]{:S(2)}, u32[]{:S(2)}) async-start(f32[32,16,224]{2,1,0:T(8,128)} %broadcast_in_dim.8), calls=%async_computation.2 | async-start | bytes 1048576 | tf_op jit(solution)/shard_map/all_to_all | solution.py:69
  162.3 0.0 copy-done.1
  162.3 8.3 %gram_inverse.1 = f32[512,512]{1,0:T(8,128)S(1)} custom-call(f32[512,512]{1,0:T(8,128)S(1)} %copy-done.1), custom_call_target="tpu_custom_call" | custom-call | tf_op jit(solution)/shard_map/gram_inverse/pallas_call | solution.py:59
  170.6 2.5 constant_dynamic-slice_fusion
  173.1 2.7 %all-to-all-done.2 = f32[32,16,224]{2,1,0:T(8,128)} async-done(((f32[32,16,224]{2,1,0:T(8,128)}), f32[32,16,224]{2,1,0:T(8,128)}, u32[]{:S(2)}, u32[]{:S(2)}) %all-to-all-start.2) | async-done | bytes 458784 | tf_op jit(solution)/shard_map/all_to_all | solution.py:69
  175.7 2.9 %convolution_convert_fusion = bf16[224,512]{1,0:T(8,128)(2,1)S(1)} fusion(f32[512,224]{1,0:T(8,128)} %bitcast.9, f32[512,512]{1,0:T(8,128)S(1)} %gram_inverse.1), kind=kOutput, calls=%fused_computation.4 | convolution fusion | flops 704757760 | bytes 1736704 | tf_op jit(solution)/shard_map/dot_general | solution.py:16
  178.6 3.3 %fusion.3 = f32[224,1024]{1,0:T(8,128)S(1)} fusion(bf16[1792,224]{1,0:T(8,128)(2,1)} %bitcast.39, bf16[1792,1024]{1,0:T(8,128)(2,1)} %all-gather.3.cloned.1.call-done.mine_ref), kind=kOutput, calls=%fused_computation.15 | convolution fusion | flops 822083584 | bytes 5390336 | tf_op jit(solution)/shard_map/dot_general | solution.py:140
  182.0 0.0 collective-permute-done.theirs_ref
  182.0 3.1 %convolution_add_fusion = f32[224,1024]{1,0:T(8,128)S(1)} fusion(f32[224,1024]{1,0:T(8,128)S(1)} %fusion.3, bf16[1792,224]{1,0:T(8,128)(2,1)S(1)} %bitcast.34, bf16[1792,1024]{1,0:T(8,128)(2,1)} %collective-permute-done.theirs_ref), kind=kOutput, calls=%fused_computation.1 | convolution fusion | flops 822312960 | bytes 6307840 | tf_op jit(solution)/shard_map/dot_general | solution.py:141
  185.0 0.5 fusion.1
  185.5 1.0 copy.16
  186.5 11.8 %all-to-all-start.3 = ((bf16[16,64,224]{2,1,0:T(8,128)(2,1)}), bf16[16,64,224]{2,1,0:T(8,128)(2,1)S(1)}, u32[]{:S(2)}, u32[]{:S(2)}) async-start(bf16[16,64,224]{2,1,0:T(8,128)(2,1)} %bitcast.11), calls=%async_computation.3 | async-start | bytes 1048576 | tf_op jit(solution)/shard_map/all_to_all | solution.py:143
  198.3 0.7 pad_add_fusion.place_ref
  199.0 0.0 copy-start.4
  199.0 10.3 %partial_weight_grads.1 = (bf16[8,112,224]{2,1,0:T(8,128)(2,1)}, bf16[8,112,224]{2,1,0:T(8,128)(2,1)}, bf16[8,112,224]{2,1,0:T(8,128)(2,1)}, bf16[8,112,224]{2,1,0:T(8,128)(2,1)}) custom-call(s32[2]{0:T(128)} %pad_add_fusion.place_ref, bf16[1792,1024]{1,0:T(8,128)(2,1)} %all-gather.3.cloned.1.call-done.mine_ref, ...), custom_call_target="tpu_custom_call" | custom-call | tf_op jit(solution)/shard_map/partial_weight_grads/pallas_call | solution.py:87
  209.3 1.9 collective-permute-start.1
  211.2 4.3 %collective-permute-start.2 = (bf16[8,112,224]{2,1,0:T(8,128)(2,1)}, bf16[8,112,224]{2,1,0:T(8,128)(2,1)S(1)}, u32[]{:S(2)}, u32[]{:S(2)}) collective-permute-start(bf16[8,112,224]{2,1,0:T(8,128)(2,1)} %get-tuple-element.8), channel_id=1, source_target_pairs={{0,32},{16,48},{32,0},{48,16},{1,33},{17,49},{33,1},{49,17},{2,34}... | collective-permute-start | bytes 1204232 | tf_op jit(solution)/shard_map/ppermute | solution.py:130
  215.5 3.1 %collective-permute-start.3 = (bf16[8,112,224]{2,1,0:T(8,128)(2,1)}, bf16[8,112,224]{2,1,0:T(8,128)(2,1)S(1)}, u32[]{:S(2)}, u32[]{:S(2)}) collective-permute-start(bf16[8,112,224]{2,1,0:T(8,128)(2,1)} %get-tuple-element.9), channel_id=1, source_target_pairs={{0,48},{16,0},{32,16},{48,32},{1,49},{17,1},{33,17},{49,33},{2,50}... | collective-permute-start | bytes 1204232 | tf_op jit(solution)/shard_map/ppermute | solution.py:130
  218.6 0.0 copy-done.4
  218.6 6.1 %collective-permute-done.1 = bf16[8,112,224]{2,1,0:T(8,128)(2,1)S(1)} collective-permute-done((bf16[8,112,224]{2,1,0:T(8,128)(2,1)}, bf16[8,112,224]{2,1,0:T(8,128)(2,1)S(1)}, u32[]{:S(2)}, u32[]{:S(2)}) %collective-permute-start.1) | collective-permute-done | bytes 401440 | tf_op jit(solution)/shard_map/ppermute | solution.py:130
  224.7 9.4 %collective-permute-done.2 = bf16[8,112,224]{2,1,0:T(8,128)(2,1)S(1)} collective-permute-done((bf16[8,112,224]{2,1,0:T(8,128)(2,1)}, bf16[8,112,224]{2,1,0:T(8,128)(2,1)S(1)}, u32[]{:S(2)}, u32[]{:S(2)}) %collective-permute-start.2) | collective-permute-done | bytes 401440 | tf_op jit(solution)/shard_map/ppermute | solution.py:130
  234.2 2.4 collective-permute-done.3
  236.6 2.0 add_convert_fusion
  238.6 0.0 all-to-all-done.3
  238.6 3.5 %all-to-all-start.4 = ((bf16[8,112,224]{2,1,0:T(8,128)(2,1)}), bf16[8,112,224]{2,1,0:T(8,128)(2,1)S(1)}, u32[]{:S(2)}, u32[]{:S(2)}) async-start(bf16[8,112,224]{2,1,0:T(8,128)(2,1)} %add_convert_fusion), calls=%async_computation.4 | async-start | bytes 917504 | tf_op jit(solution)/shard_map/all_to_all | solution.py:131
  242.1 0.1 convert_bitcast_fusion
  242.2 0.6 copy.17
  242.8 0.6 reshape.53
  243.5 1.1 broadcast_divide_fusion
  244.5 12.8 %all-to-all-done.4 = bf16[8,112,224]{2,1,0:T(8,128)(2,1)S(1)} async-done(((bf16[8,112,224]{2,1,0:T(8,128)(2,1)}), bf16[8,112,224]{2,1,0:T(8,128)(2,1)S(1)}, u32[]{:S(2)}, u32[]{:S(2)}) %all-to-all-start.4) | async-done | bytes 401440 | tf_op jit(solution)/shard_map/all_to_all | solution.py:131
  257.3 0.7 multiply_bitcast_fusion
  (1 shorter events, 0.0 us)
Async XLA Ops:
  7.2 64.3 %copy-start = (bf16[1024,512]{1,0:T(8,128)(2,1)S(1)}, bf16[1024,512]{1,0:T(8,128)(2,1)}, u32[]{:S(2)}) copy-start(bf16[1024,512]{1,0:T(8,128)(2,1)} %param.8) | copy-start | bytes 3145732
  7.2 75.8 %copy-start.3 = (bf16[112,224]{1,0:T(8,128)(2,1)S(1)}, bf16[112,224]{1,0:T(8,128)(2,1)}, u32[]{:S(2)}) copy-start(bf16[112,224]{1,0:T(8,128)(2,1)} %param.10) | copy-start | bytes 150532
  7.2 61.5 %all-gather.3.cloned.1.call-start = ((), (), s32[]{:S(2)}) async-start(), calls=%async_computation.5 | async-start | bytes 4128768 | tf_op jit(solution)/shard_map/all_gather | solution.py:109
  68.7 113.3 %collective-permute-start = (bf16[1792,1024]{1,0:T(8,128)(2,1)}, bf16[1792,1024]{1,0:T(8,128)(2,1)}, u32[]{:S(2)}, u32[]{:S(2)}) collective-permute-start(bf16[1792,1024]{1,0:T(8,128)(2,1)} %all-gather.3.cloned.1.call-done.mine_ref), channel_id=1, source_target_pairs={{0,1},{1,0},{2,3},{3,2},{4,5},{5,4},{6,7},{7,6},{8,9},{9,8},{10,11... | collective-permute-start | bytes 11010056 | tf_op jit(solution)/shard_map/ppermute | solution.py:110
  73.7 50.5 %all-to-all-start = ((f32[32,16,224]{2,1,0:T(8,128)}), f32[32,16,224]{2,1,0:T(8,128)S(1)}, u32[]{:S(2)}, u32[]{:S(2)}) async-start(f32[32,16,224]{2,1,0:T(8,128)} %bitcast.6), calls=%async_computation | async-start | bytes 1048576 | tf_op jit(solution)/shard_map/all_to_all | solution.py:113
  125.1 24.9 %all-to-all-start.1 = ((f32[16,16,224]{2,1,0:T(8,128)}), f32[16,16,224]{2,1,0:T(8,128)S(1)}, u32[]{:S(2)}, u32[]{:S(2)}) async-start(f32[16,16,224]{2,1,0:T(8,128)} %broadcast_in_dim.7), calls=%async_computation.1 | async-start | bytes 524288 | tf_op jit(solution)/shard_map/all_to_all | solution.py:69
  150.0 1.3 copy-start.2
  151.3 11.0 %copy-start.1 = (f32[512,512]{1,0:T(8,128)S(1)}, f32[512,512]{1,0:T(8,128)}, u32[]{:S(2)}) copy-start(f32[512,512]{1,0:T(8,128)} %factor_ref.1) | copy-start | bytes 3145732
  154.6 21.2 %all-to-all-start.2 = ((f32[32,16,224]{2,1,0:T(8,128)}), f32[32,16,224]{2,1,0:T(8,128)}, u32[]{:S(2)}, u32[]{:S(2)}) async-start(f32[32,16,224]{2,1,0:T(8,128)} %broadcast_in_dim.8), calls=%async_computation.2 | async-start | bytes 1048576 | tf_op jit(solution)/shard_map/all_to_all | solution.py:69
  186.5 52.1 %all-to-all-start.3 = ((bf16[16,64,224]{2,1,0:T(8,128)(2,1)}), bf16[16,64,224]{2,1,0:T(8,128)(2,1)S(1)}, u32[]{:S(2)}, u32[]{:S(2)}) async-start(bf16[16,64,224]{2,1,0:T(8,128)(2,1)} %bitcast.11), calls=%async_computation.3 | async-start | bytes 1048576 | tf_op jit(solution)/shard_map/all_to_all | solution.py:143
  199.0 19.7 %copy-start.4 = (s32[64]{0:T(128)S(1)}, s32[64]{0:T(128)}, u32[]{:S(2)}) copy-start(s32[64]{0:T(128)} %param.11) | copy-start | bytes 772
  209.3 15.5 %collective-permute-start.1 = (bf16[8,112,224]{2,1,0:T(8,128)(2,1)}, bf16[8,112,224]{2,1,0:T(8,128)(2,1)S(1)}, u32[]{:S(2)}, u32[]{:S(2)}) collective-permute-start(bf16[8,112,224]{2,1,0:T(8,128)(2,1)} %get-tuple-element.7), channel_id=1, source_target_pairs={{0,16},{16,32},{32,48},{48,0},{1,17},{17,33},{33,49},{49,1},{2,18}... | collective-permute-start | bytes 1204232 | tf_op jit(solution)/shard_map/ppermute | solution.py:130
  211.2 23.0 %collective-permute-start.2 = (bf16[8,112,224]{2,1,0:T(8,128)(2,1)}, bf16[8,112,224]{2,1,0:T(8,128)(2,1)S(1)}, u32[]{:S(2)}, u32[]{:S(2)}) collective-permute-start(bf16[8,112,224]{2,1,0:T(8,128)(2,1)} %get-tuple-element.8), channel_id=1, source_target_pairs={{0,32},{16,48},{32,0},{48,16},{1,33},{17,49},{33,1},{49,17},{2,34}... | collective-permute-start | bytes 1204232 | tf_op jit(solution)/shard_map/ppermute | solution.py:130
  215.5 21.1 %collective-permute-start.3 = (bf16[8,112,224]{2,1,0:T(8,128)(2,1)}, bf16[8,112,224]{2,1,0:T(8,128)(2,1)S(1)}, u32[]{:S(2)}, u32[]{:S(2)}) collective-permute-start(bf16[8,112,224]{2,1,0:T(8,128)(2,1)} %get-tuple-element.9), channel_id=1, source_target_pairs={{0,48},{16,0},{32,16},{48,32},{1,49},{17,1},{33,17},{49,33},{2,50}... | collective-permute-start | bytes 1204232 | tf_op jit(solution)/shard_map/ppermute | solution.py:130
  238.6 18.7 %all-to-all-start.4 = ((bf16[8,112,224]{2,1,0:T(8,128)(2,1)}), bf16[8,112,224]{2,1,0:T(8,128)(2,1)S(1)}, u32[]{:S(2)}, u32[]{:S(2)}) async-start(bf16[8,112,224]{2,1,0:T(8,128)(2,1)} %add_convert_fusion), calls=%async_computation.4 | async-start | bytes 917504 | tf_op jit(solution)/shard_map/all_to_all | solution.py:131
Sparse Core Ops, SparseCore 0:
  10.1 58.5 all-gather.2

commit v2 on v1

--- a/solution.py
+++ b/solution.py
@@ -69,32 +69,91 @@
     return lax.all_to_all(copies, axes, split_axis=0, concat_axis=0, tiled=True)
 
 
-def weight_grad_kernel(place_ref, mine_ref, theirs_ref, residual_ref, *out_refs):
+def pack_kernel(sums_ref, rows_ref, out_ref):
+    count, width = rows_ref.shape
+    share = sums_ref.shape[0] // out_ref.shape[0]
+    for i in range(out_ref.shape[0]):
+        out_ref[i, :, width:] = jnp.zeros((out_ref.shape[1], out_ref.shape[2] - width), BF16)
+        out_ref[i, :count, :width] = rows_ref[...]
+        value = sums_ref[i * share : (i + 1) * share, :]
+        high = value.astype(BF16)
+        out_ref[i, count : count + share, :width] = high
+        out_ref[i, count + share :, :width] = (value - high.astype(F32)).astype(BF16)
+
+
+def pack(sums, rows, blocks):
+    total = rows.shape[0] + 2 * (sums.shape[0] // blocks)
+    lanes = -(-rows.shape[1] // 128) * 128
+    return pl.pallas_call(
+        pack_kernel, out_shape=jax.ShapeDtypeStruct((blocks, total, lanes), BF16), name="pack"
+    )(sums, rows)
+
+
+def unpack_kernel(packed_ref, sums_ref, rows_ref):
+    count = rows_ref.shape[0] // packed_ref.shape[0]
+    share, width = sums_ref.shape
+    total = jnp.zeros(sums_ref.shape, F32)
+    for i in range(packed_ref.shape[0]):
+        rows_ref[i * count : (i + 1) * count, :] = packed_ref[i, :count, :width]
+        total = total + packed_ref[i, count : count + share, :width].astype(F32)
+        total = total + packed_ref[i, count + share :, :width].astype(F32)
+    sums_ref[...] = total
+
+
+def unpack(packed, share, width):
+    blocks, total, _ = packed.shape
+    return pl.pallas_call(
+        unpack_kernel,
+        out_shape=[
+            jax.ShapeDtypeStruct((share, width), F32),
+            jax.ShapeDtypeStruct((blocks * (total - 2 * share), width), BF16),
+        ],
+        name="unpack",
+    )(packed)
+
+
+def products_kernel(place_ref, mine_ref, theirs_ref, residual_ref, weight_ref, dense_ref, *out_refs):
     core, chip = place_ref[0], place_ref[1]
     rows = out_refs[0].shape[1]
     per = mine_ref.shape[0] // rows
-    for d, out_ref in enumerate(out_refs):
+    cols, weights = [], []
+    for d in range(len(out_refs)):
         target = (chip + d) % len(out_refs)
         at = pl.ds(pl.multiple_of((target % per) * rows, rows), rows)
-        cols = jnp.where(target // per == core, mine_ref[at, :], theirs_ref[at, :])
-        out = lax.dot_general(cols, residual_ref[...], (((1,), (1,)), ((), ())), preferred_element_type=F32)
-        out_ref[0] = out.astype(BF16)
-
-
-def partial_weight_grads(place, mine, theirs, residual, blocks, parts, rows):
+        cols.append(jnp.where(target // per == core, mine_ref[at, :], theirs_ref[at, :]))
+        weights.append(weight_ref[target])
+    cols, weights = jnp.concatenate(cols, 0), jnp.concatenate(weights, 0)
+    out = lax.dot_general(cols, residual_ref[...], (((1,), (1,)), ((), ())), preferred_element_type=F32).astype(BF16)
+    for d, out_ref in enumerate(out_refs):
+        out_ref[0] = out[d * rows : (d + 1) * rows]
+    dense = lax.dot_general(weights, cols, (((0,), (0,)), ((), ())), preferred_element_type=F32)
+
+    @pl.when(pl.program_id(0) == 0)
+    def _():
+        dense_ref[...] = dense
+
+    @pl.when(pl.program_id(0) > 0)
+    def _():
+        dense_ref[...] += dense
+
+
+def local_products(place, mine, theirs, residual, weight, blocks, rows):
     width, docs = residual.shape
+    parts = weight.shape[0]
     spec = pl.BlockSpec((width, docs), lambda i, p: (i, 0))
-    return pl.pallas_call(
-        weight_grad_kernel,
-        out_shape=[jax.ShapeDtypeStruct((blocks, rows, width), BF16)] * parts,
+    whole = pl.BlockSpec((width, docs), lambda i, p: (0, 0))
+    return pl.pallas_call(
+        products_kernel,
+        out_shape=[jax.ShapeDtypeStruct((width, docs), F32)]
+        + [jax.ShapeDtypeStruct((blocks, rows, width), BF16)] * parts,
         grid_spec=pltpu.PrefetchScalarGridSpec(
             num_scalar_prefetch=1,
             grid=(blocks,),
-            in_specs=[spec, spec, pl.BlockSpec((width, docs), lambda i, p: (0, 0))],
-            out_specs=[pl.BlockSpec((1, rows, width), lambda i, p: (i, 0, 0))] * parts,
+            in_specs=[spec, spec, whole, pl.BlockSpec((parts, rows, width), lambda i, p: (0, i, 0))],
+            out_specs=[whole] + [pl.BlockSpec((1, rows, width), lambda i, p: (i, 0, 0))] * parts,
         ),
-        name="partial_weight_grads",
-    )(place, mine, theirs, residual)
+        name="local_products",
+    )(place, mine, theirs, residual, weight)
 
 
 def shards(grad_out, residual, confounders, gram_factor, proj_weight, doc_lengths):
@@ -103,6 +162,7 @@
     docs, width = grad_out.shape
     own_rows = proj_weight.shape[0]
     kdim = confounders.shape[1]
+    krows = kdim // ndp
     norm_scale = (docs * ndp) ** (-0.5)
     core = lax.axis_index("c")
 
@@ -110,36 +170,27 @@
     theirs = lax.ppermute(mine, "c", [(0, 1), (1, 0)])
 
     cross = lax.dot_general(confounders, grad_out, (((0,), (0,)), ((), ())), preferred_element_type=F32)
-    cross = lax.all_to_all(cross.reshape(ndp, kdim // ndp, width), DP, split_axis=0, concat_axis=0, tiled=True)
-    cross = spread(jnp.sum(cross, 0), COL, ncol)
-    cross = jnp.transpose(cross, (1, 0, 2)).reshape(kdim // ndp, ncol * width)
-
-    weight = lax.all_gather(proj_weight[None], "y", axis=0, tiled=True)
-    half = ny // 2
-    weight = [lax.all_gather(w, "x", axis=1, tiled=True) for w in (weight[:half], weight[half:])]
-    weight = jnp.concatenate(weight, 0).reshape(ndp * own_rows, width)
+    packed = lax.all_to_all(pack(cross, proj_weight, ny), "y", split_axis=0, concat_axis=0, tiled=True)
+    cross, weight = unpack(packed, nx * krows, width)
+    packed = pack(cross, weight, nx)
+    packed = lax.all_to_all(packed, "x", split_axis=0, concat_axis=0, tiled=True)
+    cross, weight = unpack(packed, krows, width)
+    cross = spread(cross, COL, ncol).reshape(nz, nc, krows, nx // nc, own_rows)
+    cross = jnp.transpose(cross, (2, 1, 3, 0, 4)).reshape(krows, ncol * width)
     moments = dot_hi(cross, weight.astype(F32))
     moments = spread(moments, DP, ndp).reshape(kdim, width)
     inverse = gram_inverse(gram_factor)
     coef_b = dot_hi(inverse, moments).astype(BF16)
 
     place = jnp.stack([core, lax.axis_index("x")]).astype(jnp.int32)
-    parts = partial_weight_grads(place, mine, theirs, residual.T, nz, nx, own_rows)
+    dense, *parts = local_products(place, mine, theirs, residual.T, weight.reshape(nx, nz * own_rows, width), nz, own_rows)
     total = parts[0].astype(F32)
     for d in range(1, nx):
         total = total + lax.ppermute(parts[d], "x", [(i, (i + d) % nx) for i in range(nx)]).astype(F32)
-    parts = lax.all_to_all(total.astype(BF16), "y", split_axis=0, concat_axis=0, tiled=True)
-    total = parts[0].astype(F32)
-    for i in range(1, ny):
-        total = total + parts[i].astype(F32)
+    total = lax.psum_scatter(total, "y", scatter_dimension=0, tiled=False)
     weight_grad = total * norm_scale
 
-    split = weight.reshape(nz, nc, width, width)
-    w_mine = lax.dynamic_index_in_dim(split, core, 1, keepdims=False).reshape(nz * width, width)
-    w_theirs = lax.dynamic_index_in_dim(split, 1 - core, 1, keepdims=False).reshape(nz * width, width)
-    pooled = jnp.dot(mine.T, w_mine, preferred_element_type=F32)
-    pooled = pooled + jnp.dot(theirs.T, w_theirs, preferred_element_type=F32)
-    pooled = pooled - jnp.dot(confounders, coef_b, preferred_element_type=F32)
+    pooled = dense.T - jnp.dot(confounders, coef_b, preferred_element_type=F32)
     doc_grad = lax.all_to_all(pooled.astype(BF16), COL, split_axis=0, concat_axis=1, tiled=True)
     token_grad = doc_grad.astype(F32) / doc_lengths.astype(F32)[:, None]
     return (token_grad, weight_grad)

time: 267 us -> 242 us (0.906)
  the two profiles are of different devices: /device:TPU:1 before, /device:TPU:2 now
where the time goes in v2:
time: 242 us; the launch traced here: 241 us
  waiting for transfers between devices  101 us (42%)
  blocking collectives  43.9 us (18%)
  starting transfers between devices  32.1 us (13%)
  Pallas kernels  29 us (12%)
  between operations  14.2 us (6%)
  matrix products  8.06 us (3%)
  other arithmetic  6.95 us (3%)
  local copies, waits for them, and re-layouts  5.9 us (2%)
    all_gather x1, waiting for transfers between devices, shards(): mine = lax.all_gather(grad_out.T, 'z', axis=0, tiled=True)  48 us
    reduce_scatter x1, waiting for transfers between devices, shards(): total = lax.psum_scatter(total, 'y', scatter_dimension=0, tiled=False)  29.5 us
    all_to_all x1, blocking collectives, shards(): lax.all_to_all(packed, 'x', split_axis=0, concat_axis=0, tiled=True)  28.7 us
    all_to_all x1, blocking collectives, spread(): return lax.all_to_all(copies, axes, split_axis=0, concat_axis=0, tiled=True)  15.2 us
    ppermute x3, waiting for transfers between devices, shards(): lax.ppermute(parts[d], 'x', [(i, (i + d) % nx) for i in range(nx)])  12.5 us
    pallas_call x1, Pallas kernels, local_products(): pl.pallas_call(products_kernel, out_shape=[jax.ShapeDtypeStruct((width, d...  11.1 us
    ppermute x3, starting transfers between devices, shards(): lax.ppermute(parts[d], 'x', [(i, (i + d) % nx) for i in range(nx)])  10.4 us
    all_to_all x1, starting transfers between devices, spread(): return lax.all_to_all(copies, axes, split_axis=0, concat_axis=0, tiled=True)  9.02 us
  transfers between devices with their start and end apart: 9, of which 6 were waited for; matrix products, arithmetic and copies ran while one was open for 7% of the time, Pallas kernels for 7%

profile of v2, /device:TPU:2, one launch (start us, length us, event | category | flops | bytes accessed | tf_op | source)
XLA Modules:
  0.0 240.8 jit_solution(16041001331559350665)
XLA Ops:
  7.2 0.0 copy-start
  7.2 0.0 all-gather.2.cloned.1.call-start
  7.2 0.7 all-gather.2.cloned.1.call-update
  7.9 0.5 copy-done
  8.4 2.3 fusion.1.sums_ref
  10.7 2.2 pack.2
  12.9 7.1 %all-to-all-start = ((bf16[8,240,256]{2,1,0:T(8,128)(2,1)}), bf16[8,240,256]{2,1,0:T(8,128)(2,1)S(1)}, u32[]{:S(2)}, u32[]{:S(2)}) async-start(bf16[8,240,256]{2,1,0:T(8,128)(2,1)} %pack.2), calls=%async_computation | async-start | bytes 1966080 | tf_op jit(solution)/shard_map/all_to_all | solution.py:173
  20.0 48.0 %all-gather.2.cloned.1.call-done.mine_ref = bf16[1792,1024]{1,0:T(8,128)(2,1)} async-done(((bf16[224,1024]{1,0:T(8,128)(2,1)}), bf16[1792,1024]{1,0:T(8,128)(2,1)}) %all-gather.2.cloned.1.call-update) | async-done | bytes 3670032 | tf_op jit(solution)/shard_map/all_gather | solution.py:169
  68.0 1.9 collective-permute-start
  69.9 0.0 all-to-all-done.packed_ref
  69.9 0.0 copy-start.2
  69.9 1.0 copy-done.2
  71.0 2.0 unpack.2
  73.0 2.5 %pack.3 = bf16[4,928,256]{2,1,0:T(8,128)(2,1)} custom-call(f32[64,224]{1,0:T(8,128)} %get-tuple-element.11.sums_ref, bf16[896,224]{1,0:T(8,128)(2,1)} %get-tuple-element.12.rows_ref), custom_call_target="tpu_custom_call" | custom-call | tf_op jit(solution)/shard_map/pack/pallas_call | solution.py:87
  75.5 28.7 %all_to_all.33.packed_ref = bf16[4,928,256]{2,1,0:T(8,128)(2,1)} all-to-all(bf16[4,928,256]{2,1,0:T(8,128)(2,1)} %pack.3), channel_id=1, replica_groups=mesh['y'=8,'x'=4,'z'=8,'c'=2] {'x'}, dimensions={0} | all-to-all | bytes 3801088 | tf_op jit(solution)/shard_map/all_to_all | solution.py:176
  104.2 2.9 %unpack.3 = (f32[16,224]{1,0:T(8,128)}, bf16[3584,224]{1,0:T(8,128)(2,1)}) custom-call(bf16[4,928,256]{2,1,0:T(8,128)(2,1)} %all_to_all.33.packed_ref), custom_call_target="tpu_custom_call" | custom-call | tf_op jit(solution)/shard_map/unpack/pallas_call | solution.py:105
  107.1 0.7 broadcast_in_dim.4
  107.8 15.2 %all_to_all.34 = f32[16,16,224]{2,1,0:T(8,128)S(1)} all-to-all(f32[16,16,224]{2,1,0:T(8,128)S(1)} %broadcast_in_dim.4), channel_id=1, replica_groups=mesh['y'=8,'x'=4,'z'=8,'c'=2] {'z','c'}, dimensions={0} | all-to-all | bytes 458752 | tf_op jit(solution)/shard_map/all_to_all | solution.py:69
  123.0 0.2 reshape.27
  123.2 0.2 copy.13
  123.4 0.2 reshape.28
  123.6 0.0 copy-start.1
  123.6 2.4 %fusion.2 = f32[16,224]{1,0:T(8,128)S(1)} fusion(f32[16,3584]{1,0:T(8,128)S(1)} %reshape.28, bf16[3584,224]{1,0:T(8,128)(2,1)} %get-tuple-element.13), kind=kOutput, calls=%fused_computation.9 | convolution fusion | flops 154140672 | bytes 1849344 | tf_op jit(solution)/shard_map/dot_general | solution.py:16
  126.0 0.9 broadcast_in_dim.5
  126.9 9.0 %all-to-all-start.3 = ((f32[32,16,224]{2,1,0:T(8,128)}), f32[32,16,224]{2,1,0:T(8,128)}, u32[]{:S(2)}, u32[]{:S(2)}) async-start(f32[32,16,224]{2,1,0:T(8,128)} %broadcast_in_dim.5), calls=%async_computation.3 | async-start | bytes 1048576 | tf_op jit(solution)/shard_map/all_to_all | solution.py:69
  135.9 0.0 copy-done.1
  135.9 8.3 %gram_inverse.1 = f32[512,512]{1,0:T(8,128)S(1)} custom-call(f32[512,512]{1,0:T(8,128)S(1)} %copy-done.1), custom_call_target="tpu_custom_call" | custom-call | tf_op jit(solution)/shard_map/gram_inverse/pallas_call | solution.py:59
  144.2 0.6 pad_add_fusion.place_ref
  144.8 9.0 %all-to-all-done.3 = f32[32,16,224]{2,1,0:T(8,128)} async-done(((f32[32,16,224]{2,1,0:T(8,128)}), f32[32,16,224]{2,1,0:T(8,128)}, u32[]{:S(2)}, u32[]{:S(2)}) %all-to-all-start.3) | async-done | bytes 458784 | tf_op jit(solution)/shard_map/all_to_all | solution.py:69
  153.8 2.9 %convolution_convert_fusion = bf16[224,512]{1,0:T(8,128)(2,1)S(1)} fusion(f32[512,224]{1,0:T(8,128)} %bitcast.6, f32[512,512]{1,0:T(8,128)S(1)} %gram_inverse.1), kind=kOutput, calls=%fused_computation | convolution fusion | flops 704757760 | bytes 1736704 | tf_op jit(solution)/shard_map/dot_general | solution.py:16
  156.7 0.5 fusion.3
  157.1 0.0 collective-permute-done.theirs_ref
  157.2 11.1 %local_products.1 = (f32[224,1024]{1,0:T(8,128)}, bf16[8,112,224]{2,1,0:T(8,128)(2,1)}, bf16[8,112,224]{2,1,0:T(8,128)(2,1)}, bf16[8,112,224]{2,1,0:T(8,128)(2,1)}, bf16[8,112,224]{2,1,0:T(8,128)(2,1)}) custom-call(s32[2]{0:T(128)} %pad_add_fusion.place_ref, bf16[1792,1024]{1,0:T(8,128)(2,1)} %all-gather.2.cloned.1.call-done.mine_ref, ...), custom_call_target="tpu_custom_call" | custom-call | tf_op jit(solution)/shard_map/local_products/pallas_call | solution.py:145
  168.2 3.4 %collective-permute-start.1 = (bf16[8,112,224]{2,1,0:T(8,128)(2,1)}, bf16[8,112,224]{2,1,0:T(8,128)(2,1)S(1)}, u32[]{:S(2)}, u32[]{:S(2)}) collective-permute-start(bf16[8,112,224]{2,1,0:T(8,128)(2,1)} %get-tuple-element.17), channel_id=1, source_target_pairs={{0,16},{16,32},{32,48},{48,0},{1,17},{17,33},{33,49},{49,1},{2,18}... | collective-permute-start | bytes 1204232 | tf_op jit(solution)/shard_map/ppermute | solution.py:189
  171.6 2.9 %collective-permute-start.2 = (bf16[8,112,224]{2,1,0:T(8,128)(2,1)}, bf16[8,112,224]{2,1,0:T(8,128)(2,1)}, u32[]{:S(2)}, u32[]{:S(2)}) collective-permute-start(bf16[8,112,224]{2,1,0:T(8,128)(2,1)} %get-tuple-element.18), channel_id=1, source_target_pairs={{0,32},{16,48},{32,0},{48,16},{1,33},{17,49},{33,1},{49,17},{2,34}... | collective-permute-start | bytes 1204232 | tf_op jit(solution)/shard_map/ppermute | solution.py:189
  174.5 4.2 %collective-permute-start.3 = (bf16[8,112,224]{2,1,0:T(8,128)(2,1)}, bf16[8,112,224]{2,1,0:T(8,128)(2,1)}, u32[]{:S(2)}, u32[]{:S(2)}) collective-permute-start(bf16[8,112,224]{2,1,0:T(8,128)(2,1)} %get-tuple-element.19), channel_id=1, source_target_pairs={{0,48},{16,0},{32,16},{48,32},{1,49},{17,1},{33,17},{49,33},{2,50}... | collective-permute-start | bytes 1204232 | tf_op jit(solution)/shard_map/ppermute | solution.py:189
  178.7 0.0 copy-start.3
  178.7 1.3 fusion
  180.0 1.0 copy.14
  181.0 3.6 %all-to-all-start.4 = ((bf16[16,64,224]{2,1,0:T(8,128)(2,1)}), bf16[16,64,224]{2,1,0:T(8,128)(2,1)S(1)}, u32[]{:S(2)}, u32[]{:S(2)}) async-start(bf16[16,64,224]{2,1,0:T(8,128)(2,1)} %bitcast.8), calls=%async_computation.4 | async-start | bytes 1048576 | tf_op jit(solution)/shard_map/all_to_all | solution.py:194
  184.6 0.0 copy-start.4
  184.6 0.0 reduce-scatter.2.cloned.1.call-start
  184.7 6.9 %collective-permute-done.1 = bf16[8,112,224]{2,1,0:T(8,128)(2,1)S(1)} collective-permute-done((bf16[8,112,224]{2,1,0:T(8,128)(2,1)}, bf16[8,112,224]{2,1,0:T(8,128)(2,1)S(1)}, u32[]{:S(2)}, u32[]{:S(2)}) %collective-permute-start.1) | collective-permute-done | bytes 401440 | tf_op jit(solution)/shard_map/ppermute | solution.py:189
  191.5 0.0 collective-permute-done.2
  191.5 5.6 %collective-permute-done.3 = bf16[8,112,224]{2,1,0:T(8,128)(2,1)} collective-permute-done((bf16[8,112,224]{2,1,0:T(8,128)(2,1)}, bf16[8,112,224]{2,1,0:T(8,128)(2,1)}, u32[]{:S(2)}, u32[]{:S(2)}) %collective-permute-start.3) | collective-permute-done | bytes 401440 | tf_op jit(solution)/shard_map/ppermute | solution.py:189
  197.1 0.0 copy-done.3
  197.1 2.3 convert_add_fusion
  199.4 0.0 reduce-scatter.2.cloned.1.call-update
  199.5 0.0 copy-done.4
  199.5 1.0 all-to-all-done.4
  200.5 0.1 convert_bitcast_fusion
  200.6 0.6 copy.15
  201.2 0.6 reshape.30
  201.9 1.1 broadcast_divide_fusion
  202.9 29.5 %reduce-scatter.2.cloned.1.call-done = f32[1,112,224]{2,1,0:T(8,128)} async-done(((f32[8,112,224]{2,1,0:T(8,128)}), f32[1,112,224]{2,1,0:T(8,128)}) %reduce-scatter.2.cloned.1.call-update) | async-done | bytes 100368 | tf_op jit(solution)/shard_map/reduce_scatter | solution.py:190
  232.4 1.6 multiply_bitcast_fusion
  (1 shorter events, 0.0 us)
Async XLA Ops:
  7.2 1.2 copy-start
  7.2 60.8 %all-gather.2.cloned.1.call-start = ((), (), s32[]{:S(2)}) async-start(), calls=%async_computation.6 | async-start | bytes 4128768 | tf_op jit(solution)/shard_map/all_gather | solution.py:169
  12.9 57.0 %all-to-all-start = ((bf16[8,240,256]{2,1,0:T(8,128)(2,1)}), bf16[8,240,256]{2,1,0:T(8,128)(2,1)S(1)}, u32[]{:S(2)}, u32[]{:S(2)}) async-start(bf16[8,240,256]{2,1,0:T(8,128)(2,1)} %pack.2), calls=%async_computation | async-start | bytes 1966080 | tf_op jit(solution)/shard_map/all_to_all | solution.py:173
  68.0 89.1 %collective-permute-start = (bf16[1792,1024]{1,0:T(8,128)(2,1)}, bf16[1792,1024]{1,0:T(8,128)(2,1)}, u32[]{:S(2)}, u32[]{:S(2)}) collective-permute-start(bf16[1792,1024]{1,0:T(8,128)(2,1)} %all-gather.2.cloned.1.call-done.mine_ref), channel_id=1, source_target_pairs={{0,1},{1,0},{2,3},{3,2},{4,5},{5,4},{6,7},{7,6},{8,9},{9,8},{10,11... | collective-permute-start | bytes 11010056 | tf_op jit(solution)/shard_map/ppermute | solution.py:170
  69.9 1.0 copy-start.2
  123.6 12.3 %copy-start.1 = (f32[512,512]{1,0:T(8,128)S(1)}, f32[512,512]{1,0:T(8,128)}, u32[]{:S(2)}) copy-start(f32[512,512]{1,0:T(8,128)} %factor_ref.1) | copy-start | bytes 3145732
  126.9 26.9 %all-to-all-start.3 = ((f32[32,16,224]{2,1,0:T(8,128)}), f32[32,16,224]{2,1,0:T(8,128)}, u32[]{:S(2)}, u32[]{:S(2)}) async-start(f32[32,16,224]{2,1,0:T(8,128)} %broadcast_in_dim.5), calls=%async_computation.3 | async-start | bytes 1048576 | tf_op jit(solution)/shard_map/all_to_all | solution.py:69
  168.2 23.3 %collective-permute-start.1 = (bf16[8,112,224]{2,1,0:T(8,128)(2,1)}, bf16[8,112,224]{2,1,0:T(8,128)(2,1)S(1)}, u32[]{:S(2)}, u32[]{:S(2)}) collective-permute-start(bf16[8,112,224]{2,1,0:T(8,128)(2,1)} %get-tuple-element.17), channel_id=1, source_target_pairs={{0,16},{16,32},{32,48},{48,0},{1,17},{17,33},{33,49},{49,1},{2,18}... | collective-permute-start | bytes 1204232 | tf_op jit(solution)/shard_map/ppermute | solution.py:189
  171.6 19.9 %collective-permute-start.2 = (bf16[8,112,224]{2,1,0:T(8,128)(2,1)}, bf16[8,112,224]{2,1,0:T(8,128)(2,1)}, u32[]{:S(2)}, u32[]{:S(2)}) collective-permute-start(bf16[8,112,224]{2,1,0:T(8,128)(2,1)} %get-tuple-element.18), channel_id=1, source_target_pairs={{0,32},{16,48},{32,0},{48,16},{1,33},{17,49},{33,1},{49,17},{2,34}... | collective-permute-start | bytes 1204232 | tf_op jit(solution)/shard_map/ppermute | solution.py:189
  174.5 22.6 %collective-permute-start.3 = (bf16[8,112,224]{2,1,0:T(8,128)(2,1)}, bf16[8,112,224]{2,1,0:T(8,128)(2,1)}, u32[]{:S(2)}, u32[]{:S(2)}) collective-permute-start(bf16[8,112,224]{2,1,0:T(8,128)(2,1)} %get-tuple-element.19), channel_id=1, source_target_pairs={{0,48},{16,0},{32,16},{48,32},{1,49},{17,1},{33,17},{49,33},{2,50}... | collective-permute-start | bytes 1204232 | tf_op jit(solution)/shard_map/ppermute | solution.py:189
  178.7 18.5 %copy-start.3 = (bf16[8,112,224]{2,1,0:T(8,128)(2,1)S(1)}, bf16[8,112,224]{2,1,0:T(8,128)(2,1)}, u32[]{:S(2)}) copy-start(bf16[8,112,224]{2,1,0:T(8,128)(2,1)} %get-tuple-element.16) | copy-start | bytes 1204228
  181.0 19.5 %all-to-all-start.4 = ((bf16[16,64,224]{2,1,0:T(8,128)(2,1)}), bf16[16,64,224]{2,1,0:T(8,128)(2,1)S(1)}, u32[]{:S(2)}, u32[]{:S(2)}) async-start(bf16[16,64,224]{2,1,0:T(8,128)(2,1)} %bitcast.8), calls=%async_computation.4 | async-start | bytes 1048576 | tf_op jit(solution)/shard_map/all_to_all | solution.py:194
  184.6 14.8 %copy-start.4 = (s32[64]{0:T(128)S(1)}, s32[64]{0:T(128)}, u32[]{:S(2)}) copy-start(s32[64]{0:T(128)} %param.11) | copy-start | bytes 772
  184.6 47.7 %reduce-scatter.2.cloned.1.call-start = ((), (), s32[]{:S(2)}) async-start(), calls=%async_computation.7 | async-start | bytes 1032192 | tf_op jit(solution)/shard_map/reduce_scatter | solution.py:190
Sparse Core Ops, SparseCore 0:
  10.1 57.8 all-gather.1
  199.6 32.7 reduce-scatter.1

commit v3 on v2

--- a/solution.py
+++ b/solution.py
@@ -112,20 +112,45 @@
     )(packed)
 
 
-def products_kernel(place_ref, mine_ref, theirs_ref, residual_ref, weight_ref, dense_ref, *out_refs):
-    core, chip = place_ref[0], place_ref[1]
-    rows = out_refs[0].shape[1]
+def select_columns(place_ref, mine_ref, theirs_ref, targets, rows):
     per = mine_ref.shape[0] // rows
-    cols, weights = [], []
-    for d in range(len(out_refs)):
-        target = (chip + d) % len(out_refs)
+    cols = []
+    for target in targets:
         at = pl.ds(pl.multiple_of((target % per) * rows, rows), rows)
-        cols.append(jnp.where(target // per == core, mine_ref[at, :], theirs_ref[at, :]))
-        weights.append(weight_ref[target])
-    cols, weights = jnp.concatenate(cols, 0), jnp.concatenate(weights, 0)
+        cols.append(jnp.where(target // per == place_ref[0], mine_ref[at, :], theirs_ref[at, :]))
+    return jnp.concatenate(cols, 0)
+
+
+def weight_grad_kernel(place_ref, mine_ref, theirs_ref, residual_ref, *out_refs):
+    count, rows = len(out_refs), out_refs[0].shape[1]
+    targets = [(place_ref[1] + d) % count for d in range(count)]
+    cols = select_columns(place_ref, mine_ref, theirs_ref, targets, rows)
     out = lax.dot_general(cols, residual_ref[...], (((1,), (1,)), ((), ())), preferred_element_type=F32).astype(BF16)
     for d, out_ref in enumerate(out_refs):
         out_ref[0] = out[d * rows : (d + 1) * rows]
+
+
+def partial_weight_grads(place, mine, theirs, residual, parts, rows):
+    width, docs = residual.shape
+    blocks = mine.shape[0] // width
+    spec = pl.BlockSpec((width, docs), lambda i, p: (i, 0))
+    return pl.pallas_call(
+        weight_grad_kernel,
+        out_shape=[jax.ShapeDtypeStruct((blocks, rows, width), BF16)] * parts,
+        grid_spec=pltpu.PrefetchScalarGridSpec(
+            num_scalar_prefetch=1,
+            grid=(blocks,),
+            in_specs=[spec, spec, pl.BlockSpec((width, docs), lambda i, p: (0, 0))],
+            out_specs=[pl.BlockSpec((1, rows, width), lambda i, p: (i, 0, 0))] * parts,
+        ),
+        name="partial_weight_grads",
+    )(place, mine, theirs, residual)
+
+
+def dense_kernel(place_ref, mine_ref, theirs_ref, weight_ref, dense_ref):
+    count, rows = weight_ref.shape[:2]
+    cols = select_columns(place_ref, mine_ref, theirs_ref, list(range(count)), rows)
+    weights = jnp.concatenate([weight_ref[d] for d in range(count)], 0)
     dense = lax.dot_general(weights, cols, (((0,), (0,)), ((), ())), preferred_element_type=F32)
 
     @pl.when(pl.program_id(0) == 0)
@@ -137,23 +162,48 @@
         dense_ref[...] += dense
 
 
-def local_products(place, mine, theirs, residual, weight, blocks, rows):
-    width, docs = residual.shape
-    parts = weight.shape[0]
+def dense_grad(place, mine, theirs, weight, rows):
+    parts, _, width = weight.shape
+    docs = mine.shape[1]
     spec = pl.BlockSpec((width, docs), lambda i, p: (i, 0))
-    whole = pl.BlockSpec((width, docs), lambda i, p: (0, 0))
-    return pl.pallas_call(
-        products_kernel,
-        out_shape=[jax.ShapeDtypeStruct((width, docs), F32)]
-        + [jax.ShapeDtypeStruct((blocks, rows, width), BF16)] * parts,
+    return pl.pallas_call(
+        dense_kernel,
+        out_shape=jax.ShapeDtypeStruct((width, docs), F32),
         grid_spec=pltpu.PrefetchScalarGridSpec(
             num_scalar_prefetch=1,
-            grid=(blocks,),
-            in_specs=[spec, spec, whole, pl.BlockSpec((parts, rows, width), lambda i, p: (0, i, 0))],
-            out_specs=[whole] + [pl.BlockSpec((1, rows, width), lambda i, p: (i, 0, 0))] * parts,
+            grid=(mine.shape[0] // width,),
+            in_specs=[spec, spec, pl.BlockSpec((parts, rows, width), lambda i, p: (0, i, 0))],
+            out_specs=pl.BlockSpec((width, docs), lambda i, p: (0, 0)),
         ),
-        name="local_products",
-    )(place, mine, theirs, residual, weight)
+        name="dense_grad",
+    )(place, mine, theirs, weight)
+
+
+def sum_kernel(place_ref, *refs):
+    count = refs[0].shape[0]
+    parts, outs = refs[:-count], refs[-count:]
+    for d, out_ref in enumerate(outs):
+        at = (place_ref[2] + d) % count
+        total = parts[0][at].astype(F32)
+        for part in parts[1:]:
+            total = total + part[at].astype(F32)
+        out_ref[...] = total.astype(BF16)
+
+
+def sum_parts(place, parts):
+    count, rows, width = parts[0].shape
+    whole = pl.BlockSpec(parts[0].shape, lambda i, p: (0, 0, 0))
+    return pl.pallas_call(
+        sum_kernel,
+        out_shape=[jax.ShapeDtypeStruct((rows, width), BF16)] * count,
+        grid_spec=pltpu.PrefetchScalarGridSpec(
+            num_scalar_prefetch=1,
+            grid=(1,),
+            in_specs=[whole] * len(parts),
+            out_specs=[pl.BlockSpec((rows, width), lambda i, p: (0, 0))] * count,
+        ),
+        name="sum_parts",
+    )(place, *parts)
 
 
 def shards(grad_out, residual, confounders, gram_factor, proj_weight, doc_lengths):
@@ -182,14 +232,17 @@
     inverse = gram_inverse(gram_factor)
     coef_b = dot_hi(inverse, moments).astype(BF16)
 
-    place = jnp.stack([core, lax.axis_index("x")]).astype(jnp.int32)
-    dense, *parts = local_products(place, mine, theirs, residual.T, weight.reshape(nx, nz * own_rows, width), nz, own_rows)
+    place = jnp.stack([core, lax.axis_index("x"), lax.axis_index("y")]).astype(jnp.int32)
+    parts = partial_weight_grads(place, mine, theirs, residual.T, nx, own_rows)
+    moved = [lax.ppermute(parts[d], "x", [(i, (i + d) % nx) for i in range(nx)]) for d in range(1, nx)]
+    parts = sum_parts(place, [parts[0], *moved])
     total = parts[0].astype(F32)
-    for d in range(1, nx):
-        total = total + lax.ppermute(parts[d], "x", [(i, (i + d) % nx) for i in range(nx)]).astype(F32)
-    total = lax.psum_scatter(total, "y", scatter_dimension=0, tiled=False)
+    for d in (4, 3, 5, 2, 6, 1, 7):
+        moved = lax.ppermute(parts[d], "y", [(i, (i + d) % ny) for i in range(ny)])
+        total = total + moved.astype(F32)
     weight_grad = total * norm_scale
 
+    dense = dense_grad(place, mine, theirs, weight.reshape(nx, nz * own_rows, width), own_rows)
     pooled = dense.T - jnp.dot(confounders, coef_b, preferred_element_type=F32)
     doc_grad = lax.all_to_all(pooled.astype(BF16), COL, split_axis=0, concat_axis=1, tiled=True)
     token_grad = doc_grad.astype(F32) / doc_lengths.astype(F32)[:, None]

time: 242 us -> 258 us (1.066)
  the two profiles are of different devices: /device:TPU:2 before, /device:TPU:26 now
where the time goes in v3:
time: 258 us; the launch traced here: 256 us
  waiting for transfers between devices  78.9 us (31%)
  starting transfers between devices  60.5 us (23%)
  blocking collectives  43.9 us (17%)
  Pallas kernels  39.2 us (15%)
  between operations  14.3 us (6%)
  matrix products  8.07 us (3%)
  local copies, waits for them, and re-layouts  6.73 us (3%)
  other arithmetic  4.61 us (2%)
    all_gather x1, waiting for transfers between devices, shards(): mine = lax.all_gather(grad_out.T, 'z', axis=0, tiled=True)  47.5 us
    all_to_all x1, blocking collectives, shards(): lax.all_to_all(packed, 'x', split_axis=0, concat_axis=0, tiled=True)  28.7 us
    ppermute x7, starting transfers between devices, shards(): moved = lax.ppermute(parts[d], 'y', [(i, (i + d) % ny) for i in range(ny)])  28.6 us
    ppermute x3, waiting for transfers between devices, shards(): lax.ppermute(parts[d], 'x', [(i, (i + d) % nx) for i in range(nx)])  18.6 us
    all_to_all x1, blocking collectives, spread(): return lax.all_to_all(copies, axes, split_axis=0, concat_axis=0, tiled=True)  15.2 us
    ppermute x3, starting transfers between devices, shards(): lax.ppermute(parts[d], 'x', [(i, (i + d) % nx) for i in range(nx)])  10.1 us
    pallas_call x1, Pallas kernels, dense_grad(): pl.pallas_call(dense_kernel, out_shape=jax.ShapeDtypeStruct((width, docs)...  9.31 us
    all_to_all x1, starting transfers between devices, spread(): return lax.all_to_all(copies, axes, split_axis=0, concat_axis=0, tiled=True)  8.96 us
  transfers between devices with their start and end apart: 15, of which 7 were waited for; matrix products, arithmetic and copies ran while one was open for 5% of the time, Pallas kernels for 12%

profile of v3, /device:TPU:26, one launch (start us, length us, event | category | flops | bytes accessed | tf_op | source)
XLA Modules:
  0.0 256.2 jit_solution(1699334103666555446)
XLA Ops:
  7.2 0.0 copy-start
  7.2 0.0 all-gather.2.cloned.1.call-start
  7.2 0.7 all-gather.2.cloned.1.call-update
  7.9 0.5 copy-done
  8.4 2.3 fusion.1.sums_ref
  10.7 2.2 pack.2
  12.9 7.3 %all-to-all-start = ((bf16[8,240,256]{2,1,0:T(8,128)(2,1)}), bf16[8,240,256]{2,1,0:T(8,128)(2,1)S(1)}, u32[]{:S(2)}, u32[]{:S(2)}) async-start(bf16[8,240,256]{2,1,0:T(8,128)(2,1)} %pack.2), calls=%async_computation | async-start | bytes 1966080 | tf_op jit(solution)/shard_map/all_to_all | solution.py:223
  20.2 47.5 %all-gather.2.cloned.1.call-done.mine_ref = bf16[1792,1024]{1,0:T(8,128)(2,1)} async-done(((bf16[224,1024]{1,0:T(8,128)(2,1)}), bf16[1792,1024]{1,0:T(8,128)(2,1)}) %all-gather.2.cloned.1.call-update) | async-done | bytes 3670032 | tf_op jit(solution)/shard_map/all_gather | solution.py:219
  67.7 1.9 collective-permute-start
  69.7 0.0 all-to-all-done.packed_ref
  69.7 1.1 copy-done.2
  70.7 2.0 unpack.2
  72.7 2.6 pack.3
  75.3 28.7 %all_to_all.33.packed_ref = bf16[4,928,256]{2,1,0:T(8,128)(2,1)} all-to-all(bf16[4,928,256]{2,1,0:T(8,128)(2,1)} %pack.3), channel_id=1, replica_groups=mesh['y'=8,'x'=4,'z'=8,'c'=2] {'x'}, dimensions={0} | all-to-all | bytes 3801088 | tf_op jit(solution)/shard_map/all_to_all | solution.py:226
  104.0 2.9 %unpack.3 = (f32[16,224]{1,0:T(8,128)}, bf16[3584,224]{1,0:T(8,128)(2,1)}) custom-call(bf16[4,928,256]{2,1,0:T(8,128)(2,1)} %all_to_all.33.packed_ref), custom_call_target="tpu_custom_call" | custom-call | tf_op jit(solution)/shard_map/unpack/pallas_call | solution.py:105
  106.9 0.7 broadcast_in_dim.4
  107.6 15.2 %all_to_all.34 = f32[16,16,224]{2,1,0:T(8,128)S(1)} all-to-all(f32[16,16,224]{2,1,0:T(8,128)S(1)} %broadcast_in_dim.4), channel_id=1, replica_groups=mesh['y'=8,'x'=4,'z'=8,'c'=2] {'z','c'}, dimensions={0} | all-to-all | bytes 458752 | tf_op jit(solution)/shard_map/all_to_all | solution.py:69
  122.8 0.2 reshape.25
  123.0 0.2 copy.13
  123.2 0.2 reshape.26
  123.3 0.0 copy-start.1
  123.4 2.4 fusion.2
  125.8 0.9 broadcast_in_dim.5
  126.6 9.0 %all-to-all-start.3 = ((f32[32,16,224]{2,1,0:T(8,128)}), f32[32,16,224]{2,1,0:T(8,128)}, u32[]{:S(2)}, u32[]{:S(2)}) async-start(f32[32,16,224]{2,1,0:T(8,128)} %broadcast_in_dim.5), calls=%async_computation.3 | async-start | bytes 1048576 | tf_op jit(solution)/shard_map/all_to_all | solution.py:69
  135.6 8.3 %gram_inverse.1 = f32[512,512]{1,0:T(8,128)S(1)} custom-call(f32[512,512]{1,0:T(8,128)S(1)} %copy-done.1), custom_call_target="tpu_custom_call" | custom-call | tf_op jit(solution)/shard_map/gram_inverse/pallas_call | solution.py:59
  143.9 0.6 pad_add_fusion.place_ref
  144.6 6.6 %all-to-all-done.3 = f32[32,16,224]{2,1,0:T(8,128)} async-done(((f32[32,16,224]{2,1,0:T(8,128)}), f32[32,16,224]{2,1,0:T(8,128)}, u32[]{:S(2)}, u32[]{:S(2)}) %all-to-all-start.3) | async-done | bytes 458784 | tf_op jit(solution)/shard_map/all_to_all | solution.py:69
  151.2 2.9 %convolution_convert_fusion = bf16[224,512]{1,0:T(8,128)(2,1)S(1)} fusion(f32[512,224]{1,0:T(8,128)} %bitcast.6, f32[512,512]{1,0:T(8,128)S(1)} %gram_inverse.1), kind=kOutput, calls=%fused_computation | convolution fusion | flops 704757760 | bytes 1736704 | tf_op jit(solution)/shard_map/dot_general | solution.py:16
  154.1 0.5 fusion.3
  154.6 0.0 collective-permute-done.theirs_ref
  154.6 9.3 %dense_grad.1 = f32[224,1024]{1,0:T(8,128)} custom-call(s32[3]{0:T(128)} %pad_add_fusion.place_ref, bf16[1792,1024]{1,0:T(8,128)(2,1)} %all-gather.2.cloned.1.call-done.mine_ref, bf16[1792,1024]{1,0:T(8,128)(2,1)} %collective-permute-done.theirs_ref, bf16[4,896,224]{2,1,0:T(8,128)(2,1)} %bitcast.23), custom_call_target="tpu_custom_call" | custom-call | tf_op jit(solution)/shard_map/dense_grad/pallas_call | solution.py:169
  163.9 1.3 fusion
  165.2 1.0 copy.14
  166.2 3.6 %all-to-all-start.4 = ((bf16[16,64,224]{2,1,0:T(8,128)(2,1)}), bf16[16,64,224]{2,1,0:T(8,128)(2,1)S(1)}, u32[]{:S(2)}, u32[]{:S(2)}) async-start(bf16[16,64,224]{2,1,0:T(8,128)(2,1)} %bitcast.8), calls=%async_computation.4 | async-start | bytes 1048576 | tf_op jit(solution)/shard_map/all_to_all | solution.py:247
  169.8 0.0 copy-start.6
  169.8 8.9 %partial_weight_grads.1 = (bf16[8,112,224]{2,1,0:T(8,128)(2,1)}, bf16[8,112,224]{2,1,0:T(8,128)(2,1)}, bf16[8,112,224]{2,1,0:T(8,128)(2,1)}, bf16[8,112,224]{2,1,0:T(8,128)(2,1)}) custom-call(s32[3]{0:T(128)} %pad_add_fusion.place_ref, bf16[1792,1024]{1,0:T(8,128)(2,1)} %all-gather.2.cloned.1.call-done.mine_ref, ...), custom_call_target="tpu_custom_call" | custom-call | tf_op jit(solution)/shard_map/partial_weight_grads/pallas_call | solution.py:137
  178.6 2.8 %collective-permute-start.1 = (bf16[8,112,224]{2,1,0:T(8,128)(2,1)}, bf16[8,112,224]{2,1,0:T(8,128)(2,1)S(1)}, u32[]{:S(2)}, u32[]{:S(2)}) collective-permute-start(bf16[8,112,224]{2,1,0:T(8,128)(2,1)} %get-tuple-element.23), channel_id=1, source_target_pairs={{0,16},{16,32},{32,48},{48,0},{1,17},{17,33},{33,49},{49,1},{2,18}... | collective-permute-start | bytes 1204232 | tf_op jit(solution)/shard_map/ppermute | solution.py:237
  181.4 5.2 %collective-permute-start.2 = (bf16[8,112,224]{2,1,0:T(8,128)(2,1)}, bf16[8,112,224]{2,1,0:T(8,128)(2,1)S(1)}, u32[]{:S(2)}, u32[]{:S(2)}) collective-permute-start(bf16[8,112,224]{2,1,0:T(8,128)(2,1)} %get-tuple-element.24), channel_id=1, source_target_pairs={{0,32},{16,48},{32,0},{48,16},{1,33},{17,49},{33,1},{49,17},{2,34}... | collective-permute-start | bytes 1204232 | tf_op jit(solution)/shard_map/ppermute | solution.py:237
  186.7 2.1 collective-permute-start.3
  188.8 5.5 %collective-permute-done.1.refs_1_ = bf16[8,112,224]{2,1,0:T(8,128)(2,1)S(1)} collective-permute-done((bf16[8,112,224]{2,1,0:T(8,128)(2,1)}, bf16[8,112,224]{2,1,0:T(8,128)(2,1)S(1)}, u32[]{:S(2)}, u32[]{:S(2)}) %collective-permute-start.1) | collective-permute-done | bytes 401440 | tf_op jit(solution)/shard_map/ppermute | solution.py:237
  194.2 4.2 %collective-permute-done.2.refs_2_ = bf16[8,112,224]{2,1,0:T(8,128)(2,1)S(1)} collective-permute-done((bf16[8,112,224]{2,1,0:T(8,128)(2,1)}, bf16[8,112,224]{2,1,0:T(8,128)(2,1)S(1)}, u32[]{:S(2)}, u32[]{:S(2)}) %collective-permute-start.2) | collective-permute-done | bytes 401440 | tf_op jit(solution)/shard_map/ppermute | solution.py:237
  198.5 8.9 %collective-permute-done.3.refs_3_ = bf16[8,112,224]{2,1,0:T(8,128)(2,1)S(1)} collective-permute-done((bf16[8,112,224]{2,1,0:T(8,128)(2,1)}, bf16[8,112,224]{2,1,0:T(8,128)(2,1)S(1)}, u32[]{:S(2)}, u32[]{:S(2)}) %collective-permute-start.3) | collective-permute-done | bytes 401440 | tf_op jit(solution)/shard_map/ppermute | solution.py:237
  207.4 0.8 copy-done.5
  208.2 3.0 %sum_parts.1 = (bf16[112,224]{1,0:T(8,128)(2,1)}, bf16[112,224]{1,0:T(8,128)(2,1)}, bf16[112,224]{1,0:T(8,128)(2,1)}, bf16[112,224]{1,0:T(8,128)(2,1)}, bf16[112...) custom-call(s32[3]{0:T(128)} %pad_add_fusion.place_ref, ...), custom_call_target="tpu_custom_call" | custom-call | tf_op jit(solution)/shard_map/sum_parts/pallas_call | solution.py:196
  211.2 3.6 %collective-permute-start.4 = (bf16[112,224]{1,0:T(8,128)(2,1)}, bf16[112,224]{1,0:T(8,128)(2,1)S(1)}, u32[]{:S(2)}, u32[]{:S(2)}) collective-permute-start(bf16[112,224]{1,0:T(8,128)(2,1)} %get-tuple-element.27), channel_id=1, source_target_pairs={{0,256},{64,320},{128,384},{192,448},{256,0},{320,64},{384,128},{4... | collective-permute-start | bytes 150536 | tf_op jit(solution)/shard_map/ppermute | solution.py:241
  214.8 6.1 %collective-permute-start.5 = (bf16[112,224]{1,0:T(8,128)(2,1)}, bf16[112,224]{1,0:T(8,128)(2,1)S(1)}, u32[]{:S(2)}, u32[]{:S(2)}) collective-permute-start(bf16[112,224]{1,0:T(8,128)(2,1)} %get-tuple-element.28), channel_id=1, source_target_pairs={{0,192},{64,256},{128,320},{192,384},{256,448},{320,0},{384,64},{4... | collective-permute-start | bytes 150536 | tf_op jit(solution)/shard_map/ppermute | solution.py:241
  220.9 1.9 collective-permute-start.6
  222.8 7.1 %collective-permute-start.7 = (bf16[112,224]{1,0:T(8,128)(2,1)}, bf16[112,224]{1,0:T(8,128)(2,1)S(1)}, u32[]{:S(2)}, u32[]{:S(2)}) collective-permute-start(bf16[112,224]{1,0:T(8,128)(2,1)} %get-tuple-element.30), channel_id=1, source_target_pairs={{0,128},{64,192},{128,256},{192,320},{256,384},{320,448},{384,0},{... | collective-permute-start | bytes 150536 | tf_op jit(solution)/shard_map/ppermute | solution.py:241
  229.9 1.9 collective-permute-start.8
  231.8 0.0 collective-permute-done.4
  231.9 6.0 %collective-permute-start.9 = (bf16[112,224]{1,0:T(8,128)(2,1)}, bf16[112,224]{1,0:T(8,128)(2,1)S(1)}, u32[]{:S(2)}, u32[]{:S(2)}) collective-permute-start(bf16[112,224]{1,0:T(8,128)(2,1)} %get-tuple-element.32), channel_id=1, source_target_pairs={{0,64},{64,128},{128,192},{192,256},{256,320},{320,384},{384,448},... | collective-permute-start | bytes 150536 | tf_op jit(solution)/shard_map/ppermute | solution.py:241
  237.9 0.0 collective-permute-done.5
  237.9 1.9 collective-permute-start.10
  239.8 0.0 collective-permute-done.6
  239.8 0.0 collective-permute-done.7
  239.9 0.0 collective-permute-done.8
  239.9 0.1 collective-permute-done.9
  240.0 5.4 %collective-permute-done.10 = bf16[112,224]{1,0:T(8,128)(2,1)S(1)} collective-permute-done((bf16[112,224]{1,0:T(8,128)(2,1)}, bf16[112,224]{1,0:T(8,128)(2,1)S(1)}, u32[]{:S(2)}, u32[]{:S(2)}) %collective-permute-start.10) | collective-permute-done | bytes 50208 | tf_op jit(solution)/shard_map/ppermute | solution.py:241
  245.4 1.5 add_multiply_fusion
  246.9 0.0 all-to-all-done.4
  246.9 0.1 convert_bitcast_fusion
  247.0 0.6 copy.15
  247.6 0.6 reshape.28
  248.3 1.1 broadcast_divide_fusion
  (9 shorter events, 0.0 us)
Async XLA Ops:
  7.2 1.2 copy-start
  7.2 60.6 %all-gather.2.cloned.1.call-start = ((), (), s32[]{:S(2)}) async-start(), calls=%async_computation.5 | async-start | bytes 4128768 | tf_op jit(solution)/shard_map/all_gather | solution.py:219
  12.9 56.7 %all-to-all-start = ((bf16[8,240,256]{2,1,0:T(8,128)(2,1)}), bf16[8,240,256]{2,1,0:T(8,128)(2,1)S(1)}, u32[]{:S(2)}, u32[]{:S(2)}) async-start(bf16[8,240,256]{2,1,0:T(8,128)(2,1)} %pack.2), calls=%async_computation | async-start | bytes 1966080 | tf_op jit(solution)/shard_map/all_to_all | solution.py:223
  67.7 86.8 %collective-permute-start = (bf16[1792,1024]{1,0:T(8,128)(2,1)}, bf16[1792,1024]{1,0:T(8,128)(2,1)}, u32[]{:S(2)}, u32[]{:S(2)}) collective-permute-start(bf16[1792,1024]{1,0:T(8,128)(2,1)} %all-gather.2.cloned.1.call-done.mine_ref), channel_id=1, source_target_pairs={{0,1},{1,0},{2,3},{3,2},{4,5},{5,4},{6,7},{7,6},{8,9},{9,8},{10,11... | collective-permute-start | bytes 11010056 | tf_op jit(solution)/shard_map/ppermute | solution.py:220
  69.7 1.1 copy-start.2
  123.3 12.3 %copy-start.1 = (f32[512,512]{1,0:T(8,128)S(1)}, f32[512,512]{1,0:T(8,128)}, u32[]{:S(2)}) copy-start(f32[512,512]{1,0:T(8,128)} %factor_ref.1) | copy-start | bytes 3145732
  126.6 24.6 %all-to-all-start.3 = ((f32[32,16,224]{2,1,0:T(8,128)}), f32[32,16,224]{2,1,0:T(8,128)}, u32[]{:S(2)}, u32[]{:S(2)}) async-start(f32[32,16,224]{2,1,0:T(8,128)} %broadcast_in_dim.5), calls=%async_computation.3 | async-start | bytes 1048576 | tf_op jit(solution)/shard_map/all_to_all | solution.py:69
  166.2 80.7 %all-to-all-start.4 = ((bf16[16,64,224]{2,1,0:T(8,128)(2,1)}), bf16[16,64,224]{2,1,0:T(8,128)(2,1)S(1)}, u32[]{:S(2)}, u32[]{:S(2)}) async-start(bf16[16,64,224]{2,1,0:T(8,128)(2,1)} %bitcast.8), calls=%async_computation.4 | async-start | bytes 1048576 | tf_op jit(solution)/shard_map/all_to_all | solution.py:247
  169.8 70.0 %copy-start.6 = (s32[64]{0:T(128)S(1)}, s32[64]{0:T(128)}, u32[]{:S(2)}) copy-start(s32[64]{0:T(128)} %param.11) | copy-start | bytes 772
  178.6 15.6 %collective-permute-start.1 = (bf16[8,112,224]{2,1,0:T(8,128)(2,1)}, bf16[8,112,224]{2,1,0:T(8,128)(2,1)S(1)}, u32[]{:S(2)}, u32[]{:S(2)}) collective-permute-start(bf16[8,112,224]{2,1,0:T(8,128)(2,1)} %get-tuple-element.23), channel_id=1, source_target_pairs={{0,16},{16,32},{32,48},{48,0},{1,17},{17,33},{33,49},{49,1},{2,18}... | collective-permute-start | bytes 1204232 | tf_op jit(solution)/shard_map/ppermute | solution.py:237
  181.4 17.0 %collective-permute-start.2 = (bf16[8,112,224]{2,1,0:T(8,128)(2,1)}, bf16[8,112,224]{2,1,0:T(8,128)(2,1)S(1)}, u32[]{:S(2)}, u32[]{:S(2)}) collective-permute-start(bf16[8,112,224]{2,1,0:T(8,128)(2,1)} %get-tuple-element.24), channel_id=1, source_target_pairs={{0,32},{16,48},{32,0},{48,16},{1,33},{17,49},{33,1},{49,17},{2,34}... | collective-permute-start | bytes 1204232 | tf_op jit(solution)/shard_map/ppermute | solution.py:237
  186.7 20.7 %collective-permute-start.3 = (bf16[8,112,224]{2,1,0:T(8,128)(2,1)}, bf16[8,112,224]{2,1,0:T(8,128)(2,1)S(1)}, u32[]{:S(2)}, u32[]{:S(2)}) collective-permute-start(bf16[8,112,224]{2,1,0:T(8,128)(2,1)} %get-tuple-element.25), channel_id=1, source_target_pairs={{0,48},{16,0},{32,16},{48,32},{1,49},{17,1},{33,17},{49,33},{2,50}... | collective-permute-start | bytes 1204232 | tf_op jit(solution)/shard_map/ppermute | solution.py:237
  194.2 13.1 %copy-start.3 = (bf16[8,112,224]{2,1,0:T(8,128)(2,1)}, bf16[8,112,224]{2,1,0:T(8,128)(2,1)S(1)}, u32[]{:S(2)}) copy-start(bf16[8,112,224]{2,1,0:T(8,128)(2,1)S(1)} %collective-permute-done.1.refs_1_) | copy-start | bytes 1204228
  198.5 8.9 %copy-start.4 = (bf16[8,112,224]{2,1,0:T(8,128)(2,1)}, bf16[8,112,224]{2,1,0:T(8,128)(2,1)S(1)}, u32[]{:S(2)}) copy-start(bf16[8,112,224]{2,1,0:T(8,128)(2,1)S(1)} %collective-permute-done.2.refs_2_) | copy-start | bytes 1204228
  207.4 0.8 copy-start.5
  211.2 20.7 %collective-permute-start.4 = (bf16[112,224]{1,0:T(8,128)(2,1)}, bf16[112,224]{1,0:T(8,128)(2,1)S(1)}, u32[]{:S(2)}, u32[]{:S(2)}) collective-permute-start(bf16[112,224]{1,0:T(8,128)(2,1)} %get-tuple-element.27), channel_id=1, source_target_pairs={{0,256},{64,320},{128,384},{192,448},{256,0},{320,64},{384,128},{4... | collective-permute-start | bytes 150536 | tf_op jit(solution)/shard_map/ppermute | solution.py:241
  214.8 23.1 %collective-permute-start.5 = (bf16[112,224]{1,0:T(8,128)(2,1)}, bf16[112,224]{1,0:T(8,128)(2,1)S(1)}, u32[]{:S(2)}, u32[]{:S(2)}) collective-permute-start(bf16[112,224]{1,0:T(8,128)(2,1)} %get-tuple-element.28), channel_id=1, source_target_pairs={{0,192},{64,256},{128,320},{192,384},{256,448},{320,0},{384,64},{4... | collective-permute-start | bytes 150536 | tf_op jit(solution)/shard_map/ppermute | solution.py:241
  220.9 19.0 %collective-permute-start.6 = (bf16[112,224]{1,0:T(8,128)(2,1)}, bf16[112,224]{1,0:T(8,128)(2,1)S(1)}, u32[]{:S(2)}, u32[]{:S(2)}) collective-permute-start(bf16[112,224]{1,0:T(8,128)(2,1)} %get-tuple-element.29), channel_id=1, source_target_pairs={{0,320},{64,384},{128,448},{192,0},{256,64},{320,128},{384,192},{4... | collective-permute-start | bytes 150536 | tf_op jit(solution)/shard_map/ppermute | solution.py:241
  222.8 17.1 %collective-permute-start.7 = (bf16[112,224]{1,0:T(8,128)(2,1)}, bf16[112,224]{1,0:T(8,128)(2,1)S(1)}, u32[]{:S(2)}, u32[]{:S(2)}) collective-permute-start(bf16[112,224]{1,0:T(8,128)(2,1)} %get-tuple-element.30), channel_id=1, source_target_pairs={{0,128},{64,192},{128,256},{192,320},{256,384},{320,448},{384,0},{... | collective-permute-start | bytes 150536 | tf_op jit(solution)/shard_map/ppermute | solution.py:241
  229.9 9.9 %collective-permute-start.8 = (bf16[112,224]{1,0:T(8,128)(2,1)}, bf16[112,224]{1,0:T(8,128)(2,1)S(1)}, u32[]{:S(2)}, u32[]{:S(2)}) collective-permute-start(bf16[112,224]{1,0:T(8,128)(2,1)} %get-tuple-element.31), channel_id=1, source_target_pairs={{0,384},{64,448},{128,0},{192,64},{256,128},{320,192},{384,256},{4... | collective-permute-start | bytes 150536 | tf_op jit(solution)/shard_map/ppermute | solution.py:241
  231.9 8.1 %collective-permute-start.9 = (bf16[112,224]{1,0:T(8,128)(2,1)}, bf16[112,224]{1,0:T(8,128)(2,1)S(1)}, u32[]{:S(2)}, u32[]{:S(2)}) collective-permute-start(bf16[112,224]{1,0:T(8,128)(2,1)} %get-tuple-element.32), channel_id=1, source_target_pairs={{0,64},{64,128},{128,192},{192,256},{256,320},{320,384},{384,448},... | collective-permute-start | bytes 150536 | tf_op jit(solution)/shard_map/ppermute | solution.py:241
  237.9 7.5 %collective-permute-start.10 = (bf16[112,224]{1,0:T(8,128)(2,1)}, bf16[112,224]{1,0:T(8,128)(2,1)S(1)}, u32[]{:S(2)}, u32[]{:S(2)}) collective-permute-start(bf16[112,224]{1,0:T(8,128)(2,1)} %get-tuple-element.33), channel_id=1, source_target_pairs={{0,448},{64,0},{128,64},{192,128},{256,192},{320,256},{384,320},{4... | collective-permute-start | bytes 150536 | tf_op jit(solution)/shard_map/ppermute | solution.py:241
Sparse Core Ops, SparseCore 0:
  10.1 57.6 all-gather.1

commit v4 on v1

--- a/solution.py
+++ b/solution.py
@@ -64,25 +64,36 @@
     )(factor)
 
 
+def lanes(width):
+    return -(-width // 128) * 128
+
+
 def spread(x, axes, count):
     copies = jnp.broadcast_to(x[None], (count,) + x.shape)
     return lax.all_to_all(copies, axes, split_axis=0, concat_axis=0, tiled=True)
 
 
+def select_columns(place_ref, mine_ref, theirs_ref, targets, rows):
+    per = mine_ref.shape[0] // rows
+    cols = []
+    for target in targets:
+        at = pl.ds(pl.multiple_of((target % per) * rows, rows), rows)
+        cols.append(jnp.where(target // per == place_ref[0], mine_ref[at, :], theirs_ref[at, :]))
+    return jnp.concatenate(cols, 0)
+
+
 def weight_grad_kernel(place_ref, mine_ref, theirs_ref, residual_ref, *out_refs):
-    core, chip = place_ref[0], place_ref[1]
-    rows = out_refs[0].shape[1]
-    per = mine_ref.shape[0] // rows
+    count, rows = len(out_refs), out_refs[0].shape[1]
+    targets = [(place_ref[1] + d) % count for d in range(count)]
+    cols = select_columns(place_ref, mine_ref, theirs_ref, targets, rows)
+    out = lax.dot_general(cols, residual_ref[...], (((1,), (0,)), ((), ())), preferred_element_type=F32).astype(BF16)
     for d, out_ref in enumerate(out_refs):
-        target = (chip + d) % len(out_refs)
-        at = pl.ds(pl.multiple_of((target % per) * rows, rows), rows)
-        cols = jnp.where(target // per == core, mine_ref[at, :], theirs_ref[at, :])
-        out = lax.dot_general(cols, residual_ref[...], (((1,), (1,)), ((), ())), preferred_element_type=F32)
-        out_ref[0] = out.astype(BF16)
-
-
-def partial_weight_grads(place, mine, theirs, residual, blocks, parts, rows):
-    width, docs = residual.shape
+        out_ref[0] = out[d * rows : (d + 1) * rows]
+
+
+def partial_weight_grads(place, mine, theirs, residual, parts, rows):
+    docs, width = residual.shape
+    blocks = mine.shape[0] // width
     spec = pl.BlockSpec((width, docs), lambda i, p: (i, 0))
     return pl.pallas_call(
         weight_grad_kernel,
@@ -90,11 +101,60 @@
         grid_spec=pltpu.PrefetchScalarGridSpec(
             num_scalar_prefetch=1,
             grid=(blocks,),
-            in_specs=[spec, spec, pl.BlockSpec((width, docs), lambda i, p: (0, 0))],
+            in_specs=[spec, spec, pl.BlockSpec((docs, width), lambda i, p: (0, 0))],
             out_specs=[pl.BlockSpec((1, rows, width), lambda i, p: (i, 0, 0))] * parts,
         ),
         name="partial_weight_grads",
     )(place, mine, theirs, residual)
+
+
+def dense_kernel(place_ref, mine_ref, theirs_ref, weight_ref, dense_ref):
+    count, rows = weight_ref.shape[:2]
+    cols = select_columns(place_ref, mine_ref, theirs_ref, list(range(count)), rows)
+    weights = jnp.concatenate([weight_ref[d][:, : dense_ref.shape[0]] for d in range(count)], 0)
+    dense = lax.dot_general(weights, cols, (((0,), (0,)), ((), ())), preferred_element_type=F32)
+
+    @pl.when(pl.program_id(0) == 0)
+    def _():
+        dense_ref[...] = dense
+
+    @pl.when(pl.program_id(0) > 0)
+    def _():
+        dense_ref[...] += dense
+
+
+def dense_grad(place, mine, theirs, weight, width, rows):
+    parts, docs = weight.shape[0], mine.shape[1]
+    spec = pl.BlockSpec((width, docs), lambda i, p: (i, 0))
+    return pl.pallas_call(
+        dense_kernel,
+        out_shape=jax.ShapeDtypeStruct((width, docs), F32),
+        grid_spec=pltpu.PrefetchScalarGridSpec(
+            num_scalar_prefetch=1,
+            grid=(mine.shape[0] // width,),
+            in_specs=[spec, spec, pl.BlockSpec((parts, rows, weight.shape[2]), lambda i, p: (0, i, 0))],
+            out_specs=pl.BlockSpec((width, docs), lambda i, p: (0, 0)),
+        ),
+        name="dense_grad",
+    )(place, mine, theirs, weight)
+
+
+def sum_kernel(*refs):
+    *parts, out_ref = refs
+    width = parts[0].shape[2]
+    for i in range(out_ref.shape[0]):
+        total = parts[0][i].astype(F32)
+        for part in parts[1:]:
+            total = total + part[i].astype(F32)
+        out_ref[i, :, :width] = total.astype(BF16)
+        out_ref[i, :, width:] = jnp.zeros((out_ref.shape[1], out_ref.shape[2] - width), BF16)
+
+
+def sum_parts(parts):
+    count, rows, width = parts[0].shape
+    return pl.pallas_call(
+        sum_kernel, out_shape=jax.ShapeDtypeStruct((count, rows, lanes(width)), BF16), name="sum_parts"
+    )(*parts)
 
 
 def shards(grad_out, residual, confounders, gram_factor, proj_weight, doc_lengths):
@@ -103,6 +163,7 @@
     docs, width = grad_out.shape
     own_rows = proj_weight.shape[0]
     kdim = confounders.shape[1]
+    krows = kdim // ndp
     norm_scale = (docs * ndp) ** (-0.5)
     core = lax.axis_index("c")
 
@@ -110,36 +171,30 @@
     theirs = lax.ppermute(mine, "c", [(0, 1), (1, 0)])
 
     cross = lax.dot_general(confounders, grad_out, (((0,), (0,)), ((), ())), preferred_element_type=F32)
-    cross = lax.all_to_all(cross.reshape(ndp, kdim // ndp, width), DP, split_axis=0, concat_axis=0, tiled=True)
-    cross = spread(jnp.sum(cross, 0), COL, ncol)
-    cross = jnp.transpose(cross, (1, 0, 2)).reshape(kdim // ndp, ncol * width)
-
-    weight = lax.all_gather(proj_weight[None], "y", axis=0, tiled=True)
-    half = ny // 2
-    weight = [lax.all_gather(w, "x", axis=1, tiled=True) for w in (weight[:half], weight[half:])]
-    weight = jnp.concatenate(weight, 0).reshape(ndp * own_rows, width)
-    moments = dot_hi(cross, weight.astype(F32))
+    cross = lax.all_to_all(cross.reshape(ndp, krows, width), DP, split_axis=0, concat_axis=0, tiled=True)
+    cross = jnp.sum(cross, 0)
+    cross = lax.all_gather(cross, COL, axis=0, tiled=False)
+    cross = cross.reshape(nz, nc, krows, nx // nc, own_rows)
+    cross = jnp.transpose(cross, (2, 1, 3, 0, 4)).reshape(krows, ncol * width)
+
+    weight = jnp.pad(proj_weight, ((0, 0), (0, lanes(width) - width)))
+    weight = spread(weight, "y", ny).reshape(ny * own_rows, lanes(width))
+    weight = spread(weight, "x", nx)
+    moments = dot_hi(cross, weight.reshape(ndp * own_rows, lanes(width))[:, :width].astype(F32))
     moments = spread(moments, DP, ndp).reshape(kdim, width)
     inverse = gram_inverse(gram_factor)
     coef_b = dot_hi(inverse, moments).astype(BF16)
 
     place = jnp.stack([core, lax.axis_index("x")]).astype(jnp.int32)
-    parts = partial_weight_grads(place, mine, theirs, residual.T, nz, nx, own_rows)
-    total = parts[0].astype(F32)
-    for d in range(1, nx):
-        total = total + lax.ppermute(parts[d], "x", [(i, (i + d) % nx) for i in range(nx)]).astype(F32)
-    parts = lax.all_to_all(total.astype(BF16), "y", split_axis=0, concat_axis=0, tiled=True)
-    total = parts[0].astype(F32)
-    for i in range(1, ny):
-        total = total + parts[i].astype(F32)
-    weight_grad = total * norm_scale
-
-    split = weight.reshape(nz, nc, width, width)
-    w_mine = lax.dynamic_index_in_dim(split, core, 1, keepdims=False).reshape(nz * width, width)
-    w_theirs = lax.dynamic_index_in_dim(split, 1 - core, 1, keepdims=False).reshape(nz * width, width)
-    pooled = jnp.dot(mine.T, w_mine, preferred_element_type=F32)
-    pooled = pooled + jnp.dot(theirs.T, w_theirs, preferred_element_type=F32)
-    pooled = pooled - jnp.dot(confounders, coef_b, preferred_element_type=F32)
+    parts = partial_weight_grads(place, mine, theirs, residual, nx, own_rows)
+    moved = [lax.ppermute(parts[d], "x", [(i, (i + d) % nx) for i in range(nx)]) for d in range(1, nx)]
+    total = sum_parts([parts[0], *moved])
+    total = lax.all_to_all(total, "y", split_axis=0, concat_axis=0, tiled=True)
+    total = total[:, :, :width].astype(F32)
+    weight_grad = sum((total[i] for i in range(1, ny)), total[0]) * norm_scale
+
+    dense = dense_grad(place, mine, theirs, weight, width, own_rows)
+    pooled = dense.T - jnp.dot(confounders, coef_b, preferred_element_type=F32)
     doc_grad = lax.all_to_all(pooled.astype(BF16), COL, split_axis=0, concat_axis=1, tiled=True)
     token_grad = doc_grad.astype(F32) / doc_lengths.astype(F32)[:, None]
     return (token_grad, weight_grad)

time: 267 us -> 220 us (0.82)
  blocking collectives: 52.8 us -> 16.2 us
  Pallas kernels: 18.6 us -> 28.8 us
  waiting for transfers between devices: 94.9 us -> 86.2 us
  matrix products: 14.5 us -> 7.05 us
  starting transfers between devices: 56.8 us -> 50.7 us
    all_gather x3 -> x1, blocking collectives: 52.8 us -> 16.2 us  [shards(): cross = lax.all_gather(cross, COL, axis=0, tiled=False)]
    all_gather x1, waiting for transfers between devices: 60.8 us -> 30.6 us  [shards(): mine = lax.all_gather(grad_out.T, 'z', axis=0, tiled=True)]
    all_to_all x2 -> x3, waiting for transfers between devices: 2.66 us -> 24.6 us  [spread(): return lax.all_to_all(copies, axes, split_axis=0, concat_axis=0, tiled=True)]
    pallas_call x0 -> x2, Pallas kernels: none -> 11.8 us  [the longest x1 9.31 us: dense_grad(): pl.pallas_call(dense_kernel, out_shape=jax.ShapeDtypeStruct((width, docs)...]
    dot_general x3 -> x1, matrix products: 6.87 us -> 0.48 us  [shards(): pooled = dense.T - jnp.dot(confounders, coef_b, preferred_element_type=F32)]
    all_to_all x1, starting transfers between devices: 11.8 us -> 7.4 us  [shards(): lax.all_to_all(pooled.astype(BF16), COL, split_axis=0, concat_axis=1, til...]
    all_to_all x2 -> x3, starting transfers between devices: 20.2 us -> 19.4 us  [spread(): return lax.all_to_all(copies, axes, split_axis=0, concat_axis=0, tiled=True)]
  transfers between devices with their start and end apart: 10 -> 11, of which waited for: 6 -> 8; matrix products, arithmetic and copies ran while one was open for 8% -> 7% of each run, Pallas kernels for 7% -> 9%
where the time goes in v4:
time: 220 us; the launch traced here: 217 us
  waiting for transfers between devices  86.2 us (39%)
  starting transfers between devices  50.7 us (23%)
  Pallas kernels  28.8 us (13%)
  blocking collectives  16.2 us (7%)
  between operations  14.2 us (6%)
  local copies, waits for them, and re-layouts  9.91 us (5%)
  matrix products  7.05 us (3%)
  other arithmetic  3.96 us (2%)
    all_gather x1, waiting for transfers between devices, shards(): mine = lax.all_gather(grad_out.T, 'z', axis=0, tiled=True)  30.6 us
    all_to_all x3, waiting for transfers between devices, spread(): return lax.all_to_all(copies, axes, split_axis=0, concat_axis=0, tiled=True)  24.6 us
    all_to_all x3, starting transfers between devices, spread(): return lax.all_to_all(copies, axes, split_axis=0, concat_axis=0, tiled=True)  19.4 us
    ppermute x3, waiting for transfers between devices, shards(): lax.ppermute(parts[d], 'x', [(i, (i + d) % nx) for i in range(nx)])  17.4 us
    all_gather x1, blocking collectives, shards(): cross = lax.all_gather(cross, COL, axis=0, tiled=False)  16.2 us
    all_to_all x1, waiting for transfers between devices, shards(): total = lax.all_to_all(total, 'y', split_axis=0, concat_axis=0, tiled=True)  12.9 us
    ppermute x3, starting transfers between devices, shards(): lax.ppermute(parts[d], 'x', [(i, (i + d) % nx) for i in range(nx)])  9.89 us
    pallas_call x1, Pallas kernels, dense_grad(): pl.pallas_call(dense_kernel, out_shape=jax.ShapeDtypeStruct((width, docs)...  9.31 us
  transfers between devices with their start and end apart: 11, of which 8 were waited for; matrix products, arithmetic and copies ran while one was open for 7% of the time, Pallas kernels for 9%

profile of v4, /device:TPU:1, one launch (start us, length us, event | category | flops | bytes accessed | tf_op | source)
XLA Modules:
  0.0 217.1 jit_solution(7109024248299111480)
XLA Ops:
  7.2 0.0 copy-start
  7.2 0.0 copy-start.3
  7.2 0.0 all-gather.3.cloned.1.call-start
  7.2 0.7 all-gather.3.cloned.1.call-update
  7.9 0.8 pad.4
  8.8 0.8 broadcast_in_dim.8
  9.6 7.6 %all-to-all-start = ((bf16[8,112,256]{2,1,0:T(8,128)(2,1)}), bf16[8,112,256]{2,1,0:T(8,128)(2,1)S(1)}, u32[]{:S(2)}, u32[]{:S(2)}) async-start(bf16[8,112,256]{2,1,0:T(8,128)(2,1)} %broadcast_in_dim.8), calls=%async_computation | async-start | bytes 917504 | tf_op jit(solution)/shard_map/all_to_all | solution.py:73
  17.2 0.0 copy-done
  17.2 0.0 copy-done.3
  17.2 1.3 fusion.5
  18.5 11.8 %all-to-all-done = bf16[8,112,256]{2,1,0:T(8,128)(2,1)S(1)} async-done(((bf16[8,112,256]{2,1,0:T(8,128)(2,1)}), bf16[8,112,256]{2,1,0:T(8,128)(2,1)S(1)}, u32[]{:S(2)}, u32[]{:S(2)}) %all-to-all-start) | async-done | bytes 458784 | tf_op jit(solution)/shard_map/all_to_all | solution.py:73
  30.3 7.8 %all-to-all-start.2 = ((f32[32,16,224]{2,1,0:T(8,128)}), f32[32,16,224]{2,1,0:T(8,128)S(1)}, u32[]{:S(2)}, u32[]{:S(2)}) async-start(f32[32,16,224]{2,1,0:T(8,128)} %bitcast.4), calls=%async_computation.2 | async-start | bytes 1048576 | tf_op jit(solution)/shard_map/all_to_all | solution.py:174
  38.1 30.6 %all-gather.3.cloned.1.call-done.mine_ref = bf16[1792,1024]{1,0:T(8,128)(2,1)} async-done(((bf16[224,1024]{1,0:T(8,128)(2,1)}), bf16[1792,1024]{1,0:T(8,128)(2,1)}) %all-gather.3.cloned.1.call-update) | async-done | bytes 3670032 | tf_op jit(solution)/shard_map/all_gather | solution.py:170
  68.7 2.7 %collective-permute-start = (bf16[1792,1024]{1,0:T(8,128)(2,1)}, bf16[1792,1024]{1,0:T(8,128)(2,1)}, u32[]{:S(2)}, u32[]{:S(2)}) collective-permute-start(bf16[1792,1024]{1,0:T(8,128)(2,1)} %all-gather.3.cloned.1.call-done.mine_ref), channel_id=1, source_target_pairs={{0,1},{1,0},{2,3},{3,2},{4,5},{5,4},{6,7},{7,6},{8,9},{9,8},{10,11... | collective-permute-start | bytes 11010056 | tf_op jit(solution)/shard_map/ppermute | solution.py:171
  71.4 0.0 all-to-all-done.2
  71.4 1.4 broadcast_in_dim.10
  72.9 4.0 %all-to-all-start.1 = ((bf16[4,896,256]{2,1,0:T(8,128)(2,1)}), bf16[4,896,256]{2,1,0:T(8,128)(2,1)S(1)}, u32[]{:S(2)}, u32[]{:S(2)}) async-start(bf16[4,896,256]{2,1,0:T(8,128)(2,1)} %broadcast_in_dim.10), calls=%async_computation.1 | async-start | bytes 3670016 | tf_op jit(solution)/shard_map/all_to_all | solution.py:73
  76.9 0.1 reduce_sum.9
  76.9 16.2 %all-gather = f32[256,224]{1,0:T(8,128)S(1)} all-gather(f32[16,224]{1,0:T(8,128)S(1)} %reduce_sum.9), channel_id=2, replica_groups=mesh['y'=8,'x'=4,'z'=8,'c'=2] {'z','c'}, dimensions={0}, use_global_device_ids=true | all-gather | bytes 243712 | tf_op jit(solution)/shard_map/all_gather | solution.py:176
  93.1 0.2 reshape.33
  93.4 0.2 copy.15
  93.5 0.2 reshape.34
  93.7 6.5 %all-to-all-done.1.weight_ref = bf16[4,896,256]{2,1,0:T(8,128)(2,1)S(1)} async-done(((bf16[4,896,256]{2,1,0:T(8,128)(2,1)}), bf16[4,896,256]{2,1,0:T(8,128)(2,1)S(1)}, u32[]{:S(2)}, u32[]{:S(2)}) %all-to-all-start.1) | async-done | bytes 1835040 | tf_op jit(solution)/shard_map/all_to_all | solution.py:73
  100.2 0.0 copy-start.2
  100.2 1.3 copy-done.2
  101.5 0.0 copy-start.1
  101.5 2.4 %fusion = f32[16,224]{1,0:T(8,128)S(1)} fusion(f32[16,3584]{1,0:T(8,128)S(1)} %reshape.34, bf16[3584,256]{1,0:T(8,128)(2,1)} %bitcast.24), kind=kOutput, calls=%fused_computation | convolution fusion | flops 154140672 | bytes 2078720 | tf_op jit(solution)/shard_map/dot_general | solution.py:16
  103.9 0.9 broadcast_in_dim.11
  104.8 7.8 %all-to-all-start.3 = ((f32[32,16,224]{2,1,0:T(8,128)}), f32[32,16,224]{2,1,0:T(8,128)}, u32[]{:S(2)}, u32[]{:S(2)}) async-start(f32[32,16,224]{2,1,0:T(8,128)} %broadcast_in_dim.11), calls=%async_computation.3 | async-start | bytes 1048576 | tf_op jit(solution)/shard_map/all_to_all | solution.py:73
  112.6 0.0 copy-done.1
  112.6 8.3 %gram_inverse.1 = f32[512,512]{1,0:T(8,128)S(1)} custom-call(f32[512,512]{1,0:T(8,128)S(1)} %copy-done.1), custom_call_target="tpu_custom_call" | custom-call | tf_op jit(solution)/shard_map/gram_inverse/pallas_call | solution.py:59
  120.9 0.6 pad_add_fusion.place_ref
  121.5 6.3 %all-to-all-done.3 = f32[32,16,224]{2,1,0:T(8,128)} async-done(((f32[32,16,224]{2,1,0:T(8,128)}), f32[32,16,224]{2,1,0:T(8,128)}, u32[]{:S(2)}, u32[]{:S(2)}) %all-to-all-start.3) | async-done | bytes 458784 | tf_op jit(solution)/shard_map/all_to_all | solution.py:73
  127.8 2.9 %convolution_convert_fusion = bf16[224,512]{1,0:T(8,128)(2,1)S(1)} fusion(f32[512,224]{1,0:T(8,128)} %bitcast.7, f32[512,512]{1,0:T(8,128)S(1)} %gram_inverse.1), kind=kOutput, calls=%fused_computation.2 | convolution fusion | flops 704757760 | bytes 1736704 | tf_op jit(solution)/shard_map/dot_general | solution.py:16
  130.7 0.5 fusion.6
  131.2 0.0 collective-permute-done.theirs_ref
  131.2 9.3 %dense_grad.1 = f32[224,1024]{1,0:T(8,128)} custom-call(s32[2]{0:T(128)} %pad_add_fusion.place_ref, bf16[1792,1024]{1,0:T(8,128)(2,1)} %all-gather.3.cloned.1.call-done.mine_ref, bf16[1792,1024]{1,0:T(8,128)(2,1)} %collective-permute-done.theirs_ref, bf16[4,896,256]{2,1,0:T(8,128)(2,1)} %copy-done.2), custom_call_target="tpu_custom_call" | custom-call | tf_op jit(solution)/shard_map/dense_grad/pallas_call | solution.py:129
  140.5 1.3 fusion.2
  141.8 1.0 copy.16
  142.8 7.4 %all-to-all-start.4 = ((bf16[16,64,224]{2,1,0:T(8,128)(2,1)}), bf16[16,64,224]{2,1,0:T(8,128)(2,1)S(1)}, u32[]{:S(2)}, u32[]{:S(2)}) async-start(bf16[16,64,224]{2,1,0:T(8,128)(2,1)} %bitcast.9), calls=%async_computation.4 | async-start | bytes 1048576 | tf_op jit(solution)/shard_map/all_to_all | solution.py:198
  150.2 0.0 copy-done.4
  150.3 1.0 copy.18.residual_ref
  151.3 0.0 copy-start.8
  151.3 8.8 %partial_weight_grads.1 = (bf16[8,112,224]{2,1,0:T(8,128)(2,1)}, bf16[8,112,224]{2,1,0:T(8,128)(2,1)}, bf16[8,112,224]{2,1,0:T(8,128)(2,1)}, bf16[8,112,224]{2,1,0:T(8,128)(2,1)}) custom-call(s32[2]{0:T(128)} %pad_add_fusion.place_ref, bf16[1792,1024]{1,0:T(8,128)(2,1)} %all-gather.3.cloned.1.call-done.mine_ref, ...), custom_call_target="tpu_custom_call" | custom-call | tf_op jit(solution)/shard_map/partial_weight_grads/pallas_call | solution.py:98
  160.0 2.5 %collective-permute-start.1 = (bf16[8,112,224]{2,1,0:T(8,128)(2,1)}, bf16[8,112,224]{2,1,0:T(8,128)(2,1)S(1)}, u32[]{:S(2)}, u32[]{:S(2)}) collective-permute-start(bf16[8,112,224]{2,1,0:T(8,128)(2,1)} %get-tuple-element.7), channel_id=1, source_target_pairs={{0,16},{16,32},{32,48},{48,0},{1,17},{17,33},{33,49},{49,1},{2,18}... | collective-permute-start | bytes 1204232 | tf_op jit(solution)/shard_map/ppermute | solution.py:190
  162.5 4.3 %collective-permute-start.2 = (bf16[8,112,224]{2,1,0:T(8,128)(2,1)}, bf16[8,112,224]{2,1,0:T(8,128)(2,1)S(1)}, u32[]{:S(2)}, u32[]{:S(2)}) collective-permute-start(bf16[8,112,224]{2,1,0:T(8,128)(2,1)} %get-tuple-element.8), channel_id=1, source_target_pairs={{0,32},{16,48},{32,0},{48,16},{1,33},{17,49},{33,1},{49,17},{2,34}... | collective-permute-start | bytes 1204232 | tf_op jit(solution)/shard_map/ppermute | solution.py:190
  166.9 3.1 %collective-permute-start.3 = (bf16[8,112,224]{2,1,0:T(8,128)(2,1)}, bf16[8,112,224]{2,1,0:T(8,128)(2,1)S(1)}, u32[]{:S(2)}, u32[]{:S(2)}) collective-permute-start(bf16[8,112,224]{2,1,0:T(8,128)(2,1)} %get-tuple-element.9), channel_id=1, source_target_pairs={{0,48},{16,0},{32,16},{48,32},{1,49},{17,1},{33,17},{49,33},{2,50}... | collective-permute-start | bytes 1204232 | tf_op jit(solution)/shard_map/ppermute | solution.py:190
  170.0 0.0 copy-done.8
  170.0 5.3 %collective-permute-done.1.refs_1_ = bf16[8,112,224]{2,1,0:T(8,128)(2,1)S(1)} collective-permute-done((bf16[8,112,224]{2,1,0:T(8,128)(2,1)}, bf16[8,112,224]{2,1,0:T(8,128)(2,1)S(1)}, u32[]{:S(2)}, u32[]{:S(2)}) %collective-permute-start.1) | collective-permute-done | bytes 401440 | tf_op jit(solution)/shard_map/ppermute | solution.py:190
  175.3 10.1 %collective-permute-done.2.refs_2_ = bf16[8,112,224]{2,1,0:T(8,128)(2,1)S(1)} collective-permute-done((bf16[8,112,224]{2,1,0:T(8,128)(2,1)}, bf16[8,112,224]{2,1,0:T(8,128)(2,1)S(1)}, u32[]{:S(2)}, u32[]{:S(2)}) %collective-permute-start.2) | collective-permute-done | bytes 401440 | tf_op jit(solution)/shard_map/ppermute | solution.py:190
  185.5 1.9 collective-permute-done.3.refs_3_
  187.4 0.0 copy-done.5
  187.4 0.0 copy-done.6
  187.4 0.8 copy-done.7
  188.2 2.5 %sum_parts.1 = bf16[8,112,256]{2,1,0:T(8,128)(2,1)} custom-call(bf16[8,112,224]{2,1,0:T(8,128)(2,1)} %get-tuple-element.6.refs_0_, bf16[8,112,224]{2,1,0:T(8,128)(2,1)} %copy-done.5, bf16[8,112,224]{2,1,0:T(8,128)(2,1)} %copy-done.6, bf16[8,112,224]{2,1,0:T(8,128)(2,1)} %copy-done.7), custom_call_target="tpu_custom_call" | custom-call | tf_op jit(solution)/shard_map/sum_parts/pallas_call | solution.py:155
  190.7 0.0 all-to-all-done.4
  190.7 3.5 %all-to-all-start.5 = ((bf16[8,112,256]{2,1,0:T(8,128)(2,1)}), bf16[8,112,256]{2,1,0:T(8,128)(2,1)S(1)}, u32[]{:S(2)}, u32[]{:S(2)}) async-start(bf16[8,112,256]{2,1,0:T(8,128)(2,1)} %sum_parts.1), calls=%async_computation.5 | async-start | bytes 917504 | tf_op jit(solution)/shard_map/all_to_all | solution.py:192
  194.2 0.1 convert_bitcast_fusion
  194.3 0.6 copy.17
  194.9 0.6 reshape.37
  195.5 1.1 broadcast_divide_fusion
  196.6 12.9 %all-to-all-done.5 = bf16[8,112,256]{2,1,0:T(8,128)(2,1)S(1)} async-done(((bf16[8,112,256]{2,1,0:T(8,128)(2,1)}), bf16[8,112,256]{2,1,0:T(8,128)(2,1)S(1)}, u32[]{:S(2)}, u32[]{:S(2)}) %all-to-all-start.5) | async-done | bytes 458784 | tf_op jit(solution)/shard_map/all_to_all | solution.py:192
  209.4 0.1 slice_convert_fusion
  209.5 0.7 fusion.4
  (5 shorter events, 0.0 us)
Async XLA Ops:
  7.2 10.0 %copy-start = (bf16[1024,512]{1,0:T(8,128)(2,1)S(1)}, bf16[1024,512]{1,0:T(8,128)(2,1)}, u32[]{:S(2)}) copy-start(bf16[1024,512]{1,0:T(8,128)(2,1)} %param.8) | copy-start | bytes 3145732
  7.2 10.0 %copy-start.3 = (bf16[1024,224]{0,1:T(8,128)(2,1)S(1)}, bf16[1024,224]{0,1:T(8,128)(2,1)}, u32[]{:S(2)}) copy-start(bf16[1024,224]{0,1:T(8,128)(2,1)} %param.6) | copy-start | bytes 1376260
  7.2 61.5 %all-gather.3.cloned.1.call-start = ((), (), s32[]{:S(2)}) async-start(), calls=%async_computation.6 | async-start | bytes 4128768 | tf_op jit(solution)/shard_map/all_gather | solution.py:170
  9.6 20.8 %all-to-all-start = ((bf16[8,112,256]{2,1,0:T(8,128)(2,1)}), bf16[8,112,256]{2,1,0:T(8,128)(2,1)S(1)}, u32[]{:S(2)}, u32[]{:S(2)}) async-start(bf16[8,112,256]{2,1,0:T(8,128)(2,1)} %broadcast_in_dim.8), calls=%async_computation | async-start | bytes 917504 | tf_op jit(solution)/shard_map/all_to_all | solution.py:73
  30.3 41.1 %all-to-all-start.2 = ((f32[32,16,224]{2,1,0:T(8,128)}), f32[32,16,224]{2,1,0:T(8,128)S(1)}, u32[]{:S(2)}, u32[]{:S(2)}) async-start(f32[32,16,224]{2,1,0:T(8,128)} %bitcast.4), calls=%async_computation.2 | async-start | bytes 1048576 | tf_op jit(solution)/shard_map/all_to_all | solution.py:174
  68.7 62.5 %collective-permute-start = (bf16[1792,1024]{1,0:T(8,128)(2,1)}, bf16[1792,1024]{1,0:T(8,128)(2,1)}, u32[]{:S(2)}, u32[]{:S(2)}) collective-permute-start(bf16[1792,1024]{1,0:T(8,128)(2,1)} %all-gather.3.cloned.1.call-done.mine_ref), channel_id=1, source_target_pairs={{0,1},{1,0},{2,3},{3,2},{4,5},{5,4},{6,7},{7,6},{8,9},{9,8},{10,11... | collective-permute-start | bytes 11010056 | tf_op jit(solution)/shard_map/ppermute | solution.py:171
  72.9 27.3 %all-to-all-start.1 = ((bf16[4,896,256]{2,1,0:T(8,128)(2,1)}), bf16[4,896,256]{2,1,0:T(8,128)(2,1)S(1)}, u32[]{:S(2)}, u32[]{:S(2)}) async-start(bf16[4,896,256]{2,1,0:T(8,128)(2,1)} %broadcast_in_dim.10), calls=%async_computation.1 | async-start | bytes 3670016 | tf_op jit(solution)/shard_map/all_to_all | solution.py:73
  100.2 1.3 copy-start.2
  101.5 11.1 %copy-start.1 = (f32[512,512]{1,0:T(8,128)S(1)}, f32[512,512]{1,0:T(8,128)}, u32[]{:S(2)}) copy-start(f32[512,512]{1,0:T(8,128)} %factor_ref.1) | copy-start | bytes 3145732
  104.8 23.0 %all-to-all-start.3 = ((f32[32,16,224]{2,1,0:T(8,128)}), f32[32,16,224]{2,1,0:T(8,128)}, u32[]{:S(2)}, u32[]{:S(2)}) async-start(f32[32,16,224]{2,1,0:T(8,128)} %broadcast_in_dim.11), calls=%async_computation.3 | async-start | bytes 1048576 | tf_op jit(solution)/shard_map/all_to_all | solution.py:73
  140.5 9.8 %copy-start.4 = (bf16[1024,224]{0,1:T(8,128)(2,1)S(1)}, bf16[1024,224]{0,1:T(8,128)(2,1)}, u32[]{:S(2)}) copy-start(bf16[1024,224]{0,1:T(8,128)(2,1)} %param.7) | copy-start | bytes 1376260
  142.8 47.8 %all-to-all-start.4 = ((bf16[16,64,224]{2,1,0:T(8,128)(2,1)}), bf16[16,64,224]{2,1,0:T(8,128)(2,1)S(1)}, u32[]{:S(2)}, u32[]{:S(2)}) async-start(bf16[16,64,224]{2,1,0:T(8,128)(2,1)} %bitcast.9), calls=%async_computation.4 | async-start | bytes 1048576 | tf_op jit(solution)/shard_map/all_to_all | solution.py:198
  151.3 18.7 %copy-start.8 = (s32[64]{0:T(128)S(1)}, s32[64]{0:T(128)}, u32[]{:S(2)}) copy-start(s32[64]{0:T(128)} %param.11) | copy-start | bytes 772
  160.0 15.3 %collective-permute-start.1 = (bf16[8,112,224]{2,1,0:T(8,128)(2,1)}, bf16[8,112,224]{2,1,0:T(8,128)(2,1)S(1)}, u32[]{:S(2)}, u32[]{:S(2)}) collective-permute-start(bf16[8,112,224]{2,1,0:T(8,128)(2,1)} %get-tuple-element.7), channel_id=1, source_target_pairs={{0,16},{16,32},{32,48},{48,0},{1,17},{17,33},{33,49},{49,1},{2,18}... | collective-permute-start | bytes 1204232 | tf_op jit(solution)/shard_map/ppermute | solution.py:190
  162.5 22.9 %collective-permute-start.2 = (bf16[8,112,224]{2,1,0:T(8,128)(2,1)}, bf16[8,112,224]{2,1,0:T(8,128)(2,1)S(1)}, u32[]{:S(2)}, u32[]{:S(2)}) collective-permute-start(bf16[8,112,224]{2,1,0:T(8,128)(2,1)} %get-tuple-element.8), channel_id=1, source_target_pairs={{0,32},{16,48},{32,0},{48,16},{1,33},{17,49},{33,1},{49,17},{2,34}... | collective-permute-start | bytes 1204232 | tf_op jit(solution)/shard_map/ppermute | solution.py:190
  166.9 20.5 %collective-permute-start.3 = (bf16[8,112,224]{2,1,0:T(8,128)(2,1)}, bf16[8,112,224]{2,1,0:T(8,128)(2,1)S(1)}, u32[]{:S(2)}, u32[]{:S(2)}) collective-permute-start(bf16[8,112,224]{2,1,0:T(8,128)(2,1)} %get-tuple-element.9), channel_id=1, source_target_pairs={{0,48},{16,0},{32,16},{48,32},{1,49},{17,1},{33,17},{49,33},{2,50}... | collective-permute-start | bytes 1204232 | tf_op jit(solution)/shard_map/ppermute | solution.py:190
  175.3 12.1 %copy-start.5 = (bf16[8,112,224]{2,1,0:T(8,128)(2,1)}, bf16[8,112,224]{2,1,0:T(8,128)(2,1)S(1)}, u32[]{:S(2)}) copy-start(bf16[8,112,224]{2,1,0:T(8,128)(2,1)S(1)} %collective-permute-done.1.refs_1_) | copy-start | bytes 1204228
  185.5 1.9 copy-start.6
  187.4 0.8 copy-start.7
  190.7 18.8 %all-to-all-start.5 = ((bf16[8,112,256]{2,1,0:T(8,128)(2,1)}), bf16[8,112,256]{2,1,0:T(8,128)(2,1)S(1)}, u32[]{:S(2)}, u32[]{:S(2)}) async-start(bf16[8,112,256]{2,1,0:T(8,128)(2,1)} %sum_parts.1), calls=%async_computation.5 | async-start | bytes 917504 | tf_op jit(solution)/shard_map/all_to_all | solution.py:192
Sparse Core Ops, SparseCore 0:
  10.1 58.5 all-gather.2

commit v5 on v4

--- a/solution.py
+++ b/solution.py
@@ -73,46 +73,30 @@
     return lax.all_to_all(copies, axes, split_axis=0, concat_axis=0, tiled=True)
 
 
-def select_columns(place_ref, mine_ref, theirs_ref, targets, rows):
-    per = mine_ref.shape[0] // rows
-    cols = []
-    for target in targets:
-        at = pl.ds(pl.multiple_of((target % per) * rows, rows), rows)
-        cols.append(jnp.where(target // per == place_ref[0], mine_ref[at, :], theirs_ref[at, :]))
-    return jnp.concatenate(cols, 0)
-
-
-def weight_grad_kernel(place_ref, mine_ref, theirs_ref, residual_ref, *out_refs):
-    count, rows = len(out_refs), out_refs[0].shape[1]
-    targets = [(place_ref[1] + d) % count for d in range(count)]
-    cols = select_columns(place_ref, mine_ref, theirs_ref, targets, rows)
-    out = lax.dot_general(cols, residual_ref[...], (((1,), (0,)), ((), ())), preferred_element_type=F32).astype(BF16)
+def products_kernel(place_ref, mine_ref, theirs_ref, residual_ref, weight_ref, dense_ref, *refs):
+    *out_refs, done_ref = refs
+    count = len(out_refs)
+    blocks, rows, width = out_refs[0].shape
+    core, chip = place_ref[0], place_ref[1]
+    per = count // 2
+    dense = None
+    for k, cols_ref in enumerate((mine_ref, theirs_ref)):
+        owner = core if k == 0 else 1 - core
+        cols = cols_ref[...]
+        out = jnp.dot(cols, residual_ref[...], preferred_element_type=F32).astype(BF16)
+        for i in range(blocks):
+            for j in range(per):
+                at = (i * per + j) * rows
+                done_ref[owner * per + j, i] = out[at : at + rows]
+        weights = [
+            weight_ref[owner * per + j, i * rows : (i + 1) * rows, :width] for i in range(blocks) for j in range(per)
+        ]
+        term = lax.dot_general(
+            jnp.concatenate(weights, 0), cols, (((0,), (0,)), ((), ())), preferred_element_type=F32
+        )
+        dense = term if dense is None else dense + term
     for d, out_ref in enumerate(out_refs):
-        out_ref[0] = out[d * rows : (d + 1) * rows]
-
-
-def partial_weight_grads(place, mine, theirs, residual, parts, rows):
-    docs, width = residual.shape
-    blocks = mine.shape[0] // width
-    spec = pl.BlockSpec((width, docs), lambda i, p: (i, 0))
-    return pl.pallas_call(
-        weight_grad_kernel,
-        out_shape=[jax.ShapeDtypeStruct((blocks, rows, width), BF16)] * parts,
-        grid_spec=pltpu.PrefetchScalarGridSpec(
-            num_scalar_prefetch=1,
-            grid=(blocks,),
-            in_specs=[spec, spec, pl.BlockSpec((docs, width), lambda i, p: (0, 0))],
-            out_specs=[pl.BlockSpec((1, rows, width), lambda i, p: (i, 0, 0))] * parts,
-        ),
-        name="partial_weight_grads",
-    )(place, mine, theirs, residual)
-
-
-def dense_kernel(place_ref, mine_ref, theirs_ref, weight_ref, dense_ref):
-    count, rows = weight_ref.shape[:2]
-    cols = select_columns(place_ref, mine_ref, theirs_ref, list(range(count)), rows)
-    weights = jnp.concatenate([weight_ref[d][:, : dense_ref.shape[0]] for d in range(count)], 0)
-    dense = lax.dot_general(weights, cols, (((0,), (0,)), ((), ())), preferred_element_type=F32)
+        out_ref[...] = done_ref[(chip + d) % count]
 
     @pl.when(pl.program_id(0) == 0)
     def _():
@@ -123,20 +107,30 @@
         dense_ref[...] += dense
 
 
-def dense_grad(place, mine, theirs, weight, width, rows):
-    parts, docs = weight.shape[0], mine.shape[1]
-    spec = pl.BlockSpec((width, docs), lambda i, p: (i, 0))
+def local_products(place, mine, theirs, residual, weight, rows, blocks=2):
+    docs, width = residual.shape
+    parts = weight.shape[0]
+    total = mine.shape[0] // width
+    spec = pl.BlockSpec((blocks * width, docs), lambda i, p: (i, 0))
     return pl.pallas_call(
-        dense_kernel,
-        out_shape=jax.ShapeDtypeStruct((width, docs), F32),
+        products_kernel,
+        out_shape=[jax.ShapeDtypeStruct((width, docs), F32)]
+        + [jax.ShapeDtypeStruct((total, rows, width), BF16)] * parts,
         grid_spec=pltpu.PrefetchScalarGridSpec(
             num_scalar_prefetch=1,
-            grid=(mine.shape[0] // width,),
-            in_specs=[spec, spec, pl.BlockSpec((parts, rows, weight.shape[2]), lambda i, p: (0, i, 0))],
-            out_specs=pl.BlockSpec((width, docs), lambda i, p: (0, 0)),
+            grid=(total // blocks,),
+            in_specs=[
+                spec,
+                spec,
+                pl.BlockSpec((docs, width), lambda i, p: (0, 0)),
+                pl.BlockSpec((parts, blocks * rows, weight.shape[2]), lambda i, p: (0, i, 0)),
+            ],
+            out_specs=[pl.BlockSpec((width, docs), lambda i, p: (0, 0))]
+            + [pl.BlockSpec((blocks, rows, width), lambda i, p: (i, 0, 0))] * parts,
+            scratch_shapes=[pltpu.VMEM((parts, blocks, rows, width), BF16)],
         ),
-        name="dense_grad",
-    )(place, mine, theirs, weight)
+        name="local_products",
+    )(place, mine, theirs, residual, weight)
 
 
 def sum_kernel(*refs):
@@ -178,7 +172,7 @@
     cross = jnp.transpose(cross, (2, 1, 3, 0, 4)).reshape(krows, ncol * width)
 
     weight = jnp.pad(proj_weight, ((0, 0), (0, lanes(width) - width)))
-    weight = spread(weight, "y", ny).reshape(ny * own_rows, lanes(width))
+    weight = lax.all_gather(weight, "y", axis=0, tiled=True)
     weight = spread(weight, "x", nx)
     moments = dot_hi(cross, weight.reshape(ndp * own_rows, lanes(width))[:, :width].astype(F32))
     moments = spread(moments, DP, ndp).reshape(kdim, width)
@@ -186,14 +180,13 @@
     coef_b = dot_hi(inverse, moments).astype(BF16)
 
     place = jnp.stack([core, lax.axis_index("x")]).astype(jnp.int32)
-    parts = partial_weight_grads(place, mine, theirs, residual, nx, own_rows)
+    dense, *parts = local_products(place, mine, theirs, residual, weight, own_rows)
     moved = [lax.ppermute(parts[d], "x", [(i, (i + d) % nx) for i in range(nx)]) for d in range(1, nx)]
     total = sum_parts([parts[0], *moved])
     total = lax.all_to_all(total, "y", split_axis=0, concat_axis=0, tiled=True)
     total = total[:, :, :width].astype(F32)
     weight_grad = sum((total[i] for i in range(1, ny)), total[0]) * norm_scale
 
-    dense = dense_grad(place, mine, theirs, weight, width, own_rows)
     pooled = dense.T - jnp.dot(confounders, coef_b, preferred_element_type=F32)
     doc_grad = lax.all_to_all(pooled.astype(BF16), COL, split_axis=0, concat_axis=1, tiled=True)
     token_grad = doc_grad.astype(F32) / doc_lengths.astype(F32)[:, None]

time: 220 us -> 233 us (1.059)
  blocking collectives: 16.2 us -> 42.4 us
  Pallas kernels: 28.8 us -> 19.9 us
  starting transfers between devices: 50.7 us -> 47.4 us
    all_gather x0 -> x1, blocking collectives: none -> 20.4 us  [shards(): weight = lax.all_gather(weight, 'y', axis=0, tiled=True)]
    all_to_all x3 -> x2, waiting for transfers between devices: 24.6 us -> 6.53 us  [spread(): return lax.all_to_all(copies, axes, split_axis=0, concat_axis=0, tiled=True)]
    all_gather x1, waiting for transfers between devices: 30.6 us -> 47.5 us  [shards(): mine = lax.all_gather(grad_out.T, 'z', axis=0, tiled=True)]
    pallas_call x2 -> x1, Pallas kernels: 18.1 us -> 9.15 us  [local_products(): pl.pallas_call(products_kernel, out_shape=[jax.ShapeDtypeStruct((width, d...]
    all_to_all x3 -> x2, starting transfers between devices: 19.4 us -> 13.4 us  [spread(): return lax.all_to_all(copies, axes, split_axis=0, concat_axis=0, tiled=True)]
    all_gather x1, blocking collectives: 16.2 us -> 22 us  [shards(): cross = lax.all_gather(cross, COL, axis=0, tiled=False)]
    all_to_all x1, starting transfers between devices: 7.76 us -> 10.5 us  [shards(): lax.all_to_all(cross.reshape(ndp, krows, width), DP, split_axis=0, concat...]
  transfers between devices with their start and end apart: 11 -> 10, of which waited for: 8 -> 6; matrix products, arithmetic and copies ran while one was open for 7% -> 7% of each run, Pallas kernels for 9% -> 5%
where the time goes in v5:
time: 233 us; the launch traced here: 230 us
  waiting for transfers between devices  85 us (36%)
  starting transfers between devices  47.4 us (20%)
  blocking collectives  42.4 us (18%)
  Pallas kernels  19.9 us (9%)
  between operations  14.3 us (6%)
  local copies, waits for them, and re-layouts  9.4 us (4%)
  matrix products  8.2 us (4%)
  other arithmetic  3.96 us (2%)
    all_gather x1, waiting for transfers between devices, shards(): mine = lax.all_gather(grad_out.T, 'z', axis=0, tiled=True)  47.5 us
    all_gather x1, blocking collectives, shards(): cross = lax.all_gather(cross, COL, axis=0, tiled=False)  22 us
    all_gather x1, blocking collectives, shards(): weight = lax.all_gather(weight, 'y', axis=0, tiled=True)  20.4 us
    ppermute x3, waiting for transfers between devices, shards(): lax.ppermute(parts[d], 'x', [(i, (i + d) % nx) for i in range(nx)])  17.4 us
    all_to_all x2, starting transfers between devices, spread(): return lax.all_to_all(copies, axes, split_axis=0, concat_axis=0, tiled=True)  13.4 us
    all_to_all x1, waiting for transfers between devices, shards(): total = lax.all_to_all(total, 'y', split_axis=0, concat_axis=0, tiled=True)  12.8 us
    all_to_all x1, starting transfers between devices, shards(): lax.all_to_all(cross.reshape(ndp, krows, width), DP, split_axis=0, concat...  10.5 us
    ppermute x3, starting transfers between devices, shards(): lax.ppermute(parts[d], 'x', [(i, (i + d) % nx) for i in range(nx)])  9.9 us
  transfers between devices with their start and end apart: 10, of which 6 were waited for; matrix products, arithmetic and copies ran while one was open for 7% of the time, Pallas kernels for 5%

profile of v5, /device:TPU:1, one launch (start us, length us, event | category | flops | bytes accessed | tf_op | source)
XLA Modules:
  0.0 230.4 jit_solution(12896306675174862452)
XLA Ops:
  7.2 0.0 copy-start
  7.2 0.0 copy-start.7
  7.2 0.0 all-gather.3.cloned.1.call-start
  7.2 0.7 all-gather.3.cloned.1.call-update
  7.9 0.5 copy-done
  8.4 2.3 fusion.5
  10.7 10.5 %all-to-all-start.1 = ((f32[32,16,224]{2,1,0:T(8,128)}), f32[32,16,224]{2,1,0:T(8,128)S(1)}, u32[]{:S(2)}, u32[]{:S(2)}) async-start(f32[32,16,224]{2,1,0:T(8,128)} %bitcast.3), calls=%async_computation.1 | async-start | bytes 1048576 | tf_op jit(solution)/shard_map/all_to_all | solution.py:168
  21.2 47.5 %all-gather.3.cloned.1.call-done.mine_ref = bf16[1792,1024]{1,0:T(8,128)(2,1)} async-done(((bf16[224,1024]{1,0:T(8,128)(2,1)}), bf16[1792,1024]{1,0:T(8,128)(2,1)}) %all-gather.3.cloned.1.call-update) | async-done | bytes 3670032 | tf_op jit(solution)/shard_map/all_gather | solution.py:164
  68.7 2.7 %collective-permute-start = (bf16[1792,1024]{1,0:T(8,128)(2,1)}, bf16[1792,1024]{1,0:T(8,128)(2,1)}, u32[]{:S(2)}, u32[]{:S(2)}) collective-permute-start(bf16[1792,1024]{1,0:T(8,128)(2,1)} %all-gather.3.cloned.1.call-done.mine_ref), channel_id=1, source_target_pairs={{0,1},{1,0},{2,3},{3,2},{4,5},{5,4},{6,7},{7,6},{8,9},{9,8},{10,11... | collective-permute-start | bytes 11010056 | tf_op jit(solution)/shard_map/ppermute | solution.py:165
  71.4 0.0 copy-done.7
  71.5 20.4 %all_gather.13 = bf16[896,256]{1,0:T(8,128)(2,1)S(1)} all-gather(bf16[112,256]{1,0:T(8,128)(2,1)S(1)} %pad.4), channel_id=1, replica_groups=mesh['y'=8,'x'=4,'z'=8,'c'=2] {'y'}, dimensions={0}, use_global_device_ids=true | all-gather | bytes 516096 | tf_op jit(solution)/shard_map/all_gather | solution.py:175
  91.8 0.0 all-to-all-done.1
  91.8 1.4 broadcast_in_dim.4
  93.3 4.0 %all-to-all-start = ((bf16[4,896,256]{2,1,0:T(8,128)(2,1)}), bf16[4,896,256]{2,1,0:T(8,128)(2,1)S(1)}, u32[]{:S(2)}, u32[]{:S(2)}) async-start(bf16[4,896,256]{2,1,0:T(8,128)(2,1)} %broadcast_in_dim.4), calls=%async_computation | async-start | bytes 3670016 | tf_op jit(solution)/shard_map/all_to_all | solution.py:73
  97.2 0.1 reduce_sum.9
  97.3 22.0 %all-gather = f32[256,224]{1,0:T(8,128)S(1)} all-gather(f32[16,224]{1,0:T(8,128)S(1)} %reduce_sum.9), channel_id=2, replica_groups=mesh['y'=8,'x'=4,'z'=8,'c'=2] {'z','c'}, dimensions={0}, use_global_device_ids=true | all-gather | bytes 243712 | tf_op jit(solution)/shard_map/all_gather | solution.py:170
  119.3 0.2 reshape.32
  119.5 0.2 copy.16
  119.7 0.9 reshape.33
  120.6 0.0 all-to-all-done.weight_ref
  120.6 0.0 copy-start.2
  120.6 1.3 copy-done.2
  121.9 0.0 copy-start.1
  121.9 2.5 %fusion = f32[16,224]{1,0:T(8,128)S(1)} fusion(f32[16,3584]{1,0:T(8,128)} %reshape.33, bf16[3584,256]{1,0:T(8,128)(2,1)} %bitcast.23), kind=kOutput, calls=%fused_computation | convolution fusion | flops 154140672 | bytes 2078720 | tf_op jit(solution)/shard_map/dot_general | solution.py:16
  124.4 0.9 broadcast_in_dim.5
  125.3 9.4 %all-to-all-start.2 = ((f32[32,16,224]{2,1,0:T(8,128)}), f32[32,16,224]{2,1,0:T(8,128)}, u32[]{:S(2)}, u32[]{:S(2)}) async-start(f32[32,16,224]{2,1,0:T(8,128)} %broadcast_in_dim.5), calls=%async_computation.2 | async-start | bytes 1048576 | tf_op jit(solution)/shard_map/all_to_all | solution.py:73
  134.7 0.0 copy-done.3
  134.7 1.0 copy.14.residual_ref
  135.7 0.0 copy-done.1
  135.7 8.3 %gram_inverse.1 = f32[512,512]{1,0:T(8,128)S(1)} custom-call(f32[512,512]{1,0:T(8,128)S(1)} %copy-done.1), custom_call_target="tpu_custom_call" | custom-call | tf_op jit(solution)/shard_map/gram_inverse/pallas_call | solution.py:59
  144.0 0.6 pad_add_fusion.place_ref
  144.6 6.5 %all-to-all-done.2 = f32[32,16,224]{2,1,0:T(8,128)} async-done(((f32[32,16,224]{2,1,0:T(8,128)}), f32[32,16,224]{2,1,0:T(8,128)}, u32[]{:S(2)}, u32[]{:S(2)}) %all-to-all-start.2) | async-done | bytes 458784 | tf_op jit(solution)/shard_map/all_to_all | solution.py:73
  151.2 2.9 %convolution_convert_fusion = bf16[224,512]{1,0:T(8,128)(2,1)S(1)} fusion(f32[512,224]{1,0:T(8,128)} %bitcast.6, f32[512,512]{1,0:T(8,128)S(1)} %gram_inverse.1), kind=kOutput, calls=%fused_computation.2 | convolution fusion | flops 704757760 | bytes 1736704 | tf_op jit(solution)/shard_map/dot_general | solution.py:16
  154.1 0.5 fusion.6
  154.6 0.0 collective-permute-done.theirs_ref
  154.6 9.1 %local_products.1 = (f32[224,1024]{1,0:T(8,128)}, bf16[8,112,224]{2,1,0:T(8,128)(2,1)}, bf16[8,112,224]{2,1,0:T(8,128)(2,1)}, bf16[8,112,224]{2,1,0:T(8,128)(2,1)}, bf16[8,112,224]{2,1,0:T(8,128)(2,1)}) custom-call(s32[2]{0:T(128)} %pad_add_fusion.place_ref, bf16[1792,1024]{1,0:T(8,128)(2,1)} %all-gather.3.cloned.1.call-done.mine_ref, ...), custom_call_target="tpu_custom_call" | custom-call | tf_op jit(solution)/shard_map/local_products/pallas_call | solution.py:115
  163.7 0.0 copy-start.8
  163.7 0.0 copy-start.9
  163.7 1.3 fusion.2
  165.1 1.0 copy.17
  166.1 7.4 %all-to-all-start.3 = ((bf16[16,64,224]{2,1,0:T(8,128)(2,1)}), bf16[16,64,224]{2,1,0:T(8,128)(2,1)S(1)}, u32[]{:S(2)}, u32[]{:S(2)}) async-start(bf16[16,64,224]{2,1,0:T(8,128)(2,1)} %bitcast.8), calls=%async_computation.3 | async-start | bytes 1048576 | tf_op jit(solution)/shard_map/all_to_all | solution.py:191
  173.4 2.5 %collective-permute-start.1 = (bf16[8,112,224]{2,1,0:T(8,128)(2,1)}, bf16[8,112,224]{2,1,0:T(8,128)(2,1)S(1)}, u32[]{:S(2)}, u32[]{:S(2)}) collective-permute-start(bf16[8,112,224]{2,1,0:T(8,128)(2,1)} %get-tuple-element.9), channel_id=1, source_target_pairs={{0,16},{16,32},{32,48},{48,0},{1,17},{17,33},{33,49},{49,1},{2,18}... | collective-permute-start | bytes 1204232 | tf_op jit(solution)/shard_map/ppermute | solution.py:184
  175.9 4.3 %collective-permute-start.2 = (bf16[8,112,224]{2,1,0:T(8,128)(2,1)}, bf16[8,112,224]{2,1,0:T(8,128)(2,1)S(1)}, u32[]{:S(2)}, u32[]{:S(2)}) collective-permute-start(bf16[8,112,224]{2,1,0:T(8,128)(2,1)} %get-tuple-element.10), channel_id=1, source_target_pairs={{0,32},{16,48},{32,0},{48,16},{1,33},{17,49},{33,1},{49,17},{2,34}... | collective-permute-start | bytes 1204232 | tf_op jit(solution)/shard_map/ppermute | solution.py:184
  180.3 0.0 copy-done.8
  180.3 3.1 %collective-permute-start.3 = (bf16[8,112,224]{2,1,0:T(8,128)(2,1)S(1)}, bf16[8,112,224]{2,1,0:T(8,128)(2,1)S(1)}, u32[]{:S(2)}, u32[]{:S(2)}) collective-permute-start(bf16[8,112,224]{2,1,0:T(8,128)(2,1)S(1)} %copy-done.8), channel_id=1, source_target_pairs={{0,48},{16,0},{32,16},{48,32},{1,49},{17,1},{33,17},{49,33},{2,50}... | collective-permute-start | bytes 1204232 | tf_op jit(solution)/shard_map/ppermute | solution.py:184
  183.4 0.0 copy-done.9
  183.4 5.3 %collective-permute-done.1.refs_1_ = bf16[8,112,224]{2,1,0:T(8,128)(2,1)S(1)} collective-permute-done((bf16[8,112,224]{2,1,0:T(8,128)(2,1)}, bf16[8,112,224]{2,1,0:T(8,128)(2,1)S(1)}, u32[]{:S(2)}, u32[]{:S(2)}) %collective-permute-start.1) | collective-permute-done | bytes 401440 | tf_op jit(solution)/shard_map/ppermute | solution.py:184
  188.7 0.0 copy-start.4
  188.7 10.2 %collective-permute-done.2.refs_2_ = bf16[8,112,224]{2,1,0:T(8,128)(2,1)S(1)} collective-permute-done((bf16[8,112,224]{2,1,0:T(8,128)(2,1)}, bf16[8,112,224]{2,1,0:T(8,128)(2,1)S(1)}, u32[]{:S(2)}, u32[]{:S(2)}) %collective-permute-start.2) | collective-permute-done | bytes 401440 | tf_op jit(solution)/shard_map/ppermute | solution.py:184
  198.9 0.0 copy-start.5
  198.9 1.9 collective-permute-done.3.refs_3_
  200.8 0.0 copy-done.4
  200.8 0.0 copy-done.5
  200.8 0.8 copy-done.6
  201.6 2.5 %sum_parts.1 = bf16[8,112,256]{2,1,0:T(8,128)(2,1)} custom-call(bf16[8,112,224]{2,1,0:T(8,128)(2,1)} %get-tuple-element.8.refs_0_, bf16[8,112,224]{2,1,0:T(8,128)(2,1)} %copy-done.4, bf16[8,112,224]{2,1,0:T(8,128)(2,1)} %copy-done.5, bf16[8,112,224]{2,1,0:T(8,128)(2,1)} %copy-done.6), custom_call_target="tpu_custom_call" | custom-call | tf_op jit(solution)/shard_map/sum_parts/pallas_call | solution.py:149
  204.0 0.0 all-to-all-done.3
  204.0 3.5 %all-to-all-start.4 = ((bf16[8,112,256]{2,1,0:T(8,128)(2,1)}), bf16[8,112,256]{2,1,0:T(8,128)(2,1)S(1)}, u32[]{:S(2)}, u32[]{:S(2)}) async-start(bf16[8,112,256]{2,1,0:T(8,128)(2,1)} %sum_parts.1), calls=%async_computation.4 | async-start | bytes 917504 | tf_op jit(solution)/shard_map/all_to_all | solution.py:186
  207.5 0.1 convert_bitcast_fusion
  207.6 0.6 copy.18
  208.2 0.6 reshape.36
  208.9 1.1 broadcast_divide_fusion
  209.9 12.8 %all-to-all-done.4 = bf16[8,112,256]{2,1,0:T(8,128)(2,1)S(1)} async-done(((bf16[8,112,256]{2,1,0:T(8,128)(2,1)}), bf16[8,112,256]{2,1,0:T(8,128)(2,1)S(1)}, u32[]{:S(2)}, u32[]{:S(2)}) %all-to-all-start.4) | async-done | bytes 458784 | tf_op jit(solution)/shard_map/all_to_all | solution.py:186
  222.8 0.1 slice_convert_fusion
  222.9 0.7 fusion.4
  (4 shorter events, 0.0 us)
Async XLA Ops:
  7.2 1.2 copy-start
  7.2 64.3 %copy-start.7 = (bf16[112,224]{1,0:T(8,128)(2,1)S(1)}, bf16[112,224]{1,0:T(8,128)(2,1)}, u32[]{:S(2)}) copy-start(bf16[112,224]{1,0:T(8,128)(2,1)} %param.10) | copy-start | bytes 150532
  7.2 61.5 %all-gather.3.cloned.1.call-start = ((), (), s32[]{:S(2)}) async-start(), calls=%async_computation.5 | async-start | bytes 4128768 | tf_op jit(solution)/shard_map/all_gather | solution.py:164
  10.7 81.1 %all-to-all-start.1 = ((f32[32,16,224]{2,1,0:T(8,128)}), f32[32,16,224]{2,1,0:T(8,128)S(1)}, u32[]{:S(2)}, u32[]{:S(2)}) async-start(f32[32,16,224]{2,1,0:T(8,128)} %bitcast.3), calls=%async_computation.1 | async-start | bytes 1048576 | tf_op jit(solution)/shard_map/all_to_all | solution.py:168
  68.7 85.9 %collective-permute-start = (bf16[1792,1024]{1,0:T(8,128)(2,1)}, bf16[1792,1024]{1,0:T(8,128)(2,1)}, u32[]{:S(2)}, u32[]{:S(2)}) collective-permute-start(bf16[1792,1024]{1,0:T(8,128)(2,1)} %all-gather.3.cloned.1.call-done.mine_ref), channel_id=1, source_target_pairs={{0,1},{1,0},{2,3},{3,2},{4,5},{5,4},{6,7},{7,6},{8,9},{9,8},{10,11... | collective-permute-start | bytes 11010056 | tf_op jit(solution)/shard_map/ppermute | solution.py:165
  93.3 27.3 %all-to-all-start = ((bf16[4,896,256]{2,1,0:T(8,128)(2,1)}), bf16[4,896,256]{2,1,0:T(8,128)(2,1)S(1)}, u32[]{:S(2)}, u32[]{:S(2)}) async-start(bf16[4,896,256]{2,1,0:T(8,128)(2,1)} %broadcast_in_dim.4), calls=%async_computation | async-start | bytes 3670016 | tf_op jit(solution)/shard_map/all_to_all | solution.py:73
  120.6 1.3 copy-start.2
  121.9 12.8 %copy-start.3 = (bf16[1024,224]{0,1:T(8,128)(2,1)S(1)}, bf16[1024,224]{0,1:T(8,128)(2,1)}, u32[]{:S(2)}) copy-start(bf16[1024,224]{0,1:T(8,128)(2,1)} %param.7) | copy-start | bytes 1376260
  121.9 13.8 %copy-start.1 = (f32[512,512]{1,0:T(8,128)S(1)}, f32[512,512]{1,0:T(8,128)}, u32[]{:S(2)}) copy-start(f32[512,512]{1,0:T(8,128)} %factor_ref.1) | copy-start | bytes 3145732
  125.3 25.9 %all-to-all-start.2 = ((f32[32,16,224]{2,1,0:T(8,128)}), f32[32,16,224]{2,1,0:T(8,128)}, u32[]{:S(2)}, u32[]{:S(2)}) async-start(f32[32,16,224]{2,1,0:T(8,128)} %broadcast_in_dim.5), calls=%async_computation.2 | async-start | bytes 1048576 | tf_op jit(solution)/shard_map/all_to_all | solution.py:73
  163.7 16.5 %copy-start.8 = (bf16[8,112,224]{2,1,0:T(8,128)(2,1)S(1)}, bf16[8,112,224]{2,1,0:T(8,128)(2,1)}, u32[]{:S(2)}) copy-start(bf16[8,112,224]{2,1,0:T(8,128)(2,1)} %get-tuple-element.11) | copy-start | bytes 1204228
  163.7 19.7 %copy-start.9 = (s32[64]{0:T(128)S(1)}, s32[64]{0:T(128)}, u32[]{:S(2)}) copy-start(s32[64]{0:T(128)} %param.11) | copy-start | bytes 772
  166.1 38.0 %all-to-all-start.3 = ((bf16[16,64,224]{2,1,0:T(8,128)(2,1)}), bf16[16,64,224]{2,1,0:T(8,128)(2,1)S(1)}, u32[]{:S(2)}, u32[]{:S(2)}) async-start(bf16[16,64,224]{2,1,0:T(8,128)(2,1)} %bitcast.8), calls=%async_computation.3 | async-start | bytes 1048576 | tf_op jit(solution)/shard_map/all_to_all | solution.py:191
  173.4 15.3 %collective-permute-start.1 = (bf16[8,112,224]{2,1,0:T(8,128)(2,1)}, bf16[8,112,224]{2,1,0:T(8,128)(2,1)S(1)}, u32[]{:S(2)}, u32[]{:S(2)}) collective-permute-start(bf16[8,112,224]{2,1,0:T(8,128)(2,1)} %get-tuple-element.9), channel_id=1, source_target_pairs={{0,16},{16,32},{32,48},{48,0},{1,17},{17,33},{33,49},{49,1},{2,18}... | collective-permute-start | bytes 1204232 | tf_op jit(solution)/shard_map/ppermute | solution.py:184
  175.9 22.9 %collective-permute-start.2 = (bf16[8,112,224]{2,1,0:T(8,128)(2,1)}, bf16[8,112,224]{2,1,0:T(8,128)(2,1)S(1)}, u32[]{:S(2)}, u32[]{:S(2)}) collective-permute-start(bf16[8,112,224]{2,1,0:T(8,128)(2,1)} %get-tuple-element.10), channel_id=1, source_target_pairs={{0,32},{16,48},{32,0},{48,16},{1,33},{17,49},{33,1},{49,17},{2,34}... | collective-permute-start | bytes 1204232 | tf_op jit(solution)/shard_map/ppermute | solution.py:184
  180.3 20.5 %collective-permute-start.3 = (bf16[8,112,224]{2,1,0:T(8,128)(2,1)S(1)}, bf16[8,112,224]{2,1,0:T(8,128)(2,1)S(1)}, u32[]{:S(2)}, u32[]{:S(2)}) collective-permute-start(bf16[8,112,224]{2,1,0:T(8,128)(2,1)S(1)} %copy-done.8), channel_id=1, source_target_pairs={{0,48},{16,0},{32,16},{48,32},{1,49},{17,1},{33,17},{49,33},{2,50}... | collective-permute-start | bytes 1204232 | tf_op jit(solution)/shard_map/ppermute | solution.py:184
  188.7 12.1 %copy-start.4 = (bf16[8,112,224]{2,1,0:T(8,128)(2,1)}, bf16[8,112,224]{2,1,0:T(8,128)(2,1)S(1)}, u32[]{:S(2)}) copy-start(bf16[8,112,224]{2,1,0:T(8,128)(2,1)S(1)} %collective-permute-done.1.refs_1_) | copy-start | bytes 1204228
  198.9 1.9 copy-start.5
  200.8 0.8 copy-start.6
  204.0 18.7 %all-to-all-start.4 = ((bf16[8,112,256]{2,1,0:T(8,128)(2,1)}), bf16[8,112,256]{2,1,0:T(8,128)(2,1)S(1)}, u32[]{:S(2)}, u32[]{:S(2)}) async-start(bf16[8,112,256]{2,1,0:T(8,128)(2,1)} %sum_parts.1), calls=%async_computation.4 | async-start | bytes 917504 | tf_op jit(solution)/shard_map/all_to_all | solution.py:186
Sparse Core Ops, SparseCore 0:
  10.1 58.5 all-gather.2

commit v6 on v4

--- a/solution.py
+++ b/solution.py
@@ -1,3 +1,5 @@
+import functools
+
 import jax
 import jax.numpy as jnp
 from jax import lax
@@ -73,46 +75,54 @@
     return lax.all_to_all(copies, axes, split_axis=0, concat_axis=0, tiled=True)
 
 
-def select_columns(place_ref, mine_ref, theirs_ref, targets, rows):
-    per = mine_ref.shape[0] // rows
-    cols = []
-    for target in targets:
-        at = pl.ds(pl.multiple_of((target % per) * rows, rows), rows)
-        cols.append(jnp.where(target // per == place_ref[0], mine_ref[at, :], theirs_ref[at, :]))
-    return jnp.concatenate(cols, 0)
-
-
-def weight_grad_kernel(place_ref, mine_ref, theirs_ref, residual_ref, *out_refs):
-    count, rows = len(out_refs), out_refs[0].shape[1]
-    targets = [(place_ref[1] + d) % count for d in range(count)]
-    cols = select_columns(place_ref, mine_ref, theirs_ref, targets, rows)
-    out = lax.dot_general(cols, residual_ref[...], (((1,), (0,)), ((), ())), preferred_element_type=F32).astype(BF16)
+def weight_grad_kernel(place_ref, mine_ref, theirs_ref, residual_ref, *refs):
+    *out_refs, done_ref = refs
+    count = len(out_refs)
+    blocks, rows, _ = out_refs[0].shape
+    core, chip = place_ref[0], place_ref[1]
+    per = count // 2
+    for owner, cols_ref in ((core, mine_ref), (1 - core, theirs_ref)):
+        out = jnp.dot(cols_ref[...], residual_ref[...], preferred_element_type=F32).astype(BF16)
+        for i in range(blocks):
+            for j in range(per):
+                at = (i * per + j) * rows
+                done_ref[owner * per + j, i] = out[at : at + rows]
     for d, out_ref in enumerate(out_refs):
-        out_ref[0] = out[d * rows : (d + 1) * rows]
-
-
-def partial_weight_grads(place, mine, theirs, residual, parts, rows):
+        out_ref[...] = done_ref[(chip + d) % count]
+
+
+def partial_weight_grads(place, mine, theirs, residual, parts, rows, blocks=2):
     docs, width = residual.shape
-    blocks = mine.shape[0] // width
-    spec = pl.BlockSpec((width, docs), lambda i, p: (i, 0))
+    total = mine.shape[0] // width
+    spec = pl.BlockSpec((blocks * width, docs), lambda i, p: (i, 0))
     return pl.pallas_call(
         weight_grad_kernel,
-        out_shape=[jax.ShapeDtypeStruct((blocks, rows, width), BF16)] * parts,
+        out_shape=[jax.ShapeDtypeStruct((total, rows, width), BF16)] * parts,
         grid_spec=pltpu.PrefetchScalarGridSpec(
             num_scalar_prefetch=1,
-            grid=(blocks,),
+            grid=(total // blocks,),
             in_specs=[spec, spec, pl.BlockSpec((docs, width), lambda i, p: (0, 0))],
-            out_specs=[pl.BlockSpec((1, rows, width), lambda i, p: (i, 0, 0))] * parts,
+            out_specs=[pl.BlockSpec((blocks, rows, width), lambda i, p: (i, 0, 0))] * parts,
+            scratch_shapes=[pltpu.VMEM((parts, blocks, rows, width), BF16)],
         ),
         name="partial_weight_grads",
     )(place, mine, theirs, residual)
 
 
-def dense_kernel(place_ref, mine_ref, theirs_ref, weight_ref, dense_ref):
-    count, rows = weight_ref.shape[:2]
-    cols = select_columns(place_ref, mine_ref, theirs_ref, list(range(count)), rows)
-    weights = jnp.concatenate([weight_ref[d][:, : dense_ref.shape[0]] for d in range(count)], 0)
-    dense = lax.dot_general(weights, cols, (((0,), (0,)), ((), ())), preferred_element_type=F32)
+def dense_kernel(place_ref, mine_ref, theirs_ref, weight_ref, dense_ref, *, rows):
+    width, core = dense_ref.shape[0], place_ref[0]
+    per = weight_ref.shape[0] // 2
+    dense = None
+    for owner, cols_ref in ((core, mine_ref), (1 - core, theirs_ref)):
+        weights = [
+            weight_ref[owner * per + j, i * rows : (i + 1) * rows, :width]
+            for i in range(weight_ref.shape[1] // rows)
+            for j in range(per)
+        ]
+        term = lax.dot_general(
+            jnp.concatenate(weights, 0), cols_ref[...], (((0,), (0,)), ((), ())), preferred_element_type=F32
+        )
+        dense = term if dense is None else dense + term
 
     @pl.when(pl.program_id(0) == 0)
     def _():
@@ -123,16 +133,16 @@
         dense_ref[...] += dense
 
 
-def dense_grad(place, mine, theirs, weight, width, rows):
+def dense_grad(place, mine, theirs, weight, width, rows, blocks=2):
     parts, docs = weight.shape[0], mine.shape[1]
-    spec = pl.BlockSpec((width, docs), lambda i, p: (i, 0))
-    return pl.pallas_call(
-        dense_kernel,
+    spec = pl.BlockSpec((blocks * width, docs), lambda i, p: (i, 0))
+    return pl.pallas_call(
+        functools.partial(dense_kernel, rows=rows),
         out_shape=jax.ShapeDtypeStruct((width, docs), F32),
         grid_spec=pltpu.PrefetchScalarGridSpec(
             num_scalar_prefetch=1,
-            grid=(mine.shape[0] // width,),
-            in_specs=[spec, spec, pl.BlockSpec((parts, rows, weight.shape[2]), lambda i, p: (0, i, 0))],
+            grid=(mine.shape[0] // (blocks * width),),
+            in_specs=[spec, spec, pl.BlockSpec((parts, blocks * rows, weight.shape[2]), lambda i, p: (0, i, 0))],
             out_specs=pl.BlockSpec((width, docs), lambda i, p: (0, 0)),
         ),
         name="dense_grad",

time: 220 us -> 216 us (0.982)
  Pallas kernels: 28.8 us -> 25 us
    pallas_call x2, Pallas kernels: 18.1 us -> 14.2 us  [the longest x1 7.17 us: dense_grad(): pl.pallas_call(functools.partial(dense_kernel, rows=rows), out_shape=jax....]
  transfers between devices with their start and end apart: 11 -> 11, of which waited for: 8 -> 8; matrix products, arithmetic and copies ran while one was open for 7% -> 7% of each run, Pallas kernels for 9% -> 8%
where the time goes in v6:
time: 216 us; the launch traced here: 213 us
  waiting for transfers between devices  86.1 us (40%)
  starting transfers between devices  50.7 us (23%)
  Pallas kernels  25 us (12%)
  blocking collectives  16.2 us (8%)
  between operations  14.2 us (7%)
  local copies, waits for them, and re-layouts  9.91 us (5%)
  matrix products  7.05 us (3%)
  other arithmetic  3.96 us (2%)
    all_gather x1, waiting for transfers between devices, shards(): mine = lax.all_gather(grad_out.T, 'z', axis=0, tiled=True)  30.6 us
    all_to_all x3, waiting for transfers between devices, spread(): return lax.all_to_all(copies, axes, split_axis=0, concat_axis=0, tiled=True)  24.6 us
    all_to_all x3, starting transfers between devices, spread(): return lax.all_to_all(copies, axes, split_axis=0, concat_axis=0, tiled=True)  19.4 us
    ppermute x3, waiting for transfers between devices, shards(): lax.ppermute(parts[d], 'x', [(i, (i + d) % nx) for i in range(nx)])  17.4 us
    all_gather x1, blocking collectives, shards(): cross = lax.all_gather(cross, COL, axis=0, tiled=False)  16.2 us
    all_to_all x1, waiting for transfers between devices, shards(): total = lax.all_to_all(total, 'y', split_axis=0, concat_axis=0, tiled=True)  12.8 us
    ppermute x3, starting transfers between devices, shards(): lax.ppermute(parts[d], 'x', [(i, (i + d) % nx) for i in range(nx)])  9.89 us
    pallas_call x1, Pallas kernels, gram_inverse(): pl.pallas_call(gram_inverse_kernel, out_shape=jax.ShapeDtypeStruct(factor...  8.3 us
  transfers between devices with their start and end apart: 11, of which 8 were waited for; matrix products, arithmetic and copies ran while one was open for 7% of the time, Pallas kernels for 8%

profile of v6, /device:TPU:1, one launch (start us, length us, event | category | flops | bytes accessed | tf_op | source)
XLA Modules:
  0.0 213.2 jit_solution(18292098066324856671)
XLA Ops:
  7.2 0.0 copy-start
  7.2 0.0 copy-start.3
  7.2 0.0 all-gather.3.cloned.1.call-start
  7.2 0.7 all-gather.3.cloned.1.call-update
  7.9 0.8 pad.4
  8.8 0.8 broadcast_in_dim.8
  9.6 7.6 %all-to-all-start = ((bf16[8,112,256]{2,1,0:T(8,128)(2,1)}), bf16[8,112,256]{2,1,0:T(8,128)(2,1)S(1)}, u32[]{:S(2)}, u32[]{:S(2)}) async-start(bf16[8,112,256]{2,1,0:T(8,128)(2,1)} %broadcast_in_dim.8), calls=%async_computation | async-start | bytes 917504 | tf_op jit(solution)/shard_map/all_to_all | solution.py:75
  17.2 0.0 copy-done
  17.2 0.0 copy-done.3
  17.2 1.3 fusion.5
  18.5 11.8 %all-to-all-done = bf16[8,112,256]{2,1,0:T(8,128)(2,1)S(1)} async-done(((bf16[8,112,256]{2,1,0:T(8,128)(2,1)}), bf16[8,112,256]{2,1,0:T(8,128)(2,1)S(1)}, u32[]{:S(2)}, u32[]{:S(2)}) %all-to-all-start) | async-done | bytes 458784 | tf_op jit(solution)/shard_map/all_to_all | solution.py:75
  30.3 7.8 %all-to-all-start.2 = ((f32[32,16,224]{2,1,0:T(8,128)}), f32[32,16,224]{2,1,0:T(8,128)S(1)}, u32[]{:S(2)}, u32[]{:S(2)}) async-start(f32[32,16,224]{2,1,0:T(8,128)} %bitcast.4), calls=%async_computation.2 | async-start | bytes 1048576 | tf_op jit(solution)/shard_map/all_to_all | solution.py:184
  38.1 30.6 %all-gather.3.cloned.1.call-done.mine_ref = bf16[1792,1024]{1,0:T(8,128)(2,1)} async-done(((bf16[224,1024]{1,0:T(8,128)(2,1)}), bf16[1792,1024]{1,0:T(8,128)(2,1)}) %all-gather.3.cloned.1.call-update) | async-done | bytes 3670032 | tf_op jit(solution)/shard_map/all_gather | solution.py:180
  68.7 2.7 %collective-permute-start = (bf16[1792,1024]{1,0:T(8,128)(2,1)}, bf16[1792,1024]{1,0:T(8,128)(2,1)}, u32[]{:S(2)}, u32[]{:S(2)}) collective-permute-start(bf16[1792,1024]{1,0:T(8,128)(2,1)} %all-gather.3.cloned.1.call-done.mine_ref), channel_id=1, source_target_pairs={{0,1},{1,0},{2,3},{3,2},{4,5},{5,4},{6,7},{7,6},{8,9},{9,8},{10,11... | collective-permute-start | bytes 11010056 | tf_op jit(solution)/shard_map/ppermute | solution.py:181
  71.4 0.0 all-to-all-done.2
  71.4 1.4 broadcast_in_dim.10
  72.9 4.0 %all-to-all-start.1 = ((bf16[4,896,256]{2,1,0:T(8,128)(2,1)}), bf16[4,896,256]{2,1,0:T(8,128)(2,1)S(1)}, u32[]{:S(2)}, u32[]{:S(2)}) async-start(bf16[4,896,256]{2,1,0:T(8,128)(2,1)} %broadcast_in_dim.10), calls=%async_computation.1 | async-start | bytes 3670016 | tf_op jit(solution)/shard_map/all_to_all | solution.py:75
  76.9 0.1 reduce_sum.9
  76.9 16.2 %all-gather = f32[256,224]{1,0:T(8,128)S(1)} all-gather(f32[16,224]{1,0:T(8,128)S(1)} %reduce_sum.9), channel_id=2, replica_groups=mesh['y'=8,'x'=4,'z'=8,'c'=2] {'z','c'}, dimensions={0}, use_global_device_ids=true | all-gather | bytes 243712 | tf_op jit(solution)/shard_map/all_gather | solution.py:186
  93.1 0.2 reshape.33
  93.4 0.2 copy.15
  93.5 0.2 reshape.34
  93.7 6.5 %all-to-all-done.1.weight_ref = bf16[4,896,256]{2,1,0:T(8,128)(2,1)S(1)} async-done(((bf16[4,896,256]{2,1,0:T(8,128)(2,1)}), bf16[4,896,256]{2,1,0:T(8,128)(2,1)S(1)}, u32[]{:S(2)}, u32[]{:S(2)}) %all-to-all-start.1) | async-done | bytes 1835040 | tf_op jit(solution)/shard_map/all_to_all | solution.py:75
  100.2 0.0 copy-start.2
  100.2 1.3 copy-done.2
  101.5 0.0 copy-start.1
  101.5 2.4 %fusion = f32[16,224]{1,0:T(8,128)S(1)} fusion(f32[16,3584]{1,0:T(8,128)S(1)} %reshape.34, bf16[3584,256]{1,0:T(8,128)(2,1)} %bitcast.24), kind=kOutput, calls=%fused_computation | convolution fusion | flops 154140672 | bytes 2078720 | tf_op jit(solution)/shard_map/dot_general | solution.py:18
  103.9 0.9 broadcast_in_dim.11
  104.8 7.8 %all-to-all-start.3 = ((f32[32,16,224]{2,1,0:T(8,128)}), f32[32,16,224]{2,1,0:T(8,128)}, u32[]{:S(2)}, u32[]{:S(2)}) async-start(f32[32,16,224]{2,1,0:T(8,128)} %broadcast_in_dim.11), calls=%async_computation.3 | async-start | bytes 1048576 | tf_op jit(solution)/shard_map/all_to_all | solution.py:75
  112.6 0.0 copy-done.1
  112.6 8.3 %gram_inverse.1 = f32[512,512]{1,0:T(8,128)S(1)} custom-call(f32[512,512]{1,0:T(8,128)S(1)} %copy-done.1), custom_call_target="tpu_custom_call" | custom-call | tf_op jit(solution)/shard_map/gram_inverse/pallas_call | solution.py:61
  120.9 0.6 pad_add_fusion.place_ref
  121.5 6.3 %all-to-all-done.3 = f32[32,16,224]{2,1,0:T(8,128)} async-done(((f32[32,16,224]{2,1,0:T(8,128)}), f32[32,16,224]{2,1,0:T(8,128)}, u32[]{:S(2)}, u32[]{:S(2)}) %all-to-all-start.3) | async-done | bytes 458784 | tf_op jit(solution)/shard_map/all_to_all | solution.py:75
  127.8 2.9 %convolution_convert_fusion = bf16[224,512]{1,0:T(8,128)(2,1)S(1)} fusion(f32[512,224]{1,0:T(8,128)} %bitcast.7, f32[512,512]{1,0:T(8,128)S(1)} %gram_inverse.1), kind=kOutput, calls=%fused_computation.2 | convolution fusion | flops 704757760 | bytes 1736704 | tf_op jit(solution)/shard_map/dot_general | solution.py:18
  130.7 0.5 fusion.6
  131.2 0.0 collective-permute-done.theirs_ref
  131.2 7.2 %dense_grad.1 = f32[224,1024]{1,0:T(8,128)} custom-call(s32[2]{0:T(128)} %pad_add_fusion.place_ref, bf16[1792,1024]{1,0:T(8,128)(2,1)} %all-gather.3.cloned.1.call-done.mine_ref, bf16[1792,1024]{1,0:T(8,128)(2,1)} %collective-permute-done.theirs_ref, bf16[4,896,256]{2,1,0:T(8,128)(2,1)} %copy-done.2), custom_call_target="tpu_custom_call" | custom-call | tf_op jit(solution)/shard_map/dense_grad/pallas_call | solution.py:139
  138.4 0.0 copy-start.4
  138.4 1.3 fusion.2
  139.7 1.0 copy.16
  140.7 7.4 %all-to-all-start.4 = ((bf16[16,64,224]{2,1,0:T(8,128)(2,1)}), bf16[16,64,224]{2,1,0:T(8,128)(2,1)S(1)}, u32[]{:S(2)}, u32[]{:S(2)}) async-start(bf16[16,64,224]{2,1,0:T(8,128)(2,1)} %bitcast.9), calls=%async_computation.4 | async-start | bytes 1048576 | tf_op jit(solution)/shard_map/all_to_all | solution.py:208
  148.1 0.0 copy-done.4
  148.1 1.0 copy.18.residual_ref
  149.1 7.0 %partial_weight_grads.1 = (bf16[8,112,224]{2,1,0:T(8,128)(2,1)}, bf16[8,112,224]{2,1,0:T(8,128)(2,1)}, bf16[8,112,224]{2,1,0:T(8,128)(2,1)}, bf16[8,112,224]{2,1,0:T(8,128)(2,1)}) custom-call(s32[2]{0:T(128)} %pad_add_fusion.place_ref, bf16[1792,1024]{1,0:T(8,128)(2,1)} %all-gather.3.cloned.1.call-done.mine_ref, ...), custom_call_target="tpu_custom_call" | custom-call | tf_op jit(solution)/shard_map/partial_weight_grads/pallas_call | solution.py:98
  156.1 2.5 %collective-permute-start.1 = (bf16[8,112,224]{2,1,0:T(8,128)(2,1)}, bf16[8,112,224]{2,1,0:T(8,128)(2,1)S(1)}, u32[]{:S(2)}, u32[]{:S(2)}) collective-permute-start(bf16[8,112,224]{2,1,0:T(8,128)(2,1)} %get-tuple-element.7), channel_id=1, source_target_pairs={{0,16},{16,32},{32,48},{48,0},{1,17},{17,33},{33,49},{49,1},{2,18}... | collective-permute-start | bytes 1204232 | tf_op jit(solution)/shard_map/ppermute | solution.py:200
  158.6 4.3 %collective-permute-start.2 = (bf16[8,112,224]{2,1,0:T(8,128)(2,1)}, bf16[8,112,224]{2,1,0:T(8,128)(2,1)S(1)}, u32[]{:S(2)}, u32[]{:S(2)}) collective-permute-start(bf16[8,112,224]{2,1,0:T(8,128)(2,1)} %get-tuple-element.8), channel_id=1, source_target_pairs={{0,32},{16,48},{32,0},{48,16},{1,33},{17,49},{33,1},{49,17},{2,34}... | collective-permute-start | bytes 1204232 | tf_op jit(solution)/shard_map/ppermute | solution.py:200
  163.0 3.1 %collective-permute-start.3 = (bf16[8,112,224]{2,1,0:T(8,128)(2,1)}, bf16[8,112,224]{2,1,0:T(8,128)(2,1)S(1)}, u32[]{:S(2)}, u32[]{:S(2)}) collective-permute-start(bf16[8,112,224]{2,1,0:T(8,128)(2,1)} %get-tuple-element.9), channel_id=1, source_target_pairs={{0,48},{16,0},{32,16},{48,32},{1,49},{17,1},{33,17},{49,33},{2,50}... | collective-permute-start | bytes 1204232 | tf_op jit(solution)/shard_map/ppermute | solution.py:200
  166.1 0.0 copy-done.8
  166.1 5.3 %collective-permute-done.1.refs_1_ = bf16[8,112,224]{2,1,0:T(8,128)(2,1)S(1)} collective-permute-done((bf16[8,112,224]{2,1,0:T(8,128)(2,1)}, bf16[8,112,224]{2,1,0:T(8,128)(2,1)S(1)}, u32[]{:S(2)}, u32[]{:S(2)}) %collective-permute-start.1) | collective-permute-done | bytes 401440 | tf_op jit(solution)/shard_map/ppermute | solution.py:200
  171.4 10.1 %collective-permute-done.2.refs_2_ = bf16[8,112,224]{2,1,0:T(8,128)(2,1)S(1)} collective-permute-done((bf16[8,112,224]{2,1,0:T(8,128)(2,1)}, bf16[8,112,224]{2,1,0:T(8,128)(2,1)S(1)}, u32[]{:S(2)}, u32[]{:S(2)}) %collective-permute-start.2) | collective-permute-done | bytes 401440 | tf_op jit(solution)/shard_map/ppermute | solution.py:200
  181.6 1.9 collective-permute-done.3.refs_3_
  183.5 0.0 copy-done.5
  183.5 0.0 copy-done.6
  183.5 0.8 copy-done.7
  184.3 2.5 %sum_parts.1 = bf16[8,112,256]{2,1,0:T(8,128)(2,1)} custom-call(bf16[8,112,224]{2,1,0:T(8,128)(2,1)} %get-tuple-element.6.refs_0_, bf16[8,112,224]{2,1,0:T(8,128)(2,1)} %copy-done.5, bf16[8,112,224]{2,1,0:T(8,128)(2,1)} %copy-done.6, bf16[8,112,224]{2,1,0:T(8,128)(2,1)} %copy-done.7), custom_call_target="tpu_custom_call" | custom-call | tf_op jit(solution)/shard_map/sum_parts/pallas_call | solution.py:165
  186.8 0.0 all-to-all-done.4
  186.8 3.5 %all-to-all-start.5 = ((bf16[8,112,256]{2,1,0:T(8,128)(2,1)}), bf16[8,112,256]{2,1,0:T(8,128)(2,1)S(1)}, u32[]{:S(2)}, u32[]{:S(2)}) async-start(bf16[8,112,256]{2,1,0:T(8,128)(2,1)} %sum_parts.1), calls=%async_computation.5 | async-start | bytes 917504 | tf_op jit(solution)/shard_map/all_to_all | solution.py:202
  190.3 0.1 convert_bitcast_fusion
  190.4 0.6 copy.17
  191.0 0.6 reshape.37
  191.6 1.1 broadcast_divide_fusion
  192.7 12.8 %all-to-all-done.5 = bf16[8,112,256]{2,1,0:T(8,128)(2,1)S(1)} async-done(((bf16[8,112,256]{2,1,0:T(8,128)(2,1)}), bf16[8,112,256]{2,1,0:T(8,128)(2,1)S(1)}, u32[]{:S(2)}, u32[]{:S(2)}) %all-to-all-start.5) | async-done | bytes 458784 | tf_op jit(solution)/shard_map/all_to_all | solution.py:202
  205.5 0.1 slice_convert_fusion
  205.6 0.7 fusion.4
  (5 shorter events, 0.0 us)
Async XLA Ops:
  7.2 10.0 %copy-start = (bf16[1024,512]{1,0:T(8,128)(2,1)S(1)}, bf16[1024,512]{1,0:T(8,128)(2,1)}, u32[]{:S(2)}) copy-start(bf16[1024,512]{1,0:T(8,128)(2,1)} %param.8) | copy-start | bytes 3145732
  7.2 10.0 %copy-start.3 = (bf16[1024,224]{0,1:T(8,128)(2,1)S(1)}, bf16[1024,224]{0,1:T(8,128)(2,1)}, u32[]{:S(2)}) copy-start(bf16[1024,224]{0,1:T(8,128)(2,1)} %param.6) | copy-start | bytes 1376260
  7.2 61.5 %all-gather.3.cloned.1.call-start = ((), (), s32[]{:S(2)}) async-start(), calls=%async_computation.6 | async-start | bytes 4128768 | tf_op jit(solution)/shard_map/all_gather | solution.py:180
  9.6 20.8 %all-to-all-start = ((bf16[8,112,256]{2,1,0:T(8,128)(2,1)}), bf16[8,112,256]{2,1,0:T(8,128)(2,1)S(1)}, u32[]{:S(2)}, u32[]{:S(2)}) async-start(bf16[8,112,256]{2,1,0:T(8,128)(2,1)} %broadcast_in_dim.8), calls=%async_computation | async-start | bytes 917504 | tf_op jit(solution)/shard_map/all_to_all | solution.py:75
  30.3 41.1 %all-to-all-start.2 = ((f32[32,16,224]{2,1,0:T(8,128)}), f32[32,16,224]{2,1,0:T(8,128)S(1)}, u32[]{:S(2)}, u32[]{:S(2)}) async-start(f32[32,16,224]{2,1,0:T(8,128)} %bitcast.4), calls=%async_computation.2 | async-start | bytes 1048576 | tf_op jit(solution)/shard_map/all_to_all | solution.py:184
  68.7 62.5 %collective-permute-start = (bf16[1792,1024]{1,0:T(8,128)(2,1)}, bf16[1792,1024]{1,0:T(8,128)(2,1)}, u32[]{:S(2)}, u32[]{:S(2)}) collective-permute-start(bf16[1792,1024]{1,0:T(8,128)(2,1)} %all-gather.3.cloned.1.call-done.mine_ref), channel_id=1, source_target_pairs={{0,1},{1,0},{2,3},{3,2},{4,5},{5,4},{6,7},{7,6},{8,9},{9,8},{10,11... | collective-permute-start | bytes 11010056 | tf_op jit(solution)/shard_map/ppermute | solution.py:181
  72.9 27.3 %all-to-all-start.1 = ((bf16[4,896,256]{2,1,0:T(8,128)(2,1)}), bf16[4,896,256]{2,1,0:T(8,128)(2,1)S(1)}, u32[]{:S(2)}, u32[]{:S(2)}) async-start(bf16[4,896,256]{2,1,0:T(8,128)(2,1)} %broadcast_in_dim.10), calls=%async_computation.1 | async-start | bytes 3670016 | tf_op jit(solution)/shard_map/all_to_all | solution.py:75
  100.2 1.3 copy-start.2
  101.5 11.1 %copy-start.1 = (f32[512,512]{1,0:T(8,128)S(1)}, f32[512,512]{1,0:T(8,128)}, u32[]{:S(2)}) copy-start(f32[512,512]{1,0:T(8,128)} %factor_ref.1) | copy-start | bytes 3145732
  104.8 23.0 %all-to-all-start.3 = ((f32[32,16,224]{2,1,0:T(8,128)}), f32[32,16,224]{2,1,0:T(8,128)}, u32[]{:S(2)}, u32[]{:S(2)}) async-start(f32[32,16,224]{2,1,0:T(8,128)} %broadcast_in_dim.11), calls=%async_computation.3 | async-start | bytes 1048576 | tf_op jit(solution)/shard_map/all_to_all | solution.py:75
  138.4 9.7 %copy-start.4 = (bf16[1024,224]{0,1:T(8,128)(2,1)S(1)}, bf16[1024,224]{0,1:T(8,128)(2,1)}, u32[]{:S(2)}) copy-start(bf16[1024,224]{0,1:T(8,128)(2,1)} %param.7) | copy-start | bytes 1376260
  140.7 46.1 %all-to-all-start.4 = ((bf16[16,64,224]{2,1,0:T(8,128)(2,1)}), bf16[16,64,224]{2,1,0:T(8,128)(2,1)S(1)}, u32[]{:S(2)}, u32[]{:S(2)}) async-start(bf16[16,64,224]{2,1,0:T(8,128)(2,1)} %bitcast.9), calls=%async_computation.4 | async-start | bytes 1048576 | tf_op jit(solution)/shard_map/all_to_all | solution.py:208
  149.1 16.9 %copy-start.8 = (s32[64]{0:T(128)S(1)}, s32[64]{0:T(128)}, u32[]{:S(2)}) copy-start(s32[64]{0:T(128)} %param.11) | copy-start | bytes 772
  156.1 15.3 %collective-permute-start.1 = (bf16[8,112,224]{2,1,0:T(8,128)(2,1)}, bf16[8,112,224]{2,1,0:T(8,128)(2,1)S(1)}, u32[]{:S(2)}, u32[]{:S(2)}) collective-permute-start(bf16[8,112,224]{2,1,0:T(8,128)(2,1)} %get-tuple-element.7), channel_id=1, source_target_pairs={{0,16},{16,32},{32,48},{48,0},{1,17},{17,33},{33,49},{49,1},{2,18}... | collective-permute-start | bytes 1204232 | tf_op jit(solution)/shard_map/ppermute | solution.py:200
  158.6 22.9 %collective-permute-start.2 = (bf16[8,112,224]{2,1,0:T(8,128)(2,1)}, bf16[8,112,224]{2,1,0:T(8,128)(2,1)S(1)}, u32[]{:S(2)}, u32[]{:S(2)}) collective-permute-start(bf16[8,112,224]{2,1,0:T(8,128)(2,1)} %get-tuple-element.8), channel_id=1, source_target_pairs={{0,32},{16,48},{32,0},{48,16},{1,33},{17,49},{33,1},{49,17},{2,34}... | collective-permute-start | bytes 1204232 | tf_op jit(solution)/shard_map/ppermute | solution.py:200
  163.0 20.5 %collective-permute-start.3 = (bf16[8,112,224]{2,1,0:T(8,128)(2,1)}, bf16[8,112,224]{2,1,0:T(8,128)(2,1)S(1)}, u32[]{:S(2)}, u32[]{:S(2)}) collective-permute-start(bf16[8,112,224]{2,1,0:T(8,128)(2,1)} %get-tuple-element.9), channel_id=1, source_target_pairs={{0,48},{16,0},{32,16},{48,32},{1,49},{17,1},{33,17},{49,33},{2,50}... | collective-permute-start | bytes 1204232 | tf_op jit(solution)/shard_map/ppermute | solution.py:200
  171.4 12.1 %copy-start.5 = (bf16[8,112,224]{2,1,0:T(8,128)(2,1)}, bf16[8,112,224]{2,1,0:T(8,128)(2,1)S(1)}, u32[]{:S(2)}) copy-start(bf16[8,112,224]{2,1,0:T(8,128)(2,1)S(1)} %collective-permute-done.1.refs_1_) | copy-start | bytes 1204228
  181.6 1.9 copy-start.6
  183.5 0.8 copy-start.7
  186.8 18.7 %all-to-all-start.5 = ((bf16[8,112,256]{2,1,0:T(8,128)(2,1)}), bf16[8,112,256]{2,1,0:T(8,128)(2,1)S(1)}, u32[]{:S(2)}, u32[]{:S(2)}) async-start(bf16[8,112,256]{2,1,0:T(8,128)(2,1)} %sum_parts.1), calls=%async_computation.5 | async-start | bytes 917504 | tf_op jit(solution)/shard_map/all_to_all | solution.py:202
Sparse Core Ops, SparseCore 0:
  10.1 58.5 all-gather.2

commit v7 on v6

--- a/solution.py
+++ b/solution.py
@@ -149,22 +149,31 @@
     )(place, mine, theirs, weight)
 
 
-def sum_kernel(*refs):
-    *parts, out_ref = refs
-    width = parts[0].shape[2]
-    for i in range(out_ref.shape[0]):
-        total = parts[0][i].astype(F32)
+def sum_kernel(place_ref, *refs):
+    count = refs[0].shape[0]
+    parts, outs = refs[:-count], refs[-count:]
+    for d, out_ref in enumerate(outs):
+        at = (place_ref[2] + d) % count
+        total = parts[0][at].astype(F32)
         for part in parts[1:]:
-            total = total + part[i].astype(F32)
-        out_ref[i, :, :width] = total.astype(BF16)
-        out_ref[i, :, width:] = jnp.zeros((out_ref.shape[1], out_ref.shape[2] - width), BF16)
-
-
-def sum_parts(parts):
+            total = total + part[at].astype(F32)
+        out_ref[...] = total.astype(BF16)
+
+
+def sum_parts(place, parts):
     count, rows, width = parts[0].shape
-    return pl.pallas_call(
-        sum_kernel, out_shape=jax.ShapeDtypeStruct((count, rows, lanes(width)), BF16), name="sum_parts"
-    )(*parts)
+    whole = pl.BlockSpec(parts[0].shape, lambda i, p: (0, 0, 0))
+    return pl.pallas_call(
+        sum_kernel,
+        out_shape=[jax.ShapeDtypeStruct((rows, width), BF16)] * count,
+        grid_spec=pltpu.PrefetchScalarGridSpec(
+            num_scalar_prefetch=1,
+            grid=(1,),
+            in_specs=[whole] * len(parts),
+            out_specs=[pl.BlockSpec((rows, width), lambda i, p: (0, 0))] * count,
+        ),
+        name="sum_parts",
+    )(place, *parts)
 
 
 def shards(grad_out, residual, confounders, gram_factor, proj_weight, doc_lengths):
@@ -195,13 +204,15 @@
     inverse = gram_inverse(gram_factor)
     coef_b = dot_hi(inverse, moments).astype(BF16)
 
-    place = jnp.stack([core, lax.axis_index("x")]).astype(jnp.int32)
+    place = jnp.stack([core, lax.axis_index("x"), lax.axis_index("y")]).astype(jnp.int32)
     parts = partial_weight_grads(place, mine, theirs, residual, nx, own_rows)
     moved = [lax.ppermute(parts[d], "x", [(i, (i + d) % nx) for i in range(nx)]) for d in range(1, nx)]
-    total = sum_parts([parts[0], *moved])
-    total = lax.all_to_all(total, "y", split_axis=0, concat_axis=0, tiled=True)
-    total = total[:, :, :width].astype(F32)
-    weight_grad = sum((total[i] for i in range(1, ny)), total[0]) * norm_scale
+    parts = sum_parts(place, [parts[0], *moved])
+    total = parts[0].astype(F32)
+    for d in range(1, ny):
+        moved = lax.ppermute(parts[d], "y", [(i, (i + d) % ny) for i in range(ny)])
+        total = total + moved.astype(F32)
+    weight_grad = total * norm_scale
 
     dense = dense_grad(place, mine, theirs, weight, width, own_rows)
     pooled = dense.T - jnp.dot(confounders, coef_b, preferred_element_type=F32)

time: 216 us -> 230 us (1.065)
  starting transfers between devices: 50.7 us -> 72.8 us
  waiting for transfers between devices: 86.1 us -> 75.4 us
    ppermute x0 -> x7, starting transfers between devices: none -> 25.4 us  [shards(): moved = lax.ppermute(parts[d], 'y', [(i, (i + d) % ny) for i in range(ny)])]
    all_to_all x1 -> x0, waiting for transfers between devices: 12.8 us -> none  [shards(): total = lax.all_to_all(total, 'y', split_axis=0, concat_axis=0, tiled=True)]
    all_to_all x1 -> x0, starting transfers between devices: 3.47 us -> none  [shards(): total = lax.all_to_all(total, 'y', split_axis=0, concat_axis=0, tiled=True)]
  transfers between devices with their start and end apart: 11 -> 17, of which waited for: 8 -> 8; matrix products, arithmetic and copies ran while one was open for 7% -> 7% of each run, Pallas kernels for 8% -> 8%
where the time goes in v7:
time: 230 us; the launch traced here: 226 us
  waiting for transfers between devices  75.4 us (33%)
  starting transfers between devices  72.8 us (32%)
  Pallas kernels  25.4 us (11%)
  blocking collectives  16.2 us (7%)
  between operations  14.3 us (6%)
  local copies, waits for them, and re-layouts  9.86 us (4%)
  matrix products  7.05 us (3%)
  other arithmetic  4.71 us (2%)
    all_gather x1, waiting for transfers between devices, shards(): mine = lax.all_gather(grad_out.T, 'z', axis=0, tiled=True)  30.6 us
    ppermute x7, starting transfers between devices, shards(): moved = lax.ppermute(parts[d], 'y', [(i, (i + d) % ny) for i in range(ny)])  25.4 us
    all_to_all x3, waiting for transfers between devices, spread(): return lax.all_to_all(copies, axes, split_axis=0, concat_axis=0, tiled=True)  24.6 us
    all_to_all x3, starting transfers between devices, spread(): return lax.all_to_all(copies, axes, split_axis=0, concat_axis=0, tiled=True)  19.4 us
    ppermute x3, waiting for transfers between devices, shards(): lax.ppermute(parts[d], 'x', [(i, (i + d) % nx) for i in range(nx)])  17.5 us
    all_gather x1, blocking collectives, shards(): cross = lax.all_gather(cross, COL, axis=0, tiled=False)  16.2 us
    ppermute x3, starting transfers between devices, shards(): lax.ppermute(parts[d], 'x', [(i, (i + d) % nx) for i in range(nx)])  10 us
    pallas_call x1, Pallas kernels, gram_inverse(): pl.pallas_call(gram_inverse_kernel, out_shape=jax.ShapeDtypeStruct(factor...  8.3 us
  transfers between devices with their start and end apart: 17, of which 8 were waited for; matrix products, arithmetic and copies ran while one was open for 7% of the time, Pallas kernels for 8%

profile of v7, /device:TPU:1, one launch (start us, length us, event | category | flops | bytes accessed | tf_op | source)
XLA Modules:
  0.0 225.7 jit_solution(4660660034073483295)
XLA Ops:
  7.2 0.0 copy-start
  7.2 0.0 all-gather.3.cloned.1.call-start
  7.2 0.7 all-gather.3.cloned.1.call-update
  7.9 0.8 pad.4
  8.8 0.8 broadcast_in_dim.8
  9.6 7.6 %all-to-all-start = ((bf16[8,112,256]{2,1,0:T(8,128)(2,1)}), bf16[8,112,256]{2,1,0:T(8,128)(2,1)S(1)}, u32[]{:S(2)}, u32[]{:S(2)}) async-start(bf16[8,112,256]{2,1,0:T(8,128)(2,1)} %broadcast_in_dim.8), calls=%async_computation | async-start | bytes 917504 | tf_op jit(solution)/shard_map/all_to_all | solution.py:75
  17.2 1.3 fusion.3
  18.5 11.8 %all-to-all-done = bf16[8,112,256]{2,1,0:T(8,128)(2,1)S(1)} async-done(((bf16[8,112,256]{2,1,0:T(8,128)(2,1)}), bf16[8,112,256]{2,1,0:T(8,128)(2,1)S(1)}, u32[]{:S(2)}, u32[]{:S(2)}) %all-to-all-start) | async-done | bytes 458784 | tf_op jit(solution)/shard_map/all_to_all | solution.py:75
  30.3 7.8 %all-to-all-start.2 = ((f32[32,16,224]{2,1,0:T(8,128)}), f32[32,16,224]{2,1,0:T(8,128)S(1)}, u32[]{:S(2)}, u32[]{:S(2)}) async-start(f32[32,16,224]{2,1,0:T(8,128)} %bitcast.5), calls=%async_computation.2 | async-start | bytes 1048576 | tf_op jit(solution)/shard_map/all_to_all | solution.py:193
  38.1 30.6 %all-gather.3.cloned.1.call-done.mine_ref = bf16[1792,1024]{1,0:T(8,128)(2,1)} async-done(((bf16[224,1024]{1,0:T(8,128)(2,1)}), bf16[1792,1024]{1,0:T(8,128)(2,1)}) %all-gather.3.cloned.1.call-update) | async-done | bytes 3670032 | tf_op jit(solution)/shard_map/all_gather | solution.py:189
  68.7 2.7 %collective-permute-start = (bf16[1792,1024]{1,0:T(8,128)(2,1)}, bf16[1792,1024]{1,0:T(8,128)(2,1)}, u32[]{:S(2)}, u32[]{:S(2)}) collective-permute-start(bf16[1792,1024]{1,0:T(8,128)(2,1)} %all-gather.3.cloned.1.call-done.mine_ref), channel_id=1, source_target_pairs={{0,1},{1,0},{2,3},{3,2},{4,5},{5,4},{6,7},{7,6},{8,9},{9,8},{10,11... | collective-permute-start | bytes 11010056 | tf_op jit(solution)/shard_map/ppermute | solution.py:190
  71.4 0.0 all-to-all-done.2
  71.4 1.4 broadcast_in_dim.10
  72.9 4.0 %all-to-all-start.1 = ((bf16[4,896,256]{2,1,0:T(8,128)(2,1)}), bf16[4,896,256]{2,1,0:T(8,128)(2,1)S(1)}, u32[]{:S(2)}, u32[]{:S(2)}) async-start(bf16[4,896,256]{2,1,0:T(8,128)(2,1)} %broadcast_in_dim.10), calls=%async_computation.1 | async-start | bytes 3670016 | tf_op jit(solution)/shard_map/all_to_all | solution.py:75
  76.8 0.1 reduce_sum.9
  76.9 16.2 %all-gather = f32[256,224]{1,0:T(8,128)S(1)} all-gather(f32[16,224]{1,0:T(8,128)S(1)} %reduce_sum.9), channel_id=2, replica_groups=mesh['y'=8,'x'=4,'z'=8,'c'=2] {'z','c'}, dimensions={0}, use_global_device_ids=true | all-gather | bytes 243712 | tf_op jit(solution)/shard_map/all_gather | solution.py:195
  93.1 0.2 reshape.29
  93.3 0.2 copy.15
  93.5 0.2 reshape.30
  93.7 6.5 %all-to-all-done.1.weight_ref = bf16[4,896,256]{2,1,0:T(8,128)(2,1)S(1)} async-done(((bf16[4,896,256]{2,1,0:T(8,128)(2,1)}), bf16[4,896,256]{2,1,0:T(8,128)(2,1)S(1)}, u32[]{:S(2)}, u32[]{:S(2)}) %all-to-all-start.1) | async-done | bytes 1835040 | tf_op jit(solution)/shard_map/all_to_all | solution.py:75
  100.2 1.3 copy-done.2
  101.5 2.4 %fusion = f32[16,224]{1,0:T(8,128)S(1)} fusion(f32[16,3584]{1,0:T(8,128)S(1)} %reshape.30, bf16[3584,256]{1,0:T(8,128)(2,1)} %bitcast.23), kind=kOutput, calls=%fused_computation | convolution fusion | flops 154140672 | bytes 2078720 | tf_op jit(solution)/shard_map/dot_general | solution.py:18
  103.9 0.9 broadcast_in_dim.11
  104.8 7.8 %all-to-all-start.3 = ((f32[32,16,224]{2,1,0:T(8,128)}), f32[32,16,224]{2,1,0:T(8,128)}, u32[]{:S(2)}, u32[]{:S(2)}) async-start(f32[32,16,224]{2,1,0:T(8,128)} %broadcast_in_dim.11), calls=%async_computation.3 | async-start | bytes 1048576 | tf_op jit(solution)/shard_map/all_to_all | solution.py:75
  112.6 8.3 %gram_inverse.1 = f32[512,512]{1,0:T(8,128)S(1)} custom-call(f32[512,512]{1,0:T(8,128)S(1)} %copy-done.1), custom_call_target="tpu_custom_call" | custom-call | tf_op jit(solution)/shard_map/gram_inverse/pallas_call | solution.py:61
  120.9 0.6 pad_add_fusion.place_ref
  121.5 6.3 %all-to-all-done.3 = f32[32,16,224]{2,1,0:T(8,128)} async-done(((f32[32,16,224]{2,1,0:T(8,128)}), f32[32,16,224]{2,1,0:T(8,128)}, u32[]{:S(2)}, u32[]{:S(2)}) %all-to-all-start.3) | async-done | bytes 458784 | tf_op jit(solution)/shard_map/all_to_all | solution.py:75
  127.8 2.9 %convolution_convert_fusion = bf16[224,512]{1,0:T(8,128)(2,1)S(1)} fusion(f32[512,224]{1,0:T(8,128)} %bitcast.8, f32[512,512]{1,0:T(8,128)S(1)} %gram_inverse.1), kind=kOutput, calls=%fused_computation.2 | convolution fusion | flops 704757760 | bytes 1736704 | tf_op jit(solution)/shard_map/dot_general | solution.py:18
  130.7 0.5 fusion.4
  131.2 0.0 collective-permute-done.theirs_ref
  131.2 7.2 %dense_grad.1 = f32[224,1024]{1,0:T(8,128)} custom-call(s32[3]{0:T(128)} %pad_add_fusion.place_ref, bf16[1792,1024]{1,0:T(8,128)(2,1)} %all-gather.3.cloned.1.call-done.mine_ref, bf16[1792,1024]{1,0:T(8,128)(2,1)} %collective-permute-done.theirs_ref, bf16[4,896,256]{2,1,0:T(8,128)(2,1)} %copy-done.2), custom_call_target="tpu_custom_call" | custom-call | tf_op jit(solution)/shard_map/dense_grad/pallas_call | solution.py:139
  138.3 1.3 fusion.2
  139.7 1.0 copy.16
  140.7 7.4 %all-to-all-start.4 = ((bf16[16,64,224]{2,1,0:T(8,128)(2,1)}), bf16[16,64,224]{2,1,0:T(8,128)(2,1)S(1)}, u32[]{:S(2)}, u32[]{:S(2)}) async-start(bf16[16,64,224]{2,1,0:T(8,128)(2,1)} %bitcast.10), calls=%async_computation.4 | async-start | bytes 1048576 | tf_op jit(solution)/shard_map/all_to_all | solution.py:219
  148.1 1.0 copy.18.residual_ref
  149.1 6.9 %partial_weight_grads.1 = (bf16[8,112,224]{2,1,0:T(8,128)(2,1)}, bf16[8,112,224]{2,1,0:T(8,128)(2,1)}, bf16[8,112,224]{2,1,0:T(8,128)(2,1)}, bf16[8,112,224]{2,1,0:T(8,128)(2,1)}) custom-call(s32[3]{0:T(128)} %pad_add_fusion.place_ref, bf16[1792,1024]{1,0:T(8,128)(2,1)} %all-gather.3.cloned.1.call-done.mine_ref, ...), custom_call_target="tpu_custom_call" | custom-call | tf_op jit(solution)/shard_map/partial_weight_grads/pallas_call | solution.py:98
  156.0 2.6 %collective-permute-start.1 = (bf16[8,112,224]{2,1,0:T(8,128)(2,1)}, bf16[8,112,224]{2,1,0:T(8,128)(2,1)S(1)}, u32[]{:S(2)}, u32[]{:S(2)}) collective-permute-start(bf16[8,112,224]{2,1,0:T(8,128)(2,1)} %get-tuple-element.15), channel_id=1, source_target_pairs={{0,16},{16,32},{32,48},{48,0},{1,17},{17,33},{33,49},{49,1},{2,18}... | collective-permute-start | bytes 1204232 | tf_op jit(solution)/shard_map/ppermute | solution.py:209
  158.7 4.3 %collective-permute-start.2 = (bf16[8,112,224]{2,1,0:T(8,128)(2,1)}, bf16[8,112,224]{2,1,0:T(8,128)(2,1)S(1)}, u32[]{:S(2)}, u32[]{:S(2)}) collective-permute-start(bf16[8,112,224]{2,1,0:T(8,128)(2,1)} %get-tuple-element.16), channel_id=1, source_target_pairs={{0,32},{16,48},{32,0},{48,16},{1,33},{17,49},{33,1},{49,17},{2,34}... | collective-permute-start | bytes 1204232 | tf_op jit(solution)/shard_map/ppermute | solution.py:209
  163.0 3.1 %collective-permute-start.3 = (bf16[8,112,224]{2,1,0:T(8,128)(2,1)}, bf16[8,112,224]{2,1,0:T(8,128)(2,1)S(1)}, u32[]{:S(2)}, u32[]{:S(2)}) collective-permute-start(bf16[8,112,224]{2,1,0:T(8,128)(2,1)} %get-tuple-element.17), channel_id=1, source_target_pairs={{0,48},{16,0},{32,16},{48,32},{1,49},{17,1},{33,17},{49,33},{2,50}... | collective-permute-start | bytes 1204232 | tf_op jit(solution)/shard_map/ppermute | solution.py:209
  166.1 5.4 %collective-permute-done.1.refs_1_ = bf16[8,112,224]{2,1,0:T(8,128)(2,1)S(1)} collective-permute-done((bf16[8,112,224]{2,1,0:T(8,128)(2,1)}, bf16[8,112,224]{2,1,0:T(8,128)(2,1)S(1)}, u32[]{:S(2)}, u32[]{:S(2)}) %collective-permute-start.1) | collective-permute-done | bytes 401440 | tf_op jit(solution)/shard_map/ppermute | solution.py:209
  171.4 10.1 %collective-permute-done.2.refs_2_ = bf16[8,112,224]{2,1,0:T(8,128)(2,1)S(1)} collective-permute-done((bf16[8,112,224]{2,1,0:T(8,128)(2,1)}, bf16[8,112,224]{2,1,0:T(8,128)(2,1)S(1)}, u32[]{:S(2)}, u32[]{:S(2)}) %collective-permute-start.2) | collective-permute-done | bytes 401440 | tf_op jit(solution)/shard_map/ppermute | solution.py:209
  181.6 1.9 collective-permute-done.3.refs_3_
  183.5 0.8 copy-done.7
  184.3 3.0 %sum_parts.1 = (bf16[112,224]{1,0:T(8,128)(2,1)}, bf16[112,224]{1,0:T(8,128)(2,1)}, bf16[112,224]{1,0:T(8,128)(2,1)}, bf16[112,224]{1,0:T(8,128)(2,1)}, bf16[112...) custom-call(s32[3]{0:T(128)} %pad_add_fusion.place_ref, ...), custom_call_target="tpu_custom_call" | custom-call | tf_op jit(solution)/shard_map/sum_parts/pallas_call | solution.py:166
  187.3 2.2 collective-permute-start.10
  189.6 3.0 %collective-permute-start.4 = (bf16[112,224]{1,0:T(8,128)(2,1)}, bf16[112,224]{1,0:T(8,128)(2,1)S(1)}, u32[]{:S(2)}, u32[]{:S(2)}) collective-permute-start(bf16[112,224]{1,0:T(8,128)(2,1)} %get-tuple-element.19), channel_id=1, source_target_pairs={{0,64},{64,128},{128,192},{192,256},{256,320},{320,384},{384,448},... | collective-permute-start | bytes 150536 | tf_op jit(solution)/shard_map/ppermute | solution.py:213
  192.6 3.4 %collective-permute-start.5 = (bf16[112,224]{1,0:T(8,128)(2,1)}, bf16[112,224]{1,0:T(8,128)(2,1)S(1)}, u32[]{:S(2)}, u32[]{:S(2)}) collective-permute-start(bf16[112,224]{1,0:T(8,128)(2,1)} %get-tuple-element.20), channel_id=1, source_target_pairs={{0,128},{64,192},{128,256},{192,320},{256,384},{320,448},{384,0},{... | collective-permute-start | bytes 150536 | tf_op jit(solution)/shard_map/ppermute | solution.py:213
  196.0 3.3 %collective-permute-start.6 = (bf16[112,224]{1,0:T(8,128)(2,1)}, bf16[112,224]{1,0:T(8,128)(2,1)S(1)}, u32[]{:S(2)}, u32[]{:S(2)}) collective-permute-start(bf16[112,224]{1,0:T(8,128)(2,1)} %get-tuple-element.21), channel_id=1, source_target_pairs={{0,192},{64,256},{128,320},{192,384},{256,448},{320,0},{384,64},{4... | collective-permute-start | bytes 150536 | tf_op jit(solution)/shard_map/ppermute | solution.py:213
  199.3 5.4 %collective-permute-start.7 = (bf16[112,224]{1,0:T(8,128)(2,1)}, bf16[112,224]{1,0:T(8,128)(2,1)S(1)}, u32[]{:S(2)}, u32[]{:S(2)}) collective-permute-start(bf16[112,224]{1,0:T(8,128)(2,1)} %get-tuple-element.22), channel_id=1, source_target_pairs={{0,256},{64,320},{128,384},{192,448},{256,0},{320,64},{384,128},{4... | collective-permute-start | bytes 150536 | tf_op jit(solution)/shard_map/ppermute | solution.py:213
  204.7 0.0 collective-permute-done.10
  204.7 3.4 %collective-permute-start.8 = (bf16[112,224]{1,0:T(8,128)(2,1)}, bf16[112,224]{1,0:T(8,128)(2,1)S(1)}, u32[]{:S(2)}, u32[]{:S(2)}) collective-permute-start(bf16[112,224]{1,0:T(8,128)(2,1)} %get-tuple-element.23), channel_id=1, source_target_pairs={{0,320},{64,384},{128,448},{192,0},{256,64},{320,128},{384,192},{4... | collective-permute-start | bytes 150536 | tf_op jit(solution)/shard_map/ppermute | solution.py:213
  208.1 0.0 collective-permute-done.4
  208.1 4.7 %collective-permute-start.9 = (bf16[112,224]{1,0:T(8,128)(2,1)}, bf16[112,224]{1,0:T(8,128)(2,1)S(1)}, u32[]{:S(2)}, u32[]{:S(2)}) collective-permute-start(bf16[112,224]{1,0:T(8,128)(2,1)} %get-tuple-element.24), channel_id=1, source_target_pairs={{0,384},{64,448},{128,0},{192,64},{256,128},{320,192},{384,256},{4... | collective-permute-start | bytes 150536 | tf_op jit(solution)/shard_map/ppermute | solution.py:213
  212.9 0.0 collective-permute-done.5
  212.9 0.0 collective-permute-done.6
  212.9 0.0 collective-permute-done.7
  212.9 0.0 collective-permute-done.8
  212.9 2.0 collective-permute-done.9
  214.9 1.5 add_multiply_fusion
  216.5 0.0 all-to-all-done.4
  216.5 0.1 convert_bitcast_fusion
  216.6 0.6 copy.17
  217.2 0.6 reshape.33
  217.8 1.1 broadcast_divide_fusion
  (16 shorter events, 0.0 us)
Async XLA Ops:
  7.2 10.0 %copy-start = (bf16[1024,512]{1,0:T(8,128)(2,1)S(1)}, bf16[1024,512]{1,0:T(8,128)(2,1)}, u32[]{:S(2)}) copy-start(bf16[1024,512]{1,0:T(8,128)(2,1)} %param.8) | copy-start | bytes 3145732
  7.2 10.0 %copy-start.3 = (bf16[1024,224]{0,1:T(8,128)(2,1)S(1)}, bf16[1024,224]{0,1:T(8,128)(2,1)}, u32[]{:S(2)}) copy-start(bf16[1024,224]{0,1:T(8,128)(2,1)} %param.6) | copy-start | bytes 1376260
  7.2 61.5 %all-gather.3.cloned.1.call-start = ((), (), s32[]{:S(2)}) async-start(), calls=%async_computation.5 | async-start | bytes 4128768 | tf_op jit(solution)/shard_map/all_gather | solution.py:189
  9.6 20.8 %all-to-all-start = ((bf16[8,112,256]{2,1,0:T(8,128)(2,1)}), bf16[8,112,256]{2,1,0:T(8,128)(2,1)S(1)}, u32[]{:S(2)}, u32[]{:S(2)}) async-start(bf16[8,112,256]{2,1,0:T(8,128)(2,1)} %broadcast_in_dim.8), calls=%async_computation | async-start | bytes 917504 | tf_op jit(solution)/shard_map/all_to_all | solution.py:75
  30.3 41.1 %all-to-all-start.2 = ((f32[32,16,224]{2,1,0:T(8,128)}), f32[32,16,224]{2,1,0:T(8,128)S(1)}, u32[]{:S(2)}, u32[]{:S(2)}) async-start(f32[32,16,224]{2,1,0:T(8,128)} %bitcast.5), calls=%async_computation.2 | async-start | bytes 1048576 | tf_op jit(solution)/shard_map/all_to_all | solution.py:193
  68.7 62.5 %collective-permute-start = (bf16[1792,1024]{1,0:T(8,128)(2,1)}, bf16[1792,1024]{1,0:T(8,128)(2,1)}, u32[]{:S(2)}, u32[]{:S(2)}) collective-permute-start(bf16[1792,1024]{1,0:T(8,128)(2,1)} %all-gather.3.cloned.1.call-done.mine_ref), channel_id=1, source_target_pairs={{0,1},{1,0},{2,3},{3,2},{4,5},{5,4},{6,7},{7,6},{8,9},{9,8},{10,11... | collective-permute-start | bytes 11010056 | tf_op jit(solution)/shard_map/ppermute | solution.py:190
  72.9 27.3 %all-to-all-start.1 = ((bf16[4,896,256]{2,1,0:T(8,128)(2,1)}), bf16[4,896,256]{2,1,0:T(8,128)(2,1)S(1)}, u32[]{:S(2)}, u32[]{:S(2)}) async-start(bf16[4,896,256]{2,1,0:T(8,128)(2,1)} %broadcast_in_dim.10), calls=%async_computation.1 | async-start | bytes 3670016 | tf_op jit(solution)/shard_map/all_to_all | solution.py:75
  100.2 1.3 copy-start.2
  101.5 11.1 %copy-start.1 = (f32[512,512]{1,0:T(8,128)S(1)}, f32[512,512]{1,0:T(8,128)}, u32[]{:S(2)}) copy-start(f32[512,512]{1,0:T(8,128)} %factor_ref.1) | copy-start | bytes 3145732
  104.8 23.0 %all-to-all-start.3 = ((f32[32,16,224]{2,1,0:T(8,128)}), f32[32,16,224]{2,1,0:T(8,128)}, u32[]{:S(2)}, u32[]{:S(2)}) async-start(f32[32,16,224]{2,1,0:T(8,128)} %broadcast_in_dim.11), calls=%async_computation.3 | async-start | bytes 1048576 | tf_op jit(solution)/shard_map/all_to_all | solution.py:75
  138.3 9.8 %copy-start.4 = (bf16[1024,224]{0,1:T(8,128)(2,1)S(1)}, bf16[1024,224]{0,1:T(8,128)(2,1)}, u32[]{:S(2)}) copy-start(bf16[1024,224]{0,1:T(8,128)(2,1)} %param.7) | copy-start | bytes 1376260
  140.7 75.8 %all-to-all-start.4 = ((bf16[16,64,224]{2,1,0:T(8,128)(2,1)}), bf16[16,64,224]{2,1,0:T(8,128)(2,1)S(1)}, u32[]{:S(2)}, u32[]{:S(2)}) async-start(bf16[16,64,224]{2,1,0:T(8,128)(2,1)} %bitcast.10), calls=%async_computation.4 | async-start | bytes 1048576 | tf_op jit(solution)/shard_map/all_to_all | solution.py:219
  156.0 56.8 %copy-start.8 = (s32[64]{0:T(128)S(1)}, s32[64]{0:T(128)}, u32[]{:S(2)}) copy-start(s32[64]{0:T(128)} %param.11) | copy-start | bytes 772
  156.0 15.4 %collective-permute-start.1 = (bf16[8,112,224]{2,1,0:T(8,128)(2,1)}, bf16[8,112,224]{2,1,0:T(8,128)(2,1)S(1)}, u32[]{:S(2)}, u32[]{:S(2)}) collective-permute-start(bf16[8,112,224]{2,1,0:T(8,128)(2,1)} %get-tuple-element.15), channel_id=1, source_target_pairs={{0,16},{16,32},{32,48},{48,0},{1,17},{17,33},{33,49},{49,1},{2,18}... | collective-permute-start | bytes 1204232 | tf_op jit(solution)/shard_map/ppermute | solution.py:209
  158.7 22.9 %collective-permute-start.2 = (bf16[8,112,224]{2,1,0:T(8,128)(2,1)}, bf16[8,112,224]{2,1,0:T(8,128)(2,1)S(1)}, u32[]{:S(2)}, u32[]{:S(2)}) collective-permute-start(bf16[8,112,224]{2,1,0:T(8,128)(2,1)} %get-tuple-element.16), channel_id=1, source_target_pairs={{0,32},{16,48},{32,0},{48,16},{1,33},{17,49},{33,1},{49,17},{2,34}... | collective-permute-start | bytes 1204232 | tf_op jit(solution)/shard_map/ppermute | solution.py:209
  163.0 20.6 %collective-permute-start.3 = (bf16[8,112,224]{2,1,0:T(8,128)(2,1)}, bf16[8,112,224]{2,1,0:T(8,128)(2,1)S(1)}, u32[]{:S(2)}, u32[]{:S(2)}) collective-permute-start(bf16[8,112,224]{2,1,0:T(8,128)(2,1)} %get-tuple-element.17), channel_id=1, source_target_pairs={{0,48},{16,0},{32,16},{48,32},{1,49},{17,1},{33,17},{49,33},{2,50}... | collective-permute-start | bytes 1204232 | tf_op jit(solution)/shard_map/ppermute | solution.py:209
  171.4 12.1 %copy-start.5 = (bf16[8,112,224]{2,1,0:T(8,128)(2,1)}, bf16[8,112,224]{2,1,0:T(8,128)(2,1)S(1)}, u32[]{:S(2)}) copy-start(bf16[8,112,224]{2,1,0:T(8,128)(2,1)S(1)} %collective-permute-done.1.refs_1_) | copy-start | bytes 1204228
  181.6 1.9 copy-start.6
  183.5 0.8 copy-start.7
  187.3 17.4 %collective-permute-start.10 = (bf16[112,224]{1,0:T(8,128)(2,1)}, bf16[112,224]{1,0:T(8,128)(2,1)S(1)}, u32[]{:S(2)}, u32[]{:S(2)}) collective-permute-start(bf16[112,224]{1,0:T(8,128)(2,1)} %get-tuple-element.25), channel_id=1, source_target_pairs={{0,448},{64,0},{128,64},{192,128},{256,192},{320,256},{384,320},{4... | collective-permute-start | bytes 150536 | tf_op jit(solution)/shard_map/ppermute | solution.py:213
  189.6 18.6 %collective-permute-start.4 = (bf16[112,224]{1,0:T(8,128)(2,1)}, bf16[112,224]{1,0:T(8,128)(2,1)S(1)}, u32[]{:S(2)}, u32[]{:S(2)}) collective-permute-start(bf16[112,224]{1,0:T(8,128)(2,1)} %get-tuple-element.19), channel_id=1, source_target_pairs={{0,64},{64,128},{128,192},{192,256},{256,320},{320,384},{384,448},... | collective-permute-start | bytes 150536 | tf_op jit(solution)/shard_map/ppermute | solution.py:213
  192.6 20.3 %collective-permute-start.5 = (bf16[112,224]{1,0:T(8,128)(2,1)}, bf16[112,224]{1,0:T(8,128)(2,1)S(1)}, u32[]{:S(2)}, u32[]{:S(2)}) collective-permute-start(bf16[112,224]{1,0:T(8,128)(2,1)} %get-tuple-element.20), channel_id=1, source_target_pairs={{0,128},{64,192},{128,256},{192,320},{256,384},{320,448},{384,0},{... | collective-permute-start | bytes 150536 | tf_op jit(solution)/shard_map/ppermute | solution.py:213
  196.0 16.9 %collective-permute-start.6 = (bf16[112,224]{1,0:T(8,128)(2,1)}, bf16[112,224]{1,0:T(8,128)(2,1)S(1)}, u32[]{:S(2)}, u32[]{:S(2)}) collective-permute-start(bf16[112,224]{1,0:T(8,128)(2,1)} %get-tuple-element.21), channel_id=1, source_target_pairs={{0,192},{64,256},{128,320},{192,384},{256,448},{320,0},{384,64},{4... | collective-permute-start | bytes 150536 | tf_op jit(solution)/shard_map/ppermute | solution.py:213
  199.3 13.6 %collective-permute-start.7 = (bf16[112,224]{1,0:T(8,128)(2,1)}, bf16[112,224]{1,0:T(8,128)(2,1)S(1)}, u32[]{:S(2)}, u32[]{:S(2)}) collective-permute-start(bf16[112,224]{1,0:T(8,128)(2,1)} %get-tuple-element.22), channel_id=1, source_target_pairs={{0,256},{64,320},{128,384},{192,448},{256,0},{320,64},{384,128},{4... | collective-permute-start | bytes 150536 | tf_op jit(solution)/shard_map/ppermute | solution.py:213
  204.7 8.2 %collective-permute-start.8 = (bf16[112,224]{1,0:T(8,128)(2,1)}, bf16[112,224]{1,0:T(8,128)(2,1)S(1)}, u32[]{:S(2)}, u32[]{:S(2)}) collective-permute-start(bf16[112,224]{1,0:T(8,128)(2,1)} %get-tuple-element.23), channel_id=1, source_target_pairs={{0,320},{64,384},{128,448},{192,0},{256,64},{320,128},{384,192},{4... | collective-permute-start | bytes 150536 | tf_op jit(solution)/shard_map/ppermute | solution.py:213
  208.1 6.8 %collective-permute-start.9 = (bf16[112,224]{1,0:T(8,128)(2,1)}, bf16[112,224]{1,0:T(8,128)(2,1)S(1)}, u32[]{:S(2)}, u32[]{:S(2)}) collective-permute-start(bf16[112,224]{1,0:T(8,128)(2,1)} %get-tuple-element.24), channel_id=1, source_target_pairs={{0,384},{64,448},{128,0},{192,64},{256,128},{320,192},{384,256},{4... | collective-permute-start | bytes 150536 | tf_op jit(solution)/shard_map/ppermute | solution.py:213
Sparse Core Ops, SparseCore 0:
  10.1 58.5 all-gather.2

commit v8 on v7

--- a/solution.py
+++ b/solution.py
@@ -150,30 +150,48 @@
 
 
 def sum_kernel(place_ref, *refs):
-    count = refs[0].shape[0]
-    parts, outs = refs[:-count], refs[-count:]
-    for d, out_ref in enumerate(outs):
-        at = (place_ref[2] + d) % count
-        total = parts[0][at].astype(F32)
-        for part in parts[1:]:
-            total = total + part[at].astype(F32)
-        out_ref[...] = total.astype(BF16)
+    *parts, keep_ref, send_ref = refs
+    count, chip = parts[0].shape[0], place_ref[2]
+    partner = chip + 1 - 2 * (chip % 2)
+    for start, out_ref in ((chip, keep_ref), (partner, send_ref)):
+        for e in range(out_ref.shape[0]):
+            at = (start + 2 * e) % count
+            total = parts[0][at].astype(F32)
+            for part in parts[1:]:
+                total = total + part[at].astype(F32)
+            out_ref[e] = total
 
 
 def sum_parts(place, parts):
     count, rows, width = parts[0].shape
-    whole = pl.BlockSpec(parts[0].shape, lambda i, p: (0, 0, 0))
+    shape = (count // 2, rows, width)
     return pl.pallas_call(
         sum_kernel,
-        out_shape=[jax.ShapeDtypeStruct((rows, width), BF16)] * count,
+        out_shape=[jax.ShapeDtypeStruct(shape, F32)] * 2,
         grid_spec=pltpu.PrefetchScalarGridSpec(
             num_scalar_prefetch=1,
             grid=(1,),
-            in_specs=[whole] * len(parts),
-            out_specs=[pl.BlockSpec((rows, width), lambda i, p: (0, 0))] * count,
+            in_specs=[pl.BlockSpec(parts[0].shape, lambda i, p: (0, 0, 0))] * len(parts),
+            out_specs=[pl.BlockSpec(shape, lambda i, p: (0, 0, 0))] * 2,
         ),
         name="sum_parts",
     )(place, *parts)
+
+
+def pair_kernel(keep_ref, moved_ref, own_ref, *out_refs):
+    own_ref[...] = keep_ref[0] + moved_ref[0]
+    for e, out_ref in enumerate(out_refs, 1):
+        out_ref[...] = (keep_ref[e] + moved_ref[e]).astype(BF16)
+
+
+def sum_pair(keep, moved):
+    count, rows, width = keep.shape
+    return pl.pallas_call(
+        pair_kernel,
+        out_shape=[jax.ShapeDtypeStruct((rows, width), F32)]
+        + [jax.ShapeDtypeStruct((rows, width), BF16)] * (count - 1),
+        name="sum_pair",
+    )(keep, moved)
 
 
 def shards(grad_out, residual, confounders, gram_factor, proj_weight, doc_lengths):
@@ -207,10 +225,11 @@
     place = jnp.stack([core, lax.axis_index("x"), lax.axis_index("y")]).astype(jnp.int32)
     parts = partial_weight_grads(place, mine, theirs, residual, nx, own_rows)
     moved = [lax.ppermute(parts[d], "x", [(i, (i + d) % nx) for i in range(nx)]) for d in range(1, nx)]
-    parts = sum_parts(place, [parts[0], *moved])
-    total = parts[0].astype(F32)
-    for d in range(1, ny):
-        moved = lax.ppermute(parts[d], "y", [(i, (i + d) % ny) for i in range(ny)])
+    keep, send = sum_parts(place, [parts[0], *moved])
+    moved = lax.ppermute(send, "y", [(i, i ^ 1) for i in range(ny)])
+    total, *parts = sum_pair(keep, moved)
+    for e, part in enumerate(parts, 1):
+        moved = lax.ppermute(part, "y", [(i, (i + 2 * e) % ny) for i in range(ny)])
         total = total + moved.astype(F32)
     weight_grad = total * norm_scale
 

time: 230 us -> 215 us (0.935); the launches traced: 226 us -> 214 us
  starting transfers between devices: 72.8 us -> 59.7 us
    ppermute x3, waiting for transfers between devices: 17.5 us -> 0.01 us  [shards(): lax.ppermute(parts[d], 'x', [(i, (i + d) % nx) for i in range(nx)])]
    ppermute x7 -> x4, waiting for transfers between devices: 2.05 us -> 18.7 us  [the longest x1 11.9 us: shards(): moved = lax.ppermute(send, 'y', [(i, i ^ 1) for i in range(ny)])]
    ppermute x7 -> x4, starting transfers between devices: 25.4 us -> 11.5 us  [the longest x3 9.3 us: shards(): moved = lax.ppermute(part, 'y', [(i, (i + 2 * e) % ny) for i in range(ny)])]
    pallas_call x1 -> x2, Pallas kernels: 3.01 us -> 5.03 us  [the longest x1 3.17 us: sum_parts(): pl.pallas_call(sum_kernel, out_shape=[jax.ShapeDtypeStruct(shape, F32)] *...]
  transfers between devices with their start and end apart: 17 -> 14, of which waited for: 8 -> 7; matrix products, arithmetic and copies ran while one was open for 7% -> 8% of each run, Pallas kernels for 8% -> 10%
where the time goes in v8:
time: 215 us; the launch traced here: 214 us
  waiting for transfers between devices  73.6 us (34%)
  starting transfers between devices  59.7 us (28%)
  Pallas kernels  27.4 us (13%)
  blocking collectives  16.2 us (8%)
  between operations  14.3 us (7%)
  local copies, waits for them, and re-layouts  10.8 us (5%)
  matrix products  7.07 us (3%)
  other arithmetic  4.74 us (2%)
    all_gather x1, waiting for transfers between devices, shards(): mine = lax.all_gather(grad_out.T, 'z', axis=0, tiled=True)  30.6 us
    all_to_all x3, waiting for transfers between devices, spread(): return lax.all_to_all(copies, axes, split_axis=0, concat_axis=0, tiled=True)  23.6 us
    all_to_all x3, starting transfers between devices, spread(): return lax.all_to_all(copies, axes, split_axis=0, concat_axis=0, tiled=True)  19.4 us
    all_gather x1, blocking collectives, shards(): cross = lax.all_gather(cross, COL, axis=0, tiled=False)  16.2 us
    ppermute x1, waiting for transfers between devices, shards(): moved = lax.ppermute(send, 'y', [(i, i ^ 1) for i in range(ny)])  11.9 us
    ppermute x3, starting transfers between devices, shards(): lax.ppermute(parts[d], 'x', [(i, (i + d) % nx) for i in range(nx)])  10.8 us
    ppermute x3, starting transfers between devices, shards(): moved = lax.ppermute(part, 'y', [(i, (i + 2 * e) % ny) for i in range(ny)])  9.3 us
    pallas_call x1, Pallas kernels, gram_inverse(): pl.pallas_call(gram_inverse_kernel, out_shape=jax.ShapeDtypeStruct(factor...  8.3 us
  transfers between devices with their start and end apart: 14, of which 7 were waited for; matrix products, arithmetic and copies ran while one was open for 8% of the time, Pallas kernels for 10%

profile of v8, /device:TPU:1, one launch (start us, length us, event | category | flops | bytes accessed | tf_op | source)
XLA Modules:
  0.0 213.8 jit_solution(14064110500309329117)
XLA Ops:
  7.2 0.0 copy-start
  7.2 0.0 copy-start.3
  7.2 0.0 all-gather.3.cloned.1.call-start
  7.2 0.7 all-gather.3.cloned.1.call-update
  7.9 0.8 pad.4
  8.8 0.8 broadcast_in_dim.8
  9.5 7.6 %all-to-all-start = ((bf16[8,112,256]{2,1,0:T(8,128)(2,1)}), bf16[8,112,256]{2,1,0:T(8,128)(2,1)S(1)}, u32[]{:S(2)}, u32[]{:S(2)}) async-start(bf16[8,112,256]{2,1,0:T(8,128)(2,1)} %broadcast_in_dim.8), calls=%async_computation | async-start | bytes 917504 | tf_op jit(solution)/shard_map/all_to_all | solution.py:75
  17.2 0.0 copy-done
  17.2 1.3 fusion.3
  18.5 11.8 %all-to-all-done = bf16[8,112,256]{2,1,0:T(8,128)(2,1)S(1)} async-done(((bf16[8,112,256]{2,1,0:T(8,128)(2,1)}), bf16[8,112,256]{2,1,0:T(8,128)(2,1)S(1)}, u32[]{:S(2)}, u32[]{:S(2)}) %all-to-all-start) | async-done | bytes 458784 | tf_op jit(solution)/shard_map/all_to_all | solution.py:75
  30.3 7.8 %all-to-all-start.2 = ((f32[32,16,224]{2,1,0:T(8,128)}), f32[32,16,224]{2,1,0:T(8,128)S(1)}, u32[]{:S(2)}, u32[]{:S(2)}) async-start(f32[32,16,224]{2,1,0:T(8,128)} %bitcast.5), calls=%async_computation.2 | async-start | bytes 1048576 | tf_op jit(solution)/shard_map/all_to_all | solution.py:211
  38.1 30.6 %all-gather.3.cloned.1.call-done.mine_ref = bf16[1792,1024]{1,0:T(8,128)(2,1)} async-done(((bf16[224,1024]{1,0:T(8,128)(2,1)}), bf16[1792,1024]{1,0:T(8,128)(2,1)}) %all-gather.3.cloned.1.call-update) | async-done | bytes 3670032 | tf_op jit(solution)/shard_map/all_gather | solution.py:207
  68.7 2.7 %collective-permute-start = (bf16[1792,1024]{1,0:T(8,128)(2,1)}, bf16[1792,1024]{1,0:T(8,128)(2,1)}, u32[]{:S(2)}, u32[]{:S(2)}) collective-permute-start(bf16[1792,1024]{1,0:T(8,128)(2,1)} %all-gather.3.cloned.1.call-done.mine_ref), channel_id=1, source_target_pairs={{0,1},{1,0},{2,3},{3,2},{4,5},{5,4},{6,7},{7,6},{8,9},{9,8},{10,11... | collective-permute-start | bytes 11010056 | tf_op jit(solution)/shard_map/ppermute | solution.py:208
  71.4 0.0 all-to-all-done.2
  71.5 1.4 broadcast_in_dim.10
  72.9 4.0 %all-to-all-start.1 = ((bf16[4,896,256]{2,1,0:T(8,128)(2,1)}), bf16[4,896,256]{2,1,0:T(8,128)(2,1)S(1)}, u32[]{:S(2)}, u32[]{:S(2)}) async-start(bf16[4,896,256]{2,1,0:T(8,128)(2,1)} %broadcast_in_dim.10), calls=%async_computation.1 | async-start | bytes 3670016 | tf_op jit(solution)/shard_map/all_to_all | solution.py:75
  76.9 0.1 reduce_sum.9
  76.9 16.2 %all-gather = f32[256,224]{1,0:T(8,128)S(1)} all-gather(f32[16,224]{1,0:T(8,128)S(1)} %reduce_sum.9), channel_id=2, replica_groups=mesh['y'=8,'x'=4,'z'=8,'c'=2] {'z','c'}, dimensions={0}, use_global_device_ids=true | all-gather | bytes 243712 | tf_op jit(solution)/shard_map/all_gather | solution.py:213
  93.1 0.2 reshape.29
  93.4 0.2 copy.15
  93.5 0.2 reshape.30
  93.7 6.5 %all-to-all-done.1.weight_ref = bf16[4,896,256]{2,1,0:T(8,128)(2,1)S(1)} async-done(((bf16[4,896,256]{2,1,0:T(8,128)(2,1)}), bf16[4,896,256]{2,1,0:T(8,128)(2,1)S(1)}, u32[]{:S(2)}, u32[]{:S(2)}) %all-to-all-start.1) | async-done | bytes 1835040 | tf_op jit(solution)/shard_map/all_to_all | solution.py:75
  100.2 1.3 copy-done.2
  101.5 2.4 %fusion = f32[16,224]{1,0:T(8,128)S(1)} fusion(f32[16,3584]{1,0:T(8,128)S(1)} %reshape.30, bf16[3584,256]{1,0:T(8,128)(2,1)} %bitcast.23), kind=kOutput, calls=%fused_computation | convolution fusion | flops 154140672 | bytes 2078720 | tf_op jit(solution)/shard_map/dot_general | solution.py:18
  104.0 0.9 broadcast_in_dim.11
  104.8 7.8 %all-to-all-start.3 = ((f32[32,16,224]{2,1,0:T(8,128)}), f32[32,16,224]{2,1,0:T(8,128)}, u32[]{:S(2)}, u32[]{:S(2)}) async-start(f32[32,16,224]{2,1,0:T(8,128)} %broadcast_in_dim.11), calls=%async_computation.3 | async-start | bytes 1048576 | tf_op jit(solution)/shard_map/all_to_all | solution.py:75
  112.6 1.0 copy.18.residual_ref
  113.6 0.0 copy-done.1
  113.6 8.3 %gram_inverse.1 = f32[512,512]{1,0:T(8,128)S(1)} custom-call(f32[512,512]{1,0:T(8,128)S(1)} %copy-done.1), custom_call_target="tpu_custom_call" | custom-call | tf_op jit(solution)/shard_map/gram_inverse/pallas_call | solution.py:61
  121.9 0.7 pad_add_fusion.place_ref
  122.6 5.2 %all-to-all-done.3 = f32[32,16,224]{2,1,0:T(8,128)} async-done(((f32[32,16,224]{2,1,0:T(8,128)}), f32[32,16,224]{2,1,0:T(8,128)}, u32[]{:S(2)}, u32[]{:S(2)}) %all-to-all-start.3) | async-done | bytes 458784 | tf_op jit(solution)/shard_map/all_to_all | solution.py:75
  127.8 2.9 %convolution_convert_fusion = bf16[224,512]{1,0:T(8,128)(2,1)S(1)} fusion(f32[512,224]{1,0:T(8,128)} %bitcast.8, f32[512,512]{1,0:T(8,128)S(1)} %gram_inverse.1), kind=kOutput, calls=%fused_computation.2 | convolution fusion | flops 704757760 | bytes 1736704 | tf_op jit(solution)/shard_map/dot_general | solution.py:18
  130.7 0.5 fusion.4
  131.2 0.0 collective-permute-done.theirs_ref
  131.2 6.9 %partial_weight_grads.1 = (bf16[8,112,224]{2,1,0:T(8,128)(2,1)}, bf16[8,112,224]{2,1,0:T(8,128)(2,1)}, bf16[8,112,224]{2,1,0:T(8,128)(2,1)}, bf16[8,112,224]{2,1,0:T(8,128)(2,1)}) custom-call(s32[3]{0:T(128)} %pad_add_fusion.place_ref, bf16[1792,1024]{1,0:T(8,128)(2,1)} %all-gather.3.cloned.1.call-done.mine_ref, ...), custom_call_target="tpu_custom_call" | custom-call | tf_op jit(solution)/shard_map/partial_weight_grads/pallas_call | solution.py:98
  138.1 3.0 %collective-permute-start.1 = (bf16[8,112,224]{2,1,0:T(8,128)(2,1)}, bf16[8,112,224]{2,1,0:T(8,128)(2,1)S(1)}, u32[]{:S(2)}, u32[]{:S(2)}) collective-permute-start(bf16[8,112,224]{2,1,0:T(8,128)(2,1)} %get-tuple-element.13), channel_id=1, source_target_pairs={{0,16},{16,32},{32,48},{48,0},{1,17},{17,33},{33,49},{49,1},{2,18}... | collective-permute-start | bytes 1204232 | tf_op jit(solution)/shard_map/ppermute | solution.py:227
  141.1 4.5 %collective-permute-start.2 = (bf16[8,112,224]{2,1,0:T(8,128)(2,1)}, bf16[8,112,224]{2,1,0:T(8,128)(2,1)S(1)}, u32[]{:S(2)}, u32[]{:S(2)}) collective-permute-start(bf16[8,112,224]{2,1,0:T(8,128)(2,1)} %get-tuple-element.14), channel_id=1, source_target_pairs={{0,32},{16,48},{32,0},{48,16},{1,33},{17,49},{33,1},{49,17},{2,34}... | collective-permute-start | bytes 1204232 | tf_op jit(solution)/shard_map/ppermute | solution.py:227
  145.6 3.3 %collective-permute-start.3 = (bf16[8,112,224]{2,1,0:T(8,128)(2,1)}, bf16[8,112,224]{2,1,0:T(8,128)(2,1)}, u32[]{:S(2)}, u32[]{:S(2)}) collective-permute-start(bf16[8,112,224]{2,1,0:T(8,128)(2,1)} %get-tuple-element.15), channel_id=1, source_target_pairs={{0,48},{16,0},{32,16},{48,32},{1,49},{17,1},{33,17},{49,33},{2,50}... | collective-permute-start | bytes 1204232 | tf_op jit(solution)/shard_map/ppermute | solution.py:227
  148.9 7.2 %dense_grad.1 = f32[224,1024]{1,0:T(8,128)} custom-call(s32[3]{0:T(128)} %pad_add_fusion.place_ref, bf16[1792,1024]{1,0:T(8,128)(2,1)} %all-gather.3.cloned.1.call-done.mine_ref, bf16[1792,1024]{1,0:T(8,128)(2,1)} %collective-permute-done.theirs_ref, bf16[4,896,256]{2,1,0:T(8,128)(2,1)} %copy-done.2), custom_call_target="tpu_custom_call" | custom-call | tf_op jit(solution)/shard_map/dense_grad/pallas_call | solution.py:139
  156.1 1.3 fusion.2
  157.4 1.0 copy.16
  158.4 7.5 %all-to-all-start.4 = ((bf16[16,64,224]{2,1,0:T(8,128)(2,1)}), bf16[16,64,224]{2,1,0:T(8,128)(2,1)S(1)}, u32[]{:S(2)}, u32[]{:S(2)}) async-start(bf16[16,64,224]{2,1,0:T(8,128)(2,1)} %bitcast.10), calls=%async_computation.4 | async-start | bytes 1048576 | tf_op jit(solution)/shard_map/all_to_all | solution.py:238
  165.9 0.0 collective-permute-done.1.refs_1_
  165.9 0.0 collective-permute-done.2.refs_2_
  165.9 0.0 collective-permute-done.3.refs_3_
  165.9 0.7 copy-done.6
  166.7 0.2 copy-done.7
  166.8 3.2 %sum_parts.1 = (f32[4,112,224]{2,1,0:T(8,128)}, f32[4,112,224]{2,1,0:T(8,128)}) custom-call(s32[3]{0:T(128)} %pad_add_fusion.place_ref, bf16[8,112,224]{2,1,0:T(8,128)(2,1)} %get-tuple-element.12.refs_0_, bf16[8,112,224]{2,1,0:T(8,128)(2,1)} %copy-done.6, bf16[8,112,224]{2,1,0:T(8,128)(2,1)} %copy-done.7, bf16[8,112,224]{2,1,0:T(8,128)(2,1)} %collective-permute-done.3.refs_3_), custom_call_target="tpu_custom_call" | custom-call | tf_op jit(solution)/shard_map/sum_parts/pallas_call | solution.py:168
  170.0 2.2 %collective-permute-start.4 = (f32[4,112,224]{2,1,0:T(8,128)}, f32[4,112,224]{2,1,0:T(8,128)S(1)}, u32[]{:S(2)}, u32[]{:S(2)}) collective-permute-start(f32[4,112,224]{2,1,0:T(8,128)} %get-tuple-element.17), channel_id=1, source_target_pairs={{0,64},{64,0},{128,192},{192,128},{256,320},{320,256},{384,448},{4... | collective-permute-start | bytes 1204232 | tf_op jit(solution)/shard_map/ppermute | solution.py:229
  172.2 11.9 %collective-permute-done.4.moved_ref = f32[4,112,224]{2,1,0:T(8,128)S(1)} collective-permute-done((f32[4,112,224]{2,1,0:T(8,128)}, f32[4,112,224]{2,1,0:T(8,128)S(1)}, u32[]{:S(2)}, u32[]{:S(2)}) %collective-permute-start.4) | collective-permute-done | bytes 401440 | tf_op jit(solution)/shard_map/ppermute | solution.py:229
  184.1 0.8 copy-done.4
  184.9 1.9 sum_pair.1
  186.7 1.9 collective-permute-start.5
  188.6 3.3 %collective-permute-start.6 = (bf16[112,224]{1,0:T(8,128)(2,1)}, bf16[112,224]{1,0:T(8,128)(2,1)S(1)}, u32[]{:S(2)}, u32[]{:S(2)}) collective-permute-start(bf16[112,224]{1,0:T(8,128)(2,1)} %get-tuple-element.20), channel_id=1, source_target_pairs={{0,256},{64,320},{128,384},{192,448},{256,0},{320,64},{384,128},{4... | collective-permute-start | bytes 150536 | tf_op jit(solution)/shard_map/ppermute | solution.py:232
  191.9 4.1 %collective-permute-start.7 = (bf16[112,224]{1,0:T(8,128)(2,1)}, bf16[112,224]{1,0:T(8,128)(2,1)S(1)}, u32[]{:S(2)}, u32[]{:S(2)}) collective-permute-start(bf16[112,224]{1,0:T(8,128)(2,1)} %get-tuple-element.21), channel_id=1, source_target_pairs={{0,384},{64,448},{128,0},{192,64},{256,128},{320,192},{384,256},{4... | collective-permute-start | bytes 150536 | tf_op jit(solution)/shard_map/ppermute | solution.py:232
  196.1 0.0 collective-permute-done.5
  196.1 1.6 collective-permute-done.6
  197.7 5.3 %collective-permute-done.7 = bf16[112,224]{1,0:T(8,128)(2,1)S(1)} collective-permute-done((bf16[112,224]{1,0:T(8,128)(2,1)}, bf16[112,224]{1,0:T(8,128)(2,1)S(1)}, u32[]{:S(2)}, u32[]{:S(2)}) %collective-permute-start.7) | collective-permute-done | bytes 50208 | tf_op jit(solution)/shard_map/ppermute | solution.py:232
  202.9 1.6 add_multiply_fusion
  204.5 0.0 all-to-all-done.4
  204.5 0.1 convert_bitcast_fusion
  204.6 0.6 copy.17
  205.2 0.6 reshape.33
  205.9 1.1 broadcast_divide_fusion
  (11 shorter events, 0.0 us)
Async XLA Ops:
  7.2 10.0 %copy-start = (bf16[1024,512]{1,0:T(8,128)(2,1)S(1)}, bf16[1024,512]{1,0:T(8,128)(2,1)}, u32[]{:S(2)}) copy-start(bf16[1024,512]{1,0:T(8,128)(2,1)} %param.8) | copy-start | bytes 3145732
  7.2 10.0 %copy-start.3 = (bf16[1024,224]{0,1:T(8,128)(2,1)S(1)}, bf16[1024,224]{0,1:T(8,128)(2,1)}, u32[]{:S(2)}) copy-start(bf16[1024,224]{0,1:T(8,128)(2,1)} %param.6) | copy-start | bytes 1376260
  7.2 61.5 %all-gather.3.cloned.1.call-start = ((), (), s32[]{:S(2)}) async-start(), calls=%async_computation.5 | async-start | bytes 4128768 | tf_op jit(solution)/shard_map/all_gather | solution.py:207
  9.5 20.8 %all-to-all-start = ((bf16[8,112,256]{2,1,0:T(8,128)(2,1)}), bf16[8,112,256]{2,1,0:T(8,128)(2,1)S(1)}, u32[]{:S(2)}, u32[]{:S(2)}) async-start(bf16[8,112,256]{2,1,0:T(8,128)(2,1)} %broadcast_in_dim.8), calls=%async_computation | async-start | bytes 917504 | tf_op jit(solution)/shard_map/all_to_all | solution.py:75
  30.3 41.1 %all-to-all-start.2 = ((f32[32,16,224]{2,1,0:T(8,128)}), f32[32,16,224]{2,1,0:T(8,128)S(1)}, u32[]{:S(2)}, u32[]{:S(2)}) async-start(f32[32,16,224]{2,1,0:T(8,128)} %bitcast.5), calls=%async_computation.2 | async-start | bytes 1048576 | tf_op jit(solution)/shard_map/all_to_all | solution.py:211
  68.7 62.5 %collective-permute-start = (bf16[1792,1024]{1,0:T(8,128)(2,1)}, bf16[1792,1024]{1,0:T(8,128)(2,1)}, u32[]{:S(2)}, u32[]{:S(2)}) collective-permute-start(bf16[1792,1024]{1,0:T(8,128)(2,1)} %all-gather.3.cloned.1.call-done.mine_ref), channel_id=1, source_target_pairs={{0,1},{1,0},{2,3},{3,2},{4,5},{5,4},{6,7},{7,6},{8,9},{9,8},{10,11... | collective-permute-start | bytes 11010056 | tf_op jit(solution)/shard_map/ppermute | solution.py:208
  72.9 27.3 %all-to-all-start.1 = ((bf16[4,896,256]{2,1,0:T(8,128)(2,1)}), bf16[4,896,256]{2,1,0:T(8,128)(2,1)S(1)}, u32[]{:S(2)}, u32[]{:S(2)}) async-start(bf16[4,896,256]{2,1,0:T(8,128)(2,1)} %broadcast_in_dim.10), calls=%async_computation.1 | async-start | bytes 3670016 | tf_op jit(solution)/shard_map/all_to_all | solution.py:75
  100.2 1.3 copy-start.2
  101.5 11.1 %copy-start.5 = (bf16[1024,224]{0,1:T(8,128)(2,1)S(1)}, bf16[1024,224]{0,1:T(8,128)(2,1)}, u32[]{:S(2)}) copy-start(bf16[1024,224]{0,1:T(8,128)(2,1)} %param.7) | copy-start | bytes 1376260
  101.5 12.1 %copy-start.1 = (f32[512,512]{1,0:T(8,128)S(1)}, f32[512,512]{1,0:T(8,128)}, u32[]{:S(2)}) copy-start(f32[512,512]{1,0:T(8,128)} %factor_ref.1) | copy-start | bytes 3145732
  104.8 23.0 %all-to-all-start.3 = ((f32[32,16,224]{2,1,0:T(8,128)}), f32[32,16,224]{2,1,0:T(8,128)}, u32[]{:S(2)}, u32[]{:S(2)}) async-start(f32[32,16,224]{2,1,0:T(8,128)} %broadcast_in_dim.11), calls=%async_computation.3 | async-start | bytes 1048576 | tf_op jit(solution)/shard_map/all_to_all | solution.py:75
  138.1 27.8 %collective-permute-start.1 = (bf16[8,112,224]{2,1,0:T(8,128)(2,1)}, bf16[8,112,224]{2,1,0:T(8,128)(2,1)S(1)}, u32[]{:S(2)}, u32[]{:S(2)}) collective-permute-start(bf16[8,112,224]{2,1,0:T(8,128)(2,1)} %get-tuple-element.13), channel_id=1, source_target_pairs={{0,16},{16,32},{32,48},{48,0},{1,17},{17,33},{33,49},{49,1},{2,18}... | collective-permute-start | bytes 1204232 | tf_op jit(solution)/shard_map/ppermute | solution.py:227
  141.1 24.8 %collective-permute-start.2 = (bf16[8,112,224]{2,1,0:T(8,128)(2,1)}, bf16[8,112,224]{2,1,0:T(8,128)(2,1)S(1)}, u32[]{:S(2)}, u32[]{:S(2)}) collective-permute-start(bf16[8,112,224]{2,1,0:T(8,128)(2,1)} %get-tuple-element.14), channel_id=1, source_target_pairs={{0,32},{16,48},{32,0},{48,16},{1,33},{17,49},{33,1},{49,17},{2,34}... | collective-permute-start | bytes 1204232 | tf_op jit(solution)/shard_map/ppermute | solution.py:227
  145.6 20.3 %collective-permute-start.3 = (bf16[8,112,224]{2,1,0:T(8,128)(2,1)}, bf16[8,112,224]{2,1,0:T(8,128)(2,1)}, u32[]{:S(2)}, u32[]{:S(2)}) collective-permute-start(bf16[8,112,224]{2,1,0:T(8,128)(2,1)} %get-tuple-element.15), channel_id=1, source_target_pairs={{0,48},{16,0},{32,16},{48,32},{1,49},{17,1},{33,17},{49,33},{2,50}... | collective-permute-start | bytes 1204232 | tf_op jit(solution)/shard_map/ppermute | solution.py:227
  158.4 37.7 %copy-start.8 = (s32[64]{0:T(128)S(1)}, s32[64]{0:T(128)}, u32[]{:S(2)}) copy-start(s32[64]{0:T(128)} %param.11) | copy-start | bytes 772
  158.4 46.1 %all-to-all-start.4 = ((bf16[16,64,224]{2,1,0:T(8,128)(2,1)}), bf16[16,64,224]{2,1,0:T(8,128)(2,1)S(1)}, u32[]{:S(2)}, u32[]{:S(2)}) async-start(bf16[16,64,224]{2,1,0:T(8,128)(2,1)} %bitcast.10), calls=%async_computation.4 | async-start | bytes 1048576 | tf_op jit(solution)/shard_map/all_to_all | solution.py:238
  165.9 0.8 copy-start.6
  165.9 0.9 copy-start.7
  170.0 14.1 %collective-permute-start.4 = (f32[4,112,224]{2,1,0:T(8,128)}, f32[4,112,224]{2,1,0:T(8,128)S(1)}, u32[]{:S(2)}, u32[]{:S(2)}) collective-permute-start(f32[4,112,224]{2,1,0:T(8,128)} %get-tuple-element.17), channel_id=1, source_target_pairs={{0,64},{64,0},{128,192},{192,128},{256,320},{320,256},{384,448},{4... | collective-permute-start | bytes 1204232 | tf_op jit(solution)/shard_map/ppermute | solution.py:229
  184.1 0.8 copy-start.4
  186.7 9.3 %collective-permute-start.5 = (bf16[112,224]{1,0:T(8,128)(2,1)}, bf16[112,224]{1,0:T(8,128)(2,1)S(1)}, u32[]{:S(2)}, u32[]{:S(2)}) collective-permute-start(bf16[112,224]{1,0:T(8,128)(2,1)} %get-tuple-element.19), channel_id=1, source_target_pairs={{0,128},{64,192},{128,256},{192,320},{256,384},{320,448},{384,0},{... | collective-permute-start | bytes 150536 | tf_op jit(solution)/shard_map/ppermute | solution.py:232
  188.6 9.0 %collective-permute-start.6 = (bf16[112,224]{1,0:T(8,128)(2,1)}, bf16[112,224]{1,0:T(8,128)(2,1)S(1)}, u32[]{:S(2)}, u32[]{:S(2)}) collective-permute-start(bf16[112,224]{1,0:T(8,128)(2,1)} %get-tuple-element.20), channel_id=1, source_target_pairs={{0,256},{64,320},{128,384},{192,448},{256,0},{320,64},{384,128},{4... | collective-permute-start | bytes 150536 | tf_op jit(solution)/shard_map/ppermute | solution.py:232
  191.9 11.0 %collective-permute-start.7 = (bf16[112,224]{1,0:T(8,128)(2,1)}, bf16[112,224]{1,0:T(8,128)(2,1)S(1)}, u32[]{:S(2)}, u32[]{:S(2)}) collective-permute-start(bf16[112,224]{1,0:T(8,128)(2,1)} %get-tuple-element.21), channel_id=1, source_target_pairs={{0,384},{64,448},{128,0},{192,64},{256,128},{320,192},{384,256},{4... | collective-permute-start | bytes 150536 | tf_op jit(solution)/shard_map/ppermute | solution.py:232
Sparse Core Ops, SparseCore 0:
  10.1 58.5 all-gather.2
